TPU v7x, 512 devices: a whole 4x8x8 slice. The times are simulated.
512 devices in a mesh: req: 16 (over y_hi, z), cand: 32 (over x, y_lo, core).
Axes of the slice: x: 4, y: 8 (y_hi: 2, y_lo: 4; y = y_hi * 4 + y_lo), z: 8, core: 2. Of those that a mesh axis runs over, the one named last changes fastest.
Arguments:
- dense_feat: bfloat16 [65536, 512], P(('req', 'cand')), may hold values from -6 to 6
- emb_ids: int32 [32, 4, 65536], P('cand', None, 'req'), may hold values from 0 to 32767
- tables: bfloat16 [32, 16, 32768], P('cand'), may hold values from -3 to 3
- history_kv: bfloat16 [32, 64, 2048], P('req', 'cand'), may hold values from -6 to 6
- hist_len: int32 [32], P('req'), may hold values from 1 to 64, 1024 in all
- cand_request: int32 [65536], P(('req', 'cand')), may hold values from 0 to 1
- w_query: bfloat16 [1024, 1024], P(('req', 'cand')), may hold values from -0.1875 to 0.1875
- w_out: bfloat16 [1024, 1024], P(('req', 'cand')), may hold values from -0.1875 to 0.1875
- cotangent: bfloat16 [65536, 1024], P(('req', 'cand')), may hold values from -2 to 2
Outputs:
- cand_out: bfloat16 [65536, 1024], P(('req', 'cand'))
- d_kv: float32 [32, 64, 2048], P('req', 'cand')
- d_pooled: bfloat16 [32, 16, 65536], P('cand', None, 'req')
Inputs may be any that keep to these rules, and one draw needn't show every extreme that they name: `hist_len`: the lengths sum to 1024 and the largest equals 64.
All inputs are finite; a program needn't handle non-finite values. No bound on the sum of `hist_len` on one device may be relied on, other than what follows from the above.
Results may differ from a plain program's by a relative error of at most 0.023.
Values may be sent and summed in bfloat16 or wider, within the bound.
No kernel may reach another device: no remote copies, remote signals or barrier semaphores. Data moves between devices by JAX's collectives and lax.ppermute only.
A program may use at most 64 MiB of HBM per device.

v0:
```python
import math

import jax
import jax.numpy as jnp
from jax import lax
from jax.sharding import PartitionSpec as P

H = 8


norm_eps = 1e-05


def silu_slope(argument):
    sigmoid_value = jax.nn.sigmoid(argument)
    return sigmoid_value * (1.0 + argument * (1.0 - sigmoid_value))


def event_mask(requests, lengths, row_count):
    owned_count = lengths.shape[0]
    positions = jnp.arange(row_count, dtype=jnp.int32)
    in_length = positions[None, :] < lengths[:, None]
    same_request = requests[:, None] == jnp.arange(owned_count, dtype=jnp.int32)[None, :]
    joined_mask = same_request[:, :, None] & in_length[None, :, :]
    return joined_mask.reshape(requests.shape[0], owned_count * row_count).astype(jnp.float32)


def forward_events(query_heads, kv_piece, live_mask, score_scale):
    owned_count, row_count, kv_width = kv_piece.shape
    model_width = kv_width // 2
    events = owned_count * row_count
    flat_events = kv_piece.reshape(events, kv_width)
    key_heads = flat_events[:, :model_width].reshape(events, H, model_width // H)
    value_heads = flat_events[:, model_width:].reshape(events, H, model_width // H)
    scores = (
        jnp.einsum("chd,ehd->che", query_heads, key_heads, preferred_element_type=jnp.float32)
        * score_scale
    )
    weights = (jax.nn.silu(scores) * live_mask[:, None, :]).astype(jnp.bfloat16)
    return (scores, weights, key_heads, value_heads)


def backward_core(
    query_heads, back_att, scores, weights, key_heads, value_heads, live_mask, score_scale
):
    back_w = jnp.einsum("chd,ehd->che", back_att, value_heads, preferred_element_type=jnp.float32)
    back_s = (back_w * live_mask[:, None, :] * silu_slope(scores) * score_scale).astype(
        jnp.bfloat16
    )
    back_query = jnp.einsum("che,ehd->chd", back_s, key_heads, preferred_element_type=jnp.float32)
    key_part = jnp.einsum("che,chd->ehd", back_s, query_heads, preferred_element_type=jnp.float32)
    value_part = jnp.einsum("che,chd->ehd", weights, back_att, preferred_element_type=jnp.float32)
    events = key_part.shape[0]
    joined = jnp.concatenate([key_part.reshape(events, -1), value_part.reshape(events, -1)], axis=1)
    return (back_query, joined.astype(jnp.bfloat16))


def take_columns(table, indices):
    return jnp.take(table, indices, axis=1)


def on_device(
    dense_feat, emb_ids, tables, history_kv, hist_len, cand_request, w_query, w_out, cotangent
):
    tab_dev, emb_width, table_rows = tables.shape
    bag_size = emb_ids.shape[1]
    group_size = emb_ids.shape[2]
    pooled_sum = jnp.zeros((tab_dev, emb_width, group_size), jnp.float32)
    for slot in range(bag_size):
        pooled_sum = pooled_sum + jax.vmap(take_columns)(tables, emb_ids[:, slot, :]).astype(
            jnp.float32
        )
    pooled_rows = pooled_sum.astype(jnp.bfloat16).reshape(tab_dev * emb_width, group_size)
    pooled_cols = lax.all_to_all(pooled_rows, "cand", split_axis=1, concat_axis=0, tiled=True)
    pooled = jnp.transpose(pooled_cols, (1, 0))
    features = jnp.concatenate([pooled, dense_feat], axis=1)
    cand_count, model_width = features.shape
    pooled_width = pooled.shape[1]
    head_dim = model_width // H
    score_scale = 1.0 / math.sqrt(head_dim)
    owned_count, shard_events, kv_width = history_kv.shape
    hist_events = shard_events * lax.axis_size("cand")
    full_query, full_out = (
        lax.all_gather(w_query, ("req", "cand"), axis=0, tiled=True),
        lax.all_gather(w_out, ("req", "cand"), axis=0, tiled=True),
    )
    query_pre = jnp.dot(features, full_query, preferred_element_type=jnp.float32)
    query_heads = jax.nn.silu(query_pre).astype(jnp.bfloat16).reshape(cand_count, H, head_dim)
    full_history = lax.all_gather(history_kv, "cand", axis=1, tiled=True)
    live_mask = event_mask(cand_request, hist_len, hist_events)
    scores, weights, key_heads, value_heads = forward_events(
        query_heads, full_history, live_mask, score_scale
    )
    attended = jnp.einsum("che,ehd->chd", weights, value_heads, preferred_element_type=jnp.float32)
    attended = attended.reshape(cand_count, model_width)
    centered = attended - jnp.mean(attended, axis=1, keepdims=True)
    inverse = lax.rsqrt(jnp.mean(centered * centered, axis=1, keepdims=True) + norm_eps)
    normed = centered * inverse
    normed_b = normed.astype(jnp.bfloat16)
    mixed_out = jnp.dot(normed_b, full_out, preferred_element_type=jnp.float32)
    back_y = lax.dot_general(
        cotangent, full_out, (((1,), (1,)), ((), ())), preferred_element_type=jnp.float32
    )
    cand_out = (mixed_out + features.astype(jnp.float32)).astype(jnp.bfloat16)
    back_att = inverse * (
        back_y
        - jnp.mean(back_y, axis=1, keepdims=True)
        - normed * jnp.mean(back_y * normed, axis=1, keepdims=True)
    )
    back_att = back_att.astype(jnp.bfloat16).reshape(cand_count, H, head_dim)
    back_query, joined = backward_core(
        query_heads, back_att, scores, weights, key_heads, value_heads, live_mask, score_scale
    )
    kv_part = joined.reshape(owned_count, hist_events, kv_width)
    d_kv = lax.psum_scatter(kv_part, "cand", scatter_dimension=1, tiled=True).astype(jnp.float32)
    back_pre = (back_query.reshape(cand_count, model_width) * silu_slope(query_pre)).astype(
        jnp.bfloat16
    )
    back_columns = lax.dot_general(
        back_pre,
        full_query[:pooled_width],
        (((1,), (1,)), ((), ())),
        preferred_element_type=jnp.float32,
    )
    back_pool = (cotangent[:, :pooled_width].astype(jnp.float32) + back_columns).astype(
        jnp.bfloat16
    )
    pool_cols = jnp.transpose(back_pool, (1, 0))
    pool_rows = lax.all_to_all(pool_cols, "cand", split_axis=0, concat_axis=1, tiled=True)
    d_pooled = pool_rows.reshape(tab_dev, emb_width, pool_rows.shape[1])
    return (cand_out, d_kv, d_pooled)


def solution(mesh):
    return jax.shard_map(
        on_device,
        mesh=mesh,
        in_specs=(
            P(("req", "cand"), None),
            P("cand", None, "req"),
            P("cand", None, None),
            P("req", "cand", None),
            P("req"),
            P(("req", "cand")),
            P(("req", "cand"), None),
            P(("req", "cand"), None),
            P(("req", "cand"), None),
        ),
        out_specs=(P(("req", "cand"), None), P("req", "cand", None), P("cand", None, "req")),
        check_vma=False,
    )
```

profile of v0, /device:TPU:1, one launch (start us, length us, event | category | flops | bytes accessed | tf_op | source)
XLA Modules:
  0.0 1853.4 jit_solution(14604145347478205442)
XLA Ops:
  8.6 1.3 and_reduce_fusion.3
  10.0 7.1 copy.95
  17.1 45.7 %gather_fusion.2 = bf16[4096,16]{1,0:T(8,128)(2,1)S(1)} fusion(bf16[1,16,32768]{1,2,0:T(8,128)(2,1)} %copy.95, s32[4096]{0:T(1024)S(1)} %bitcast.122), kind=kCustom, calls=%fused_computation.2.clone | custom fusion | bytes 294912 | tf_op jit(solution)/shard_map/vmap(jit(_take))/gather | solution.py:59
  63.3 45.6 %gather_fusion.3 = bf16[4096,16]{1,0:T(8,128)(2,1)S(1)} fusion(bf16[1,16,32768]{1,2,0:T(8,128)(2,1)} %copy.95, s32[4096]{0:T(1024)S(1)} %bitcast.124), kind=kCustom, calls=%fused_computation.3.clone | custom fusion | bytes 294912 | tf_op jit(solution)/shard_map/vmap(jit(_take))/gather | solution.py:59
  109.3 45.6 %gather_fusion = bf16[4096,16]{1,0:T(8,128)(2,1)S(1)} fusion(bf16[1,16,32768]{1,2,0:T(8,128)(2,1)} %copy.95, s32[4096]{0:T(1024)S(1)} %bitcast.125), kind=kCustom, calls=%fused_computation.clone | custom fusion | bytes 294912 | tf_op jit(solution)/shard_map/vmap(jit(_take))/gather | solution.py:59
  155.3 45.5 %gather_fusion.1 = bf16[4096,16]{1,0:T(8,128)(2,1)S(1)} fusion(bf16[1,16,32768]{1,2,0:T(8,128)(2,1)} %copy.95, s32[4096]{0:T(1024)S(1)} %bitcast.123), kind=kCustom, calls=%fused_computation.1.clone | custom fusion | bytes 294912 | tf_op jit(solution)/shard_map/vmap(jit(_take))/gather | solution.py:59
  202.0 11.0 all-to-all-start
  213.2 45.9 %all_gather.10 = bf16[2,64,2048]{2,0,1:T(2,128)(2,1)S(1)} all-gather(bf16[2,2,2048]{2,0,1:T(2,128)(2,1)S(1)} %copy.105), channel_id=1, replica_groups=mesh['req'=16,'cand'=32] {'cand'}, dimensions={1}, use_global_device_ids=true | all-gather | bytes 540672 | tf_op jit(solution)/shard_map/all_gather | solution.py:89
  260.1 1.3 dynamic-slice
  262.2 520.2 %all-gather.5.cloned.1.call-done = bf16[512,2,1024]{2,1,0:T(2,128)(2,1)} async-done(((bf16[1,2,1024]{2,1,0:T(2,128)(2,1)}), bf16[512,2,1024]{2,1,0:T(2,128)(2,1)}) %all-gather.5.cloned.1.call-update) | async-done | bytes 2097168 | tf_op jit(solution)/shard_map/all_gather | solution.py:84
  782.4 2.7 reshape.215
  785.2 1.3 multiply_convert_fusion.3
  788.6 758.8 %all-gather.7.cloned.1.call-done = bf16[512,2,1024]{2,1,0:T(2,128)(2,1)} async-done(((bf16[1,2,1024]{2,1,0:T(2,128)(2,1)}), bf16[512,2,1024]{2,1,0:T(2,128)(2,1)}) %all-gather.7.cloned.1.call-update) | async-done | bytes 2097168 | tf_op jit(solution)/shard_map/all_gather | solution.py:85
  1547.3 2.7 reshape.217
  1552.2 1.5 fusion.4
  1557.2 3.0 slice.59
  1560.2 2.3 reshape.218
  1563.8 1.8 pad_maximum_fusion
  1565.6 2.1 fusion.9
  1568.4 5.5 all-to-all-start.1
  1573.9 1.2 fusion.5
  1575.1 7.6 all-to-all-done.1
  1583.5 261.9 %all-reduce.3.cloned.1.call-done = bf16[2,64,2048]{2,1,0:T(8,128)(2,1)} async-done(((bf16[2,64,2048]{2,1,0:T(8,128)(2,1)}), bf16[2,64,2048]{2,1,0:T(8,128)(2,1)}) %all-reduce.3.cloned.1.call-update) | async-done | bytes 524304
  1845.4 1.5 dynamic-slice_convert_fusion
  (88 shorter events, 15.4 us)
Async XLA Ops:
  7.2 775.3 %all-gather.5.cloned.1.call-start = ((), (), s32[]{:S(2)}) async-start(), calls=%async_computation.2 | async-start | bytes 2101248 | tf_op jit(solution)/shard_map/all_gather | solution.py:84
  7.9 1539.4 %all-gather.7.cloned.1.call-start = ((), (), s32[]{:S(2)}) async-start(), calls=%async_computation.3 | async-start | bytes 2101248 | tf_op jit(solution)/shard_map/all_gather | solution.py:85
  200.8 12.3 copy-start.12
  201.3 58.3 %copy-start.13 = (s32[2]{0:T(128)S(1)}, s32[2]{0:T(128)}, u32[]{:S(2)}) copy-start(s32[2]{0:T(128)} %param.15) | copy-start | bytes 28
  201.3 58.4 %copy-start.14 = (s32[128]{0:T(128)S(1)}, s32[128]{0:T(128)}, u32[]{:S(2)}) copy-start(s32[128]{0:T(128)} %param.16) | copy-start | bytes 1540
  202.0 60.1 %all-to-all-start = ((bf16[16,32,128]{2,0,1:T(8,128)(2,1)}), bf16[16,32,128]{2,0,1:T(8,128)(2,1)S(1)}, u32[]{:S(2)}, u32[]{:S(2)}) async-start(bf16[16,32,128]{2,0,1:T(8,128)(2,1)} %copy.103), calls=%async_computation | async-start | bytes 262144 | tf_op jit(solution)/shard_map/all_to_all | solution.py:74
  213.1 1632.4 %all-reduce.3.cloned.1.call-start = ((), (), s32[]{:S(2)}) async-start(), calls=%async_computation.4 | async-start | bytes 1048576
  259.5 527.2 %copy-start.4 = (bf16[128,1024]{0,1:T(8,128)(2,1)}, bf16[128,1024]{0,1:T(8,128)(2,1)S(1)}, u32[]{:S(2)}) copy-start(bf16[128,1024]{0,1:T(8,128)(2,1)S(1)} %copy.107) | copy-start | bytes 786436
  259.9 526.7 %copy-start.11 = (f32[128,128]{1,0:T(8,128)}, f32[128,128]{1,0:T(8,128)S(1)}, u32[]{:S(2)}) copy-start(f32[128,128]{1,0:T(8,128)S(1)} %copy.110) | copy-start | bytes 196612
  260.1 527.7 %copy-start.6 = (bf16[128,1024]{0,1:T(8,128)(2,1)}, bf16[128,1024]{0,1:T(8,128)(2,1)S(1)}, u32[]{:S(2)}) copy-start(bf16[128,1024]{0,1:T(8,128)(2,1)S(1)} %copy.111) | copy-start | bytes 786436
  262.2 523.0 %copy-start.9 = (bf16[128,512]{1,0:T(8,128)(2,1)S(1)}, bf16[128,512]{1,0:T(8,128)(2,1)}, u32[]{:S(2)}) copy-start(bf16[128,512]{1,0:T(8,128)(2,1)} %param.11) | copy-start | bytes 393220
  787.8 0.7 copy-start.2
  788.5 761.6 %copy-start.7 = (bf16[128,1024]{1,0:T(8,128)(2,1)S(1)}, bf16[128,1024]{1,0:T(8,128)(2,1)}, u32[]{:S(2)}) copy-start(bf16[128,1024]{1,0:T(8,128)(2,1)} %param.19) | copy-start | bytes 786436
  1551.5 0.7 copy-start
  1551.5 2.2 copy-start.5
  1552.2 2.8 copy-start.3
  1557.2 5.3 copy-start.1
  1563.6 1.9 copy-start.8
  1565.6 8.3 copy-start.10
  1568.4 14.4 all-to-all-start.1
Sparse Core Ops, SparseCore 0:
  10.1 772.2 all-gather.4
  784.5 762.7 all-gather.6
  1565.7 279.7 all-reduce.2
where the time goes:
time: 1860 us; the launch traced here: 1850 us
  waiting for transfers between devices  1550 us (83%)
  local copies, waits for them, and re-layouts  210 us (11%)
  blocking collectives  45.9 us (2%)
    all_gather x1, waiting for transfers between devices, on_device(): lax.all_gather(w_out, ('req', 'cand'), axis=0, tiled=True)  759 us
    all_gather x1, waiting for transfers between devices, on_device(): lax.all_gather(w_query, ('req', 'cand'), axis=0, tiled=True)  520 us
    unnamed x4, waiting for transfers between devices  263 us
    gather x12, local copies, waits for them, and re-layouts, take_columns(): return jnp.take(table, indices, axis=1)  184 us
    all_gather x1, blocking collectives, on_device(): full_history = lax.all_gather(history_kv, 'cand', axis=1, tiled=True)  45.9 us
  transfers between devices with their start and end apart: 5, of which 4 were waited for; matrix products, arithmetic and copies ran while one was open for 11% of the time, Pallas kernels for 0%

commit v1 on v0

v1 whole, which is shorter than its diff:
```python
import math

import jax
import jax.numpy as jnp
from jax import lax
from jax.experimental import pallas as pl
from jax.experimental.pallas import tpu as pltpu
from jax.sharding import Mesh, PartitionSpec as P


H = 8
norm_eps = 1e-05

REQ = ("yh", "z")
CAND = ("x", "yl", "core")
ALL = REQ + CAND

LOW = 512
TILE = 256


def pooled_lookup(ids, table):
    bag, count = ids.shape
    emb, rows = table.shape
    highs = rows // LOW
    step = min(count, 4 * TILE)

    def kernel(ids_ref, table_ref, out_ref, stacked_ref):
        @pl.when(pl.program_id(0) == 0)
        def _():
            for high in range(highs):
                stacked_ref[high * emb : (high + 1) * emb, :] = table_ref[:, high * LOW : (high + 1) * LOW]

        low_iota = lax.broadcasted_iota(jnp.int32, (LOW, TILE), 0)
        for tile in range(step // TILE):
            span = slice(tile * TILE, (tile + 1) * TILE)
            total = jnp.zeros((emb, TILE), jnp.float32)
            for slot in range(bag):
                row = ids_ref[slot : slot + 1, span]
                low = jnp.bitwise_and(row, LOW - 1)
                high_of = jnp.broadcast_to(jnp.right_shift(row, LOW.bit_length() - 1), (emb, TILE))
                one_hot = (low_iota == low).astype(jnp.float32).astype(jnp.bfloat16)
                picked = jnp.dot(stacked_ref[...], one_hot, preferred_element_type=jnp.float32)
                found = jnp.zeros((emb, TILE), jnp.float32)
                for high in range(highs):
                    found = jnp.where(high_of == high, picked[high * emb : (high + 1) * emb, :], found)
                total = total + found
            out_ref[:, span] = total.astype(jnp.bfloat16)

    return pl.pallas_call(
        kernel,
        grid=(count // step,),
        in_specs=[
            pl.BlockSpec((bag, step), lambda i: (0, i)),
            pl.BlockSpec((emb, rows), lambda i: (0, 0)),
        ],
        out_specs=pl.BlockSpec((emb, step), lambda i: (0, i)),
        out_shape=jax.ShapeDtypeStruct((emb, count), jnp.bfloat16),
        scratch_shapes=[pltpu.VMEM((highs * emb, LOW), jnp.bfloat16)],
        compiler_params=pltpu.CompilerParams(vmem_limit_bytes=32 << 20),
        cost_estimate=pl.CostEstimate(
            flops=2 * emb * rows * bag * count, bytes_accessed=2 * emb * rows, transcendentals=0
        ),
        name="pooled_lookup",
    )(ids, table)


def dot_nn(left, right):
    return jnp.dot(left, right, preferred_element_type=jnp.float32)


def dot_nt(left, right):
    return lax.dot_general(left, right, (((1,), (1,)), ((), ())), preferred_element_type=jnp.float32)


def dot_tn(left, right):
    return lax.dot_general(left, right, (((0,), (0,)), ((), ())), preferred_element_type=jnp.float32)


def layer(pooled_t, dense, cot, mine, other, core, events, requests, lengths):
    pooled_width, cands = pooled_t.shape
    outer, middle, inner, width = mine.shape
    dim = width // H
    event_count = events.shape[0]
    owned = lengths.shape[0]
    scale = 1.0 / math.sqrt(dim)

    def kernel(
        core_ref, len_ref, pt_ref, dense_ref, cot_ref, mine_ref, other_ref, ev_ref, req_ref,
        out_ref, kv_ref, pool_ref, wq_ref, wo_ref,
    ):
        def place(source, target):
            for i in range(middle):
                for j in range(outer):
                    start = (i * outer + j) * inner
                    target[start : start + inner, :] = source[j, i]

        @pl.when(core_ref[0] == 0)
        def _():
            place(mine_ref, wq_ref)
            place(other_ref, wo_ref)

        @pl.when(core_ref[0] != 0)
        def _():
            place(other_ref, wq_ref)
            place(mine_ref, wo_ref)

        pooled = jnp.transpose(pt_ref[...].astype(jnp.float32))
        query_pre = dot_nn(pooled.astype(jnp.bfloat16), wq_ref[:pooled_width, :]) + dot_nn(
            dense_ref[...], wq_ref[pooled_width:, :]
        )
        gate = jax.nn.sigmoid(query_pre)
        query = (query_pre * gate).astype(jnp.bfloat16)
        query_slope = gate * (1.0 + query_pre * (1.0 - gate))

        index = lax.broadcasted_iota(jnp.int32, (cands, event_count), 1)
        owner = index % owned
        limit = jnp.full((cands, event_count), len_ref[0], jnp.int32)
        for a in range(1, owned):
            limit = jnp.where(owner == a, len_ref[a], limit)
        live = ((owner == req_ref[...]) & (index // owned < limit)).astype(jnp.float32)

        weights, slopes, attended = [], [], []
        for h in range(H):
            cols = slice(h * dim, (h + 1) * dim)
            vcols = slice(width + h * dim, width + (h + 1) * dim)
            score = dot_nt(query[:, cols], ev_ref[:, cols]) * scale
            sig = jax.nn.sigmoid(score)
            weight = (score * sig * live).astype(jnp.bfloat16)
            weights.append(weight)
            slopes.append(live * (sig * (1.0 + score * (1.0 - sig))) * scale)
            attended.append(dot_nn(weight, ev_ref[:, vcols]))
        attended = jnp.concatenate(attended, axis=1)
        centered = attended - jnp.mean(attended, axis=1, keepdims=True)
        inverse = lax.rsqrt(jnp.mean(centered * centered, axis=1, keepdims=True) + norm_eps)
        normed = centered * inverse
        mixed = dot_nn(normed.astype(jnp.bfloat16), wo_ref[...])
        out_ref[:, :pooled_width] = (mixed[:, :pooled_width] + pooled).astype(jnp.bfloat16)
        out_ref[:, pooled_width:] = (mixed[:, pooled_width:] + dense_ref[...].astype(jnp.float32)).astype(
            jnp.bfloat16
        )
        back_y = dot_nt(cot_ref[...], wo_ref[...])
        back_att = inverse * (
            back_y
            - jnp.mean(back_y, axis=1, keepdims=True)
            - normed * jnp.mean(back_y * normed, axis=1, keepdims=True)
        )
        back_att = back_att.astype(jnp.bfloat16)
        back_query = []
        for h in range(H):
            cols = slice(h * dim, (h + 1) * dim)
            vcols = slice(width + h * dim, width + (h + 1) * dim)
            back_w = dot_nt(back_att[:, cols], ev_ref[:, vcols])
            back_s = (back_w * slopes[h]).astype(jnp.bfloat16)
            back_query.append(dot_nn(back_s, ev_ref[:, cols]))
            kv_ref[:, cols] = dot_tn(back_s, query[:, cols]).astype(jnp.bfloat16)
            kv_ref[:, vcols] = dot_tn(weights[h], back_att[:, cols]).astype(jnp.bfloat16)
        back_pre = (jnp.concatenate(back_query, axis=1) * query_slope).astype(jnp.bfloat16)
        columns = dot_nt(wq_ref[:pooled_width, :], back_pre)
        pool_ref[...] = (jnp.transpose(cot_ref[:, :pooled_width].astype(jnp.float32)) + columns).astype(
            jnp.bfloat16
        )

    vmem = pl.BlockSpec(memory_space=pltpu.VMEM)
    return pl.pallas_call(
        kernel,
        in_specs=[pl.BlockSpec(memory_space=pltpu.SMEM)] * 2 + [vmem] * 7,
        out_specs=[vmem] * 3,
        out_shape=[
            jax.ShapeDtypeStruct((cands, width), jnp.bfloat16),
            jax.ShapeDtypeStruct((event_count, 2 * width), jnp.bfloat16),
            jax.ShapeDtypeStruct((pooled_width, cands), jnp.bfloat16),
        ],
        scratch_shapes=[pltpu.VMEM((width, width), jnp.bfloat16)] * 2,
        compiler_params=pltpu.CompilerParams(vmem_limit_bytes=40 << 20),
        cost_estimate=pl.CostEstimate(
            flops=8 * cands * width * width, bytes_accessed=8 * width * width, transcendentals=0
        ),
        name="layer",
    )(core, lengths, pooled_t, dense, cot, mine, other, events, requests)


def spread(block, axes):
    size = math.prod(lax.axis_size(a) for a in axes)
    return lax.all_to_all(jnp.broadcast_to(block[None], (size,) + block.shape), axes, 0, 0)


def on_device(dense_feat, emb_ids, tables, history_kv, hist_len, cand_request, w_query, w_out, cotangent):
    _, emb_width, _ = tables.shape
    sizes = {a: lax.axis_size(a) for a in ALL}
    cand_devices = sizes["x"] * sizes["yl"] * sizes["core"]
    own_rows, model_width = w_query.shape
    owned, own_events, kv_width = history_kv.shape
    group = emb_ids.shape[2]
    cands = group // cand_devices

    own = jnp.concatenate([w_query, w_out], axis=0).reshape(1, 2, own_rows, model_width)
    slab = sizes["yh"] * sizes["z"] * sizes["yl"]
    own = jnp.broadcast_to(own, (slab, 2, own_rows, model_width)).reshape(2 * slab, own_rows, model_width)
    w1 = lax.all_to_all(own, ("yh", "z", "yl", "core"), 0, 0).reshape(2 * slab * own_rows, model_width)
    own_hist = jnp.transpose(history_kv, (1, 0, 2)).reshape(own_events * owned, kv_width)
    events = spread(own_hist, CAND).reshape(cand_devices * own_events * owned, kv_width)

    pooled_rows = pooled_lookup(emb_ids[0], tables[0])

    mine = spread(w1, ("x",))
    mine = mine.reshape(sizes["x"], sizes["yh"] * sizes["z"], -1, model_width)
    other = lax.ppermute(mine, "core", [(0, 1), (1, 0)])

    sent = jnp.transpose(pooled_rows.reshape(emb_width, cand_devices, cands), (1, 0, 2))
    pooled_t = lax.all_to_all(sent, CAND, 0, 0).reshape(-1, cands)

    cand_out, kv_part, back_pool = layer(
        pooled_t,
        dense_feat,
        cotangent,
        mine,
        other,
        lax.axis_index("core").reshape(1),
        events,
        cand_request.reshape(-1, 1),
        hist_len,
    )

    own = own_events * owned
    joined = jnp.concatenate(
        [kv_part.reshape(cand_devices, own, kv_width), back_pool.reshape(cand_devices, own, -1)], axis=2
    )
    back = lax.all_to_all(joined, CAND, 0, 0)
    d_kv = jnp.sum(back[:, :, :kv_width].astype(jnp.float32), axis=0)
    d_kv = jnp.transpose(d_kv.reshape(own_events, owned, kv_width), (1, 0, 2))
    pool_all = back[:, :, kv_width:].reshape(cand_devices, emb_width, cands)
    d_pooled = jnp.transpose(pool_all, (1, 0, 2)).reshape(1, emb_width, group)
    return cand_out, d_kv, d_pooled


def solution(mesh):
    parts = Mesh(mesh.devices.reshape(2, 8, 4, 4, 2), ALL)
    rows = P(ALL, None)
    return jax.shard_map(
        on_device,
        mesh=parts,
        in_specs=(
            rows,
            P(CAND, None, REQ),
            P(CAND, None, None),
            P(REQ, CAND, None),
            P(REQ),
            P(ALL),
            rows,
            rows,
            rows,
        ),
        out_specs=(rows, P(REQ, CAND, None), P(CAND, None, REQ)),
        check_vma=False,
    )
```

time: 1860 us -> 150 us (0.08)
  waiting for transfers between devices: 1550 us -> 7.4 us
  local copies, waits for them, and re-layouts: 210 us -> 8.1 us
  blocking collectives: 45.9 us -> 89.4 us
  Pallas kernels: 0 us -> 25.4 us
    all_gather x2 -> x0, waiting for transfers between devices: 1280 us -> none  [the longest x1 759 us: on_device(): lax.all_gather(w_out, ('req', 'cand'), axis=0, tiled=True)]
    unnamed x4 -> x0, waiting for transfers between devices: 263 us -> none
    gather x12 -> x0, local copies, waits for them, and re-layouts: 184 us -> none  [take_columns(): return jnp.take(table, indices, axis=1)]
    all_to_all x0 -> x3, blocking collectives: none -> 89.4 us  [the longest x1 37.8 us: on_device(): lax.all_to_all(own, ('yh', 'z', 'yl', 'core'), 0, 0)]
    all_gather x1 -> x0, blocking collectives: 45.9 us -> none  [on_device(): full_history = lax.all_gather(history_kv, 'cand', axis=1, tiled=True)]
    pallas_call x0 -> x2, Pallas kernels: none -> 25.4 us  [the longest x1 18.3 us: pooled_lookup(): pl.pallas_call(kernel, grid=(count // step,), in_specs=[pl.BlockSpec((bag...]
  transfers between devices with their start and end apart: 5 -> 3, of which waited for: 4 -> 1; matrix products, arithmetic and copies ran while one was open for 11% -> 2% of each run, Pallas kernels for 0% -> 12%
where the time goes in v1:
time: 150 us; the launch traced here: 149 us
  blocking collectives  89.4 us (60%)
  Pallas kernels  25.4 us (17%)
  starting transfers between devices  16.6 us (11%)
  local copies, waits for them, and re-layouts  8.1 us (5%)
  waiting for transfers between devices  7.4 us (5%)
    all_to_all x1, blocking collectives, on_device(): lax.all_to_all(own, ('yh', 'z', 'yl', 'core'), 0, 0)  37.8 us
    all_to_all x1, blocking collectives, spread(): lax.all_to_all(jnp.broadcast_to(block[None], (size,) + block.shape), axes...  28.7 us
    all_to_all x1, blocking collectives, on_device(): back = lax.all_to_all(joined, CAND, 0, 0)  22.9 us
    pallas_call x1, Pallas kernels, pooled_lookup(): pl.pallas_call(kernel, grid=(count // step,), in_specs=[pl.BlockSpec((bag...  18.3 us
    all_to_all x1, starting transfers between devices, on_device(): pooled_t = lax.all_to_all(sent, CAND, 0, 0).reshape(-1, cands)  7.69 us
    all_to_all x1, waiting for transfers between devices, on_device(): pooled_t = lax.all_to_all(sent, CAND, 0, 0).reshape(-1, cands)  7.39 us
    pallas_call x1, Pallas kernels, layer(): pl.pallas_call(kernel, in_specs=[pl.BlockSpec(memory_space=pltpu.SMEM)] *...  7.12 us
    all_to_all x1, starting transfers between devices, spread(): lax.all_to_all(jnp.broadcast_to(block[None], (size,) + block.shape), axes...  4.45 us
  transfers between devices with their start and end apart: 3, of which 1 were waited for; matrix products, arithmetic and copies ran while one was open for 2% of the time, Pallas kernels for 12%

profile of v1, /device:TPU:1, one launch (start us, length us, event | category | flops | bytes accessed | tf_op | source)
XLA Modules:
  0.0 149.0 jit_solution(17002935745055660155)
XLA Ops:
  0.6 0.7 pad_maximum_fusion.1
  1.4 0.3 broadcast_in_dim.22
  1.6 37.8 %all_to_all.25 = bf16[128,2,1024]{2,1,0:T(2,128)(2,1)S(1)} all-to-all(bf16[128,2,1024]{2,1,0:T(2,128)(2,1)S(1)} %bitcast.24), channel_id=1, replica_groups=mesh['yh'=2,'z'=8,'x'=4,'yl'=4,'core'=2] {'yh','z','yl','core'}, dimensions={0} | all-to-all | bytes 1048576 | tf_op jit(solution)/shard_map/all_to_all | solution.py:200
  39.4 0.2 broadcast_in_dim.23
  39.6 0.3 broadcast_in_dim.24
  39.9 28.7 %all_to_all.26 = bf16[4,256,1024]{2,1,0:T(8,128)(2,1)S(1)} all-to-all(bf16[4,256,1024]{2,1,0:T(8,128)(2,1)S(1)} %broadcast_in_dim.24), channel_id=1, replica_groups=mesh['yh'=2,'z'=8,'x'=4,'yl'=4,'core'=2] {'x'}, dimensions={0} | all-to-all | bytes 4194304 | tf_op jit(solution)/shard_map/all_to_all | solution.py:185
  68.6 4.4 %collective-permute-start = (bf16[4,16,16,1024]{3,2,1,0:T(8,128)(2,1)S(1)}, bf16[4,16,16,1024]{3,2,1,0:T(8,128)(2,1)}, u32[]{:S(2)}, u32[]{:S(2)}) collective-permute-start(bf16[4,16,16,1024]{3,2,1,0:T(8,128)(2,1)S(1)} %bitcast.19), channel_id=1, source_target_pairs={{0,1},{1,0},{2,3},{3,2},{4,5},{5,4},{6,7},{7,6},{8,9},{9,8},{10,11... | collective-permute-start | bytes 6291464 | tf_op jit(solution)/shard_map/ppermute | solution.py:208
  73.1 1.0 broadcast_in_dim.26
  74.2 4.5 %all-to-all-start.3 = ((bf16[32,4,2048]{2,1,0:T(4,128)(2,1)}), bf16[32,4,2048]{2,1,0:T(4,128)(2,1)}, u32[]{:S(2)}, u32[]{:S(2)}) async-start(bf16[32,4,2048]{2,1,0:T(4,128)(2,1)} %broadcast_in_dim.26), calls=%async_computation.3 | async-start | bytes 1048576 | tf_op jit(solution)/shard_map/all_to_all | solution.py:185
  78.7 18.3 %pooled_lookup.1 = bf16[16,4096]{1,0:T(8,128)(2,1)S(1)} custom-call(s32[4,4096]{1,0:T(4,128)S(1)} %bitcast.23, bf16[16,32768]{1,0:T(8,128)(2,1)S(1)} %bitcast.22), custom_call_target="tpu_custom_call" | custom-call | flops 17179869184 | bytes 1048576 | tf_op jit(solution)/shard_map/pooled_lookup/pallas_call | solution.py:50
  97.0 0.7 bitcast_bitcast_fusion
  97.7 7.7 %all-to-all-start = ((bf16[32,16,128]{2,1,0:T(8,128)(2,1)}), bf16[32,16,128]{2,1,0:T(8,128)(2,1)S(1)}, u32[]{:S(2)}, u32[]{:S(2)}) async-start(bf16[32,16,128]{2,1,0:T(8,128)(2,1)} %bitcast_bitcast_fusion), calls=%async_computation | async-start | bytes 262144 | tf_op jit(solution)/shard_map/all_to_all | solution.py:211
  105.5 1.2 reshape.51.ev_ref
  106.7 7.4 %all-to-all-done = bf16[32,16,128]{2,1,0:T(8,128)(2,1)S(1)} async-done(((bf16[32,16,128]{2,1,0:T(8,128)(2,1)}), bf16[32,16,128]{2,1,0:T(8,128)(2,1)S(1)}, u32[]{:S(2)}, u32[]{:S(2)}) %all-to-all-start) | async-done | bytes 131104 | tf_op jit(solution)/shard_map/all_to_all | solution.py:211
  114.1 0.9 copy-done
  115.0 7.1 %layer.1 = (bf16[128,1024]{1,0:T(8,128)(2,1)}, bf16[128,2048]{1,0:T(8,128)(2,1)S(1)}, bf16[512,128]{1,0:T(8,128)(2,1)S(1)}) custom-call(s32[1]{0:T(128)} %bitcast.core_ref, s32[2]{0:T(128)S(1)} %copy-done.3, bf16[512,128]{1,0:T(8,128)(2,1)S(1)} %bitcast.21, bf16[128,512]{1,0:T(8,128)(2,1)S(1)} %copy-done.1, bf16[128,1024]{1,0:T(8,128)(2,1)S(1)} %copy-done, ...), custom_call_target="tpu_custom_call" | custom-call | flops 1073741824 | bytes 8388608 | tf_op jit(solution)/shard_map/layer/pallas_call | solution.py:165
  122.1 0.6 copy-done.2
  122.8 1.0 reshape.54
  123.8 0.2 reshape.53
  124.0 0.3 pad_maximum_fusion
  124.3 22.9 %all_to_all.27 = bf16[32,4,2560]{2,1,0:T(4,128)(2,1)S(1)} all-to-all(bf16[32,4,2560]{2,1,0:T(4,128)(2,1)S(1)} %pad_maximum_fusion), channel_id=1, replica_groups=mesh['yh'=2,'z'=8,'x'=4,'yl'=4,'core'=2] {'x','yl','core'}, dimensions={0} | all-to-all | bytes 1310720 | tf_op jit(solution)/shard_map/all_to_all | solution.py:229
  147.3 0.7 reshape.57
  148.1 0.2 convert_reduce_fusion
  148.3 0.6 copy.19
  (24 shorter events, 0.4 us)
Async XLA Ops:
  39.9 33.2 %copy-start.6 = (bf16[2,2,2048]{2,1,0:T(2,128)(2,1)S(1)}, bf16[2,2,2048]{2,1,0:T(2,128)(2,1)}, u32[]{:S(2)}) copy-start(bf16[2,2,2048]{2,1,0:T(2,128)(2,1)} %param.12) | copy-start | bytes 49156
  39.9 38.7 %copy-start.4 = (bf16[1,16,32768]{2,1,0:T(8,128)(2,1)S(1)}, bf16[1,16,32768]{2,1,0:T(8,128)(2,1)}, u32[]{:S(2)}) copy-start(bf16[1,16,32768]{2,1,0:T(8,128)(2,1)} %param.11) | copy-start | bytes 3145732
  39.9 38.7 %copy-start.5 = (s32[1,4,4096]{2,1,0:T(4,128)S(1)}, s32[1,4,4096]{2,1,0:T(4,128)}, u32[]{:S(2)}) copy-start(s32[1,4,4096]{2,1,0:T(4,128)} %param.10) | copy-start | bytes 196612
  68.6 45.4 %collective-permute-start = (bf16[4,16,16,1024]{3,2,1,0:T(8,128)(2,1)S(1)}, bf16[4,16,16,1024]{3,2,1,0:T(8,128)(2,1)}, u32[]{:S(2)}, u32[]{:S(2)}) collective-permute-start(bf16[4,16,16,1024]{3,2,1,0:T(8,128)(2,1)S(1)} %bitcast.19), channel_id=1, source_target_pairs={{0,1},{1,0},{2,3},{3,2},{4,5},{5,4},{6,7},{7,6},{8,9},{9,8},{10,11... | collective-permute-start | bytes 6291464 | tf_op jit(solution)/shard_map/ppermute | solution.py:208
  74.2 23.5 %all-to-all-start.3 = ((bf16[32,4,2048]{2,1,0:T(4,128)(2,1)}), bf16[32,4,2048]{2,1,0:T(4,128)(2,1)}, u32[]{:S(2)}, u32[]{:S(2)}) async-start(bf16[32,4,2048]{2,1,0:T(4,128)(2,1)} %broadcast_in_dim.26), calls=%async_computation.3 | async-start | bytes 1048576 | tf_op jit(solution)/shard_map/all_to_all | solution.py:185
  78.6 26.7 %copy-start.7 = (s32[128]{0:T(128)S(1)}, s32[128]{0:T(128)}, u32[]{:S(2)}) copy-start(s32[128]{0:T(128)} %param.14) | copy-start | bytes 1540
  78.7 35.4 %copy-start.1 = (bf16[128,512]{1,0:T(8,128)(2,1)S(1)}, bf16[128,512]{1,0:T(8,128)(2,1)}, u32[]{:S(2)}) copy-start(bf16[128,512]{1,0:T(8,128)(2,1)} %dense_ref.1) | copy-start | bytes 393220
  78.7 35.4 %copy-start.3 = (s32[2]{0:T(128)S(1)}, s32[2]{0:T(128)}, u32[]{:S(2)}) copy-start(s32[2]{0:T(128)} %len_ref.1) | copy-start | bytes 28
  97.7 16.4 %all-to-all-start = ((bf16[32,16,128]{2,1,0:T(8,128)(2,1)}), bf16[32,16,128]{2,1,0:T(8,128)(2,1)S(1)}, u32[]{:S(2)}, u32[]{:S(2)}) async-start(bf16[32,16,128]{2,1,0:T(8,128)(2,1)} %bitcast_bitcast_fusion), calls=%async_computation | async-start | bytes 262144 | tf_op jit(solution)/shard_map/all_to_all | solution.py:211
  114.1 1.0 copy-start
  122.1 0.7 copy-start.2

commit v2 on v1

--- a/solution.py
+++ b/solution.py
@@ -14,6 +14,7 @@
 REQ = ("yh", "z")
 CAND = ("x", "yl", "core")
 ALL = REQ + CAND
+
 
 LOW = 512
 TILE = 256
@@ -77,33 +78,47 @@
     return lax.dot_general(left, right, (((0,), (0,)), ((), ())), preferred_element_type=jnp.float32)
 
 
-def layer(pooled_t, dense, cot, mine, other, core, events, requests, lengths):
+def layer(pooled_t, dense, cot, mine, other, place_index, events, requests, lengths):
     pooled_width, cands = pooled_t.shape
-    outer, middle, inner, width = mine.shape
+    own_shape, _, _ = (piece.shape for piece in mine)
+    width = own_shape[1]
+    block = own_shape[0]
+    outer = width // block
+    inner = 16
     dim = width // H
     event_count = events.shape[0]
     owned = lengths.shape[0]
     scale = 1.0 / math.sqrt(dim)
 
     def kernel(
-        core_ref, len_ref, pt_ref, dense_ref, cot_ref, mine_ref, other_ref, ev_ref, req_ref,
+        place_ref, len_ref, pt_ref, dense_ref, cot_ref,
+        own_a, sides_a, far_a, own_b, sides_b, far_b, ev_ref, req_ref,
         out_ref, kv_ref, pool_ref, wq_ref, wo_ref,
     ):
-        def place(source, target):
-            for i in range(middle):
-                for j in range(outer):
-                    start = (i * outer + j) * inner
-                    target[start : start + inner, :] = source[j, i]
-
-        @pl.when(core_ref[0] == 0)
+        x = place_ref[1]
+
+        def place(own, sides, far, target):
+            def put(source, first, offset):
+                for i in range(source.shape[0] // inner):
+                    start = pl.multiple_of(((first + i) * outer + lax.rem(x + offset, outer)) * inner, inner)
+                    target[pl.ds(start, inner), :] = source[i * inner : (i + 1) * inner, :]
+
+            put(own, 0, 0)
+            put(sides.at[0], 0, outer - 1)
+            put(sides.at[1], 0, 1)
+            half = block // inner // 2
+            put(far.at[0], 0, 2)
+            put(far.at[1], half, 2)
+
+        @pl.when(place_ref[0] == 0)
         def _():
-            place(mine_ref, wq_ref)
-            place(other_ref, wo_ref)
-
-        @pl.when(core_ref[0] != 0)
+            place(own_a, sides_a, far_a, wq_ref)
+            place(own_b, sides_b, far_b, wo_ref)
+
+        @pl.when(place_ref[0] != 0)
         def _():
-            place(other_ref, wq_ref)
-            place(mine_ref, wo_ref)
+            place(own_b, sides_b, far_b, wq_ref)
+            place(own_a, sides_a, far_a, wo_ref)
 
         pooled = jnp.transpose(pt_ref[...].astype(jnp.float32))
         query_pre = dot_nn(pooled.astype(jnp.bfloat16), wq_ref[:pooled_width, :]) + dot_nn(
@@ -164,7 +179,7 @@
     vmem = pl.BlockSpec(memory_space=pltpu.VMEM)
     return pl.pallas_call(
         kernel,
-        in_specs=[pl.BlockSpec(memory_space=pltpu.SMEM)] * 2 + [vmem] * 7,
+        in_specs=[pl.BlockSpec(memory_space=pltpu.SMEM)] * 2 + [vmem] * 11,
         out_specs=[vmem] * 3,
         out_shape=[
             jax.ShapeDtypeStruct((cands, width), jnp.bfloat16),
@@ -177,12 +192,7 @@
             flops=8 * cands * width * width, bytes_accessed=8 * width * width, transcendentals=0
         ),
         name="layer",
-    )(core, lengths, pooled_t, dense, cot, mine, other, events, requests)
-
-
-def spread(block, axes):
-    size = math.prod(lax.axis_size(a) for a in axes)
-    return lax.all_to_all(jnp.broadcast_to(block[None], (size,) + block.shape), axes, 0, 0)
+    )(place_index, lengths, pooled_t, dense, cot, *mine, *other, events, requests)
 
 
 def on_device(dense_feat, emb_ids, tables, history_kv, hist_len, cand_request, w_query, w_out, cotangent):
@@ -198,31 +208,48 @@
     slab = sizes["yh"] * sizes["z"] * sizes["yl"]
     own = jnp.broadcast_to(own, (slab, 2, own_rows, model_width)).reshape(2 * slab, own_rows, model_width)
     w1 = lax.all_to_all(own, ("yh", "z", "yl", "core"), 0, 0).reshape(2 * slab * own_rows, model_width)
-    own_hist = jnp.transpose(history_kv, (1, 0, 2)).reshape(own_events * owned, kv_width)
-    events = spread(own_hist, CAND).reshape(cand_devices * own_events * owned, kv_width)
-
-    pooled_rows = pooled_lookup(emb_ids[0], tables[0])
-
-    mine = spread(w1, ("x",))
-    mine = mine.reshape(sizes["x"], sizes["yh"] * sizes["z"], -1, model_width)
-    other = lax.ppermute(mine, "core", [(0, 1), (1, 0)])
-
-    sent = jnp.transpose(pooled_rows.reshape(emb_width, cand_devices, cands), (1, 0, 2))
-    pooled_t = lax.all_to_all(sent, CAND, 0, 0).reshape(-1, cands)
+    half = group // 2
+    pooled_a = pooled_lookup(emb_ids[0, :, :half], tables[0])
+
+    ring = sizes["x"]
+    up = [(i, (i + 1) % ring) for i in range(ring)]
+    down = [(i, (i - 1) % ring) for i in range(ring)]
+    swap = [(0, 1), (1, 0)]
+    left = lax.ppermute(w1, "x", up)
+    right = lax.ppermute(w1, "x", down)
+    other_own = lax.ppermute(w1, "core", swap)
+
+    pooled_b = pooled_lookup(emb_ids[0, :, half:], tables[0])
+
+    own = own_events * owned
+    own_hist = jnp.transpose(history_kv, (1, 0, 2)).reshape(1, own, kv_width)
+    sent = jnp.concatenate([pooled_a, pooled_b], axis=1).reshape(emb_width, cand_devices, cands)
+    sent = jnp.transpose(sent, (1, 0, 2)).reshape(cand_devices, own, -1)
+    joined = jnp.concatenate([jnp.broadcast_to(own_hist, (cand_devices, own, kv_width)), sent], axis=2)
+    front = lax.all_to_all(joined, CAND, 0, 0)
+    events = front[:, :, :kv_width].reshape(cand_devices * own, kv_width)
+    pooled_t = front[:, :, kv_width:].reshape(-1, cands)
+
+    middle = w1.shape[0] // 2
+    far_a = lax.ppermute(left[:middle], "x", up)
+    far_b = lax.ppermute(right[middle:], "x", down)
+    sides = jnp.stack([left, right])
+    other_sides = lax.ppermute(sides, "core", swap)
+    far = jnp.stack([far_a, far_b])
+    other_far = lax.ppermute(far, "core", swap)
 
     cand_out, kv_part, back_pool = layer(
         pooled_t,
         dense_feat,
         cotangent,
-        mine,
-        other,
-        lax.axis_index("core").reshape(1),
+        (w1, sides, far),
+        (other_own, other_sides, other_far),
+        jnp.stack([lax.axis_index("core"), lax.axis_index("x")]),
         events,
         cand_request.reshape(-1, 1),
         hist_len,
     )
 
-    own = own_events * owned
     joined = jnp.concatenate(
         [kv_part.reshape(cand_devices, own, kv_width), back_pool.reshape(cand_devices, own, -1)], axis=2
     )

time: 150 us -> 128 us (0.85)
  blocking collectives: 89.4 us -> 23.5 us
  starting transfers between devices: 16.6 us -> 51 us
  local copies, waits for them, and re-layouts: 8.1 us -> 13.7 us
  waiting for transfers between devices: 7.4 us -> 10.3 us
    all_to_all x2 -> x0, blocking collectives: 66.5 us -> none  [the longest x1 37.8 us: on_device(): lax.all_to_all(own, ('yh', 'z', 'yl', 'core'), 0, 0)]
    ppermute x1 -> x7, starting transfers between devices: 4.42 us -> 25.4 us  [the longest x1 8.41 us: on_device(): other_sides = lax.ppermute(sides, 'core', swap)]
    all_to_all x2, starting transfers between devices: 12.1 us -> 25.6 us  [the longest x1 18.4 us: on_device(): lax.all_to_all(own, ('yh', 'z', 'yl', 'core'), 0, 0)]
    ppermute x1 -> x7, waiting for transfers between devices: 0.01 us -> 9.22 us  [the longest x1 4.29 us: on_device(): left = lax.ppermute(w1, 'x', up)]
    all_to_all x2, waiting for transfers between devices: 7.4 us -> 1.07 us  [the longest x1 1.07 us: on_device(): lax.all_to_all(own, ('yh', 'z', 'yl', 'core'), 0, 0)]
    slice x0 -> x4, local copies, waits for them, and re-layouts: none -> 2.73 us  [the longest x1 1.61 us: on_device(): pooled_t = front[:, :, kv_width:].reshape(-1, cands)]
    unnamed x17 -> x22, local copies, waits for them, and re-layouts: 2.27 us -> 3.93 us
    pallas_call x1 -> x2, Pallas kernels: 18.3 us -> 18.4 us  [pooled_lookup(): pl.pallas_call(kernel, grid=(count // step,), in_specs=[pl.BlockSpec((bag...]
  transfers between devices with their start and end apart: 3 -> 9, of which waited for: 1 -> 4; matrix products, arithmetic and copies ran while one was open for 2% -> 5% of each run, Pallas kernels for 12% -> 14%
where the time goes in v2:
time: 128 us; the launch traced here: 127 us
  starting transfers between devices  51 us (40%)
  Pallas kernels  25.1 us (20%)
  blocking collectives  23.5 us (18%)
  local copies, waits for them, and re-layouts  13.7 us (11%)
  waiting for transfers between devices  10.3 us (8%)
  other arithmetic  2.74 us (2%)
    all_to_all x1, blocking collectives, on_device(): back = lax.all_to_all(joined, CAND, 0, 0)  23.5 us
    all_to_all x1, starting transfers between devices, on_device(): lax.all_to_all(own, ('yh', 'z', 'yl', 'core'), 0, 0)  18.4 us
    pallas_call x2, Pallas kernels, pooled_lookup(): pl.pallas_call(kernel, grid=(count // step,), in_specs=[pl.BlockSpec((bag...  18.4 us
    ppermute x1, starting transfers between devices, on_device(): other_sides = lax.ppermute(sides, 'core', swap)  8.41 us
    all_to_all x1, starting transfers between devices, on_device(): front = lax.all_to_all(joined, CAND, 0, 0)  7.14 us
    pallas_call x1, Pallas kernels, layer(): pl.pallas_call(kernel, in_specs=[pl.BlockSpec(memory_space=pltpu.SMEM)] *...  6.71 us
    ppermute x1, starting transfers between devices, on_device(): right = lax.ppermute(w1, 'x', down)  4.39 us
    ppermute x1, waiting for transfers between devices, on_device(): left = lax.ppermute(w1, 'x', up)  4.29 us
  transfers between devices with their start and end apart: 9, of which 4 were waited for; matrix products, arithmetic and copies ran while one was open for 5% of the time, Pallas kernels for 14%

profile of v2, /device:TPU:1, one launch (start us, length us, event | category | flops | bytes accessed | tf_op | source)
XLA Modules:
  0.0 127.3 jit_solution(15414763577948888376)
XLA Ops:
  1.5 1.1 broadcast_in_dim.17
  2.5 18.4 %all-to-all-start.1 = ((bf16[128,2,1024]{2,1,0:T(2,128)(2,1)}), bf16[128,2,1024]{2,1,0:T(2,128)(2,1)S(1)}, u32[]{:S(2)}, u32[]{:S(2)}) async-start(bf16[128,2,1024]{2,1,0:T(2,128)(2,1)} %bitcast.7), calls=%async_computation.1 | async-start | bytes 1048576 | tf_op jit(solution)/shard_map/all_to_all | solution.py:210
  21.0 9.2 %pooled_lookup.2 = bf16[16,2048]{1,0:T(8,128)(2,1)S(1)} custom-call(s32[4,2048]{1,0:T(4,128)S(1)} %get-tuple-element.12.ids_ref, bf16[16,32768]{1,0:T(8,128)(2,1)S(1)} %bitcast.23), custom_call_target="tpu_custom_call" | custom-call | flops 8589934592 | bytes 1048576 | tf_op jit(solution)/shard_map/pooled_lookup/pallas_call | solution.py:51
  30.3 9.2 %pooled_lookup.3 = bf16[16,2048]{1,0:T(8,128)(2,1)S(1)} custom-call(s32[4,2048]{1,0:T(4,128)S(1)} %get-tuple-element.13.ids_ref, bf16[16,32768]{1,0:T(8,128)(2,1)S(1)} %bitcast.24), custom_call_target="tpu_custom_call" | custom-call | flops 8589934592 | bytes 1048576 | tf_op jit(solution)/shard_map/pooled_lookup/pallas_call | solution.py:51
  39.4 1.1 all-to-all-done.1
  40.7 4.4 %collective-permute-start.1 = (bf16[256,1024]{1,0:T(8,128)(2,1)S(1)}, bf16[256,1024]{1,0:T(8,128)(2,1)S(1)}, u32[]{:S(2)}, u32[]{:S(2)}) collective-permute-start(bf16[256,1024]{1,0:T(8,128)(2,1)S(1)} %reshape.50.own_a), channel_id=1, source_target_pairs={{0,24},{8,0},{16,8},{24,16},{1,25},{9,1},{17,9},{25,17},{2,26},{10... | collective-permute-start | bytes 1572872 | tf_op jit(solution)/shard_map/ppermute | solution.py:219
  45.1 1.9 %collective-permute-start = (bf16[256,1024]{1,0:T(8,128)(2,1)S(1)}, bf16[256,1024]{1,0:T(8,128)(2,1)S(1)}, u32[]{:S(2)}, u32[]{:S(2)}) collective-permute-start(bf16[256,1024]{1,0:T(8,128)(2,1)S(1)} %reshape.50.own_a), channel_id=1, source_target_pairs={{0,8},{8,16},{16,24},{24,0},{1,9},{9,17},{17,25},{25,1},{2,10},{10... | collective-permute-start | bytes 1572872 | tf_op jit(solution)/shard_map/ppermute | solution.py:218
  47.5 1.2 pad_maximum_fusion.1
  48.6 7.1 %all-to-all-start = ((bf16[32,4,2560]{2,1,0:T(4,128)(2,1)}), bf16[32,4,2560]{2,1,0:T(4,128)(2,1)S(1)}, u32[]{:S(2)}, u32[]{:S(2)}) async-start(bf16[32,4,2560]{2,1,0:T(4,128)(2,1)} %pad_maximum_fusion.1), calls=%async_computation | async-start | bytes 1310720 | tf_op jit(solution)/shard_map/all_to_all | solution.py:229
  55.8 4.3 %collective-permute-done = bf16[256,1024]{1,0:T(8,128)(2,1)S(1)} collective-permute-done((bf16[256,1024]{1,0:T(8,128)(2,1)S(1)}, bf16[256,1024]{1,0:T(8,128)(2,1)S(1)}, u32[]{:S(2)}, u32[]{:S(2)}) %collective-permute-start) | collective-permute-done | bytes 524320 | tf_op jit(solution)/shard_map/ppermute | solution.py:218
  60.2 8.4 %collective-permute-start.5 = (bf16[2,256,1024]{2,1,0:T(8,128)(2,1)S(1)}, bf16[2,256,1024]{2,1,0:T(8,128)(2,1)}, u32[]{:S(2)}, u32[]{:S(2)}) collective-permute-start(bf16[2,256,1024]{2,1,0:T(8,128)(2,1)S(1)} %pad_maximum_fusion.sides_a), channel_id=1, source_target_pairs={{0,1},{1,0},{2,3},{3,2},{4,5},{5,4},{6,7},{7,6},{8,9},{9,8},{10,11... | collective-permute-start | bytes 3145736 | tf_op jit(solution)/shard_map/ppermute | solution.py:237
  68.6 1.9 %collective-permute-start.3 = (bf16[128,1024]{1,0:T(8,128)(2,1)S(1)}, bf16[128,1024]{1,0:T(8,128)(2,1)S(1)}, u32[]{:S(2)}, u32[]{:S(2)}) collective-permute-start(bf16[128,1024]{1,0:T(8,128)(2,1)S(1)} %slice.34), channel_id=1, source_target_pairs={{0,24},{8,0},{16,8},{24,16},{1,25},{9,1},{17,9},{25,17},{2,26},{10... | collective-permute-start | bytes 786440 | tf_op jit(solution)/shard_map/ppermute | solution.py:235
  70.6 3.4 %collective-permute-start.2 = (bf16[128,1024]{1,0:T(8,128)(2,1)S(1)}, bf16[128,1024]{1,0:T(8,128)(2,1)S(1)}, u32[]{:S(2)}, u32[]{:S(2)}) collective-permute-start(bf16[128,1024]{1,0:T(8,128)(2,1)S(1)} %slice.33), channel_id=1, source_target_pairs={{0,8},{8,16},{16,24},{24,0},{1,9},{9,17},{17,25},{25,1},{2,10},{10... | collective-permute-start | bytes 786440 | tf_op jit(solution)/shard_map/ppermute | solution.py:234
  74.0 2.7 %collective-permute-start.4 = (bf16[256,1024]{1,0:T(8,128)(2,1)S(1)}, bf16[256,1024]{1,0:T(8,128)(2,1)S(1)}, u32[]{:S(2)}, u32[]{:S(2)}) collective-permute-start(bf16[256,1024]{1,0:T(8,128)(2,1)S(1)} %reshape.50.own_a), channel_id=1, source_target_pairs={{0,1},{1,0},{2,3},{3,2},{4,5},{5,4},{6,7},{7,6},{8,9},{9,8},{10,11... | collective-permute-start | bytes 1572872 | tf_op jit(solution)/shard_map/ppermute | solution.py:220
  76.6 2.2 %collective-permute-done.3 = bf16[128,1024]{1,0:T(8,128)(2,1)S(1)} collective-permute-done((bf16[128,1024]{1,0:T(8,128)(2,1)S(1)}, bf16[128,1024]{1,0:T(8,128)(2,1)S(1)}, u32[]{:S(2)}, u32[]{:S(2)}) %collective-permute-start.3) | collective-permute-done | bytes 262176 | tf_op jit(solution)/shard_map/ppermute | solution.py:235
  78.8 2.7 %collective-permute-done.2 = bf16[128,1024]{1,0:T(8,128)(2,1)S(1)} collective-permute-done((bf16[128,1024]{1,0:T(8,128)(2,1)S(1)}, bf16[128,1024]{1,0:T(8,128)(2,1)S(1)}, u32[]{:S(2)}, u32[]{:S(2)}) %collective-permute-start.2) | collective-permute-done | bytes 262176 | tf_op jit(solution)/shard_map/ppermute | solution.py:234
  81.6 2.8 %collective-permute-start.6 = (bf16[2,128,1024]{2,1,0:T(8,128)(2,1)S(1)}, bf16[2,128,1024]{2,1,0:T(8,128)(2,1)}, u32[]{:S(2)}, u32[]{:S(2)}) collective-permute-start(bf16[2,128,1024]{2,1,0:T(8,128)(2,1)S(1)} %pad_maximum_fusion.3.far_a), channel_id=1, source_target_pairs={{0,1},{1,0},{2,3},{3,2},{4,5},{5,4},{6,7},{7,6},{8,9},{9,8},{10,11... | collective-permute-start | bytes 1572872 | tf_op jit(solution)/shard_map/ppermute | solution.py:239
  85.5 1.1 slice.35
  86.5 1.2 reshape.51.ev_ref
  87.7 1.6 %slice.32 = bf16[32,4,512]{2,1,0:T(4,128)(2,1)} slice(bf16[32,4,2560]{2,1,0:T(4,128)(2,1)} %copy-done.6), slice={[0:32], [0:4], [2048:2560]} | slice | bytes 262144 | tf_op jit(solution)/shard_map/slice | solution.py:231
  89.3 1.0 reshape.48.pt_ref
  91.3 6.7 %layer.1 = (bf16[128,1024]{1,0:T(8,128)(2,1)}, bf16[128,2048]{1,0:T(8,128)(2,1)S(1)}, bf16[512,128]{1,0:T(8,128)(2,1)S(1)}) custom-call(s32[2]{0:T(128)S(1)} %pad_add_fusion.place_ref, s32[2]{0:T(128)S(1)} %copy-done.4, bf16[512,128]{1,0:T(8,128)(2,1)S(1)} %reshape.48.pt_ref, bf16[128,512]{1,0:T(8,128)(2,1)S(1)} %copy-done.2, ...), custom_call_target="tpu_custom_call" | custom-call | flops 1073741824 | bytes 8388608 | tf_op jit(solution)/shard_map/layer/pallas_call | solution.py:180
  100.4 1.2 reshape.53
  102.0 23.5 %all_to_all.15 = bf16[32,4,2560]{2,1,0:T(4,128)(2,1)S(1)} all-to-all(bf16[32,4,2560]{2,1,0:T(4,128)(2,1)S(1)} %pad_maximum_fusion.2), channel_id=1, replica_groups=mesh['yh'=2,'z'=8,'x'=4,'yl'=4,'core'=2] {'x','yl','core'}, dimensions={0} | all-to-all | bytes 1310720 | tf_op jit(solution)/shard_map/all_to_all | solution.py:256
  (51 shorter events, 8.1 us)
Async XLA Ops:
  0.6 20.3 %copy-start.7 = (s32[1,4,4096]{2,1,0:T(4,128)S(1)}, s32[1,4,4096]{2,1,0:T(4,128)}, u32[]{:S(2)}) copy-start(s32[1,4,4096]{2,1,0:T(4,128)} %param.10) | copy-start | bytes 196612
  0.6 20.3 %copy-start.5 = (bf16[1,16,32768]{2,1,0:T(8,128)(2,1)S(1)}, bf16[1,16,32768]{2,1,0:T(8,128)(2,1)}, u32[]{:S(2)}) copy-start(bf16[1,16,32768]{2,1,0:T(8,128)(2,1)} %param.11) | copy-start | bytes 3145732
  2.5 38.0 %all-to-all-start.1 = ((bf16[128,2,1024]{2,1,0:T(2,128)(2,1)}), bf16[128,2,1024]{2,1,0:T(2,128)(2,1)S(1)}, u32[]{:S(2)}, u32[]{:S(2)}) async-start(bf16[128,2,1024]{2,1,0:T(2,128)(2,1)} %bitcast.7), calls=%async_computation.1 | async-start | bytes 1048576 | tf_op jit(solution)/shard_map/all_to_all | solution.py:210
  21.0 9.2 %copy-start.8 = (bf16[2,2,2048]{2,1,0:T(2,128)(2,1)S(1)}, bf16[2,2,2048]{2,1,0:T(2,128)(2,1)}, u32[]{:S(2)}) copy-start(bf16[2,2,2048]{2,1,0:T(2,128)(2,1)} %param.12) | copy-start | bytes 49156
  40.7 15.1 %collective-permute-start.1 = (bf16[256,1024]{1,0:T(8,128)(2,1)S(1)}, bf16[256,1024]{1,0:T(8,128)(2,1)S(1)}, u32[]{:S(2)}, u32[]{:S(2)}) collective-permute-start(bf16[256,1024]{1,0:T(8,128)(2,1)S(1)} %reshape.50.own_a), channel_id=1, source_target_pairs={{0,24},{8,0},{16,8},{24,16},{1,25},{9,1},{17,9},{25,17},{2,26},{10... | collective-permute-start | bytes 1572872 | tf_op jit(solution)/shard_map/ppermute | solution.py:219
  45.1 15.0 %collective-permute-start = (bf16[256,1024]{1,0:T(8,128)(2,1)S(1)}, bf16[256,1024]{1,0:T(8,128)(2,1)S(1)}, u32[]{:S(2)}, u32[]{:S(2)}) collective-permute-start(bf16[256,1024]{1,0:T(8,128)(2,1)S(1)} %reshape.50.own_a), channel_id=1, source_target_pairs={{0,8},{8,16},{16,24},{24,0},{1,9},{9,17},{17,25},{25,1},{2,10},{10... | collective-permute-start | bytes 1572872 | tf_op jit(solution)/shard_map/ppermute | solution.py:218
  48.6 36.0 %all-to-all-start = ((bf16[32,4,2560]{2,1,0:T(4,128)(2,1)}), bf16[32,4,2560]{2,1,0:T(4,128)(2,1)S(1)}, u32[]{:S(2)}, u32[]{:S(2)}) async-start(bf16[32,4,2560]{2,1,0:T(4,128)(2,1)} %pad_maximum_fusion.1), calls=%async_computation | async-start | bytes 1310720 | tf_op jit(solution)/shard_map/all_to_all | solution.py:229
  60.2 24.2 %copy-start.9 = (s32[128]{0:T(128)S(1)}, s32[128]{0:T(128)}, u32[]{:S(2)}) copy-start(s32[128]{0:T(128)} %param.14) | copy-start | bytes 1540
  60.2 30.1 %collective-permute-start.5 = (bf16[2,256,1024]{2,1,0:T(8,128)(2,1)S(1)}, bf16[2,256,1024]{2,1,0:T(8,128)(2,1)}, u32[]{:S(2)}, u32[]{:S(2)}) collective-permute-start(bf16[2,256,1024]{2,1,0:T(8,128)(2,1)S(1)} %pad_maximum_fusion.sides_a), channel_id=1, source_target_pairs={{0,1},{1,0},{2,3},{3,2},{4,5},{5,4},{6,7},{7,6},{8,9},{9,8},{10,11... | collective-permute-start | bytes 3145736 | tf_op jit(solution)/shard_map/ppermute | solution.py:237
  68.6 10.2 %collective-permute-start.3 = (bf16[128,1024]{1,0:T(8,128)(2,1)S(1)}, bf16[128,1024]{1,0:T(8,128)(2,1)S(1)}, u32[]{:S(2)}, u32[]{:S(2)}) collective-permute-start(bf16[128,1024]{1,0:T(8,128)(2,1)S(1)} %slice.34), channel_id=1, source_target_pairs={{0,24},{8,0},{16,8},{24,16},{1,25},{9,1},{17,9},{25,17},{2,26},{10... | collective-permute-start | bytes 786440 | tf_op jit(solution)/shard_map/ppermute | solution.py:235
  70.6 11.0 %collective-permute-start.2 = (bf16[128,1024]{1,0:T(8,128)(2,1)S(1)}, bf16[128,1024]{1,0:T(8,128)(2,1)S(1)}, u32[]{:S(2)}, u32[]{:S(2)}) collective-permute-start(bf16[128,1024]{1,0:T(8,128)(2,1)S(1)} %slice.33), channel_id=1, source_target_pairs={{0,8},{8,16},{16,24},{24,0},{1,9},{9,17},{17,25},{25,1},{2,10},{10... | collective-permute-start | bytes 786440 | tf_op jit(solution)/shard_map/ppermute | solution.py:234
  74.0 16.4 %collective-permute-start.4 = (bf16[256,1024]{1,0:T(8,128)(2,1)S(1)}, bf16[256,1024]{1,0:T(8,128)(2,1)S(1)}, u32[]{:S(2)}, u32[]{:S(2)}) collective-permute-start(bf16[256,1024]{1,0:T(8,128)(2,1)S(1)} %reshape.50.own_a), channel_id=1, source_target_pairs={{0,1},{1,0},{2,3},{3,2},{4,5},{5,4},{6,7},{7,6},{8,9},{9,8},{10,11... | collective-permute-start | bytes 1572872 | tf_op jit(solution)/shard_map/ppermute | solution.py:220
  81.6 8.7 %collective-permute-start.6 = (bf16[2,128,1024]{2,1,0:T(8,128)(2,1)S(1)}, bf16[2,128,1024]{2,1,0:T(8,128)(2,1)}, u32[]{:S(2)}, u32[]{:S(2)}) collective-permute-start(bf16[2,128,1024]{2,1,0:T(8,128)(2,1)S(1)} %pad_maximum_fusion.3.far_a), channel_id=1, source_target_pairs={{0,1},{1,0},{2,3},{3,2},{4,5},{5,4},{6,7},{7,6},{8,9},{9,8},{10,11... | collective-permute-start | bytes 1572872 | tf_op jit(solution)/shard_map/ppermute | solution.py:239
  84.6 0.9 copy-start.6
  86.5 3.8 %copy-start.2 = (bf16[128,512]{1,0:T(8,128)(2,1)S(1)}, bf16[128,512]{1,0:T(8,128)(2,1)}, u32[]{:S(2)}) copy-start(bf16[128,512]{1,0:T(8,128)(2,1)} %dense_ref.1) | copy-start | bytes 393220
  86.5 3.8 %copy-start.4 = (s32[2]{0:T(128)S(1)}, s32[2]{0:T(128)}, u32[]{:S(2)}) copy-start(s32[2]{0:T(128)} %len_ref.1) | copy-start | bytes 28
  90.4 1.0 copy-start.1
  98.0 0.8 copy-start
  98.8 0.7 copy-start.3

commit v3 on v2

v3 whole, which is shorter than its diff:
```python
import math

import jax
import jax.numpy as jnp
from jax import lax
from jax.experimental import pallas as pl
from jax.experimental.pallas import tpu as pltpu
from jax.sharding import Mesh, PartitionSpec as P


H = 8
norm_eps = 1e-05

REQ = ("yh", "z")
CAND = ("x", "yl", "core")
ALL = REQ + CAND


LOW = 512
TILE = 256


def lookup(ids, table, history, cands):
    bag, count = ids.shape
    emb, rows = table.shape
    hist_rows, hist_width = history.shape
    highs = rows // LOW
    step = min(count, 4 * TILE)
    half = emb // 2

    def kernel(ids_ref, table_ref, history_ref, out_ref, stacked_ref):
        @pl.when(pl.program_id(0) == 0)
        def _():
            for high in range(highs):
                stacked_ref[high * emb : (high + 1) * emb, :] = table_ref[:, high * LOW : (high + 1) * LOW]

        low_iota = lax.broadcasted_iota(jnp.int32, (LOW, TILE), 0)
        for run in range(step // cands):
            out_ref[run, :, :hist_width] = history_ref[...]
        for tile in range(step // TILE):
            span = slice(tile * TILE, (tile + 1) * TILE)
            total = jnp.zeros((emb, TILE), jnp.float32)
            for slot in range(bag):
                row = ids_ref[slot : slot + 1, span]
                low = jnp.bitwise_and(row, LOW - 1)
                high_of = jnp.broadcast_to(jnp.right_shift(row, LOW.bit_length() - 1), (emb, TILE))
                one_hot = (low_iota == low).astype(jnp.float32).astype(jnp.bfloat16)
                picked = jnp.dot(stacked_ref[...], one_hot, preferred_element_type=jnp.float32)
                found = jnp.zeros((emb, TILE), jnp.float32)
                for high in range(highs):
                    found = jnp.where(high_of == high, picked[high * emb : (high + 1) * emb, :], found)
                total = total + found
            for run in range(TILE // cands):
                cols = slice(run * cands, (run + 1) * cands)
                for part in range(2):
                    first = hist_width + part * cands
                    out_ref[tile * (TILE // cands) + run, :, first : first + cands] = total[
                        part * half : (part + 1) * half, cols
                    ].astype(jnp.bfloat16)

    width = hist_width + 2 * cands
    return pl.pallas_call(
        kernel,
        grid=(count // step,),
        in_specs=[
            pl.BlockSpec((bag, step), lambda i: (0, i)),
            pl.BlockSpec((emb, rows), lambda i: (0, 0)),
            pl.BlockSpec((hist_rows, hist_width), lambda i: (0, 0)),
        ],
        out_specs=pl.BlockSpec((step // cands, hist_rows, width), lambda i: (i, 0, 0)),
        out_shape=jax.ShapeDtypeStruct((count // cands, hist_rows, width), jnp.bfloat16),
        scratch_shapes=[pltpu.VMEM((highs * emb, LOW), jnp.bfloat16)],
        compiler_params=pltpu.CompilerParams(vmem_limit_bytes=32 << 20),
        cost_estimate=pl.CostEstimate(
            flops=2 * emb * rows * bag * count, bytes_accessed=2 * emb * rows, transcendentals=0
        ),
        name="lookup",
    )(ids, table, history)


def dot_nn(left, right):
    return jnp.dot(left, right, preferred_element_type=jnp.float32)


def dot_nt(left, right):
    return lax.dot_general(left, right, (((1,), (1,)), ((), ())), preferred_element_type=jnp.float32)


def dot_tn(left, right):
    return lax.dot_general(left, right, (((0,), (0,)), ((), ())), preferred_element_type=jnp.float32)


def layer(front, dense, cot, mine, other, place_index, requests, lengths, own_events):
    cands, dense_width = dense.shape
    own_shape = mine[0].shape
    width = own_shape[1]
    pooled_width = width - dense_width
    block = own_shape[0]
    outer = width // block
    inner = 16
    dim = width // H
    row_count = front.shape[0]
    owned = lengths.shape[0]
    shift = owned * own_events
    group_rows = 2 * shift
    sources = row_count // group_rows
    scale = 1.0 / math.sqrt(dim)

    def kernel(
        place_ref, len_ref, front_ref, dense_ref, cot_hbm,
        own_a, sides_a, far_a, own_b, sides_b, far_b, req_ref,
        out_ref, back_ref, wq_ref, wo_ref, cot_ref, cot_sem,
    ):
        cot_copy = pltpu.make_async_copy(cot_hbm, cot_ref, cot_sem)
        cot_copy.start()
        x = place_ref[1]

        def place(own, sides, far, target):
            def put(source, first, offset):
                for i in range(source.shape[0] // inner):
                    start = pl.multiple_of(((first + i) * outer + lax.rem(x + offset, outer)) * inner, inner)
                    target[pl.ds(start, inner), :] = source[i * inner : (i + 1) * inner, :]

            put(own, 0, 0)
            put(sides.at[0], 0, outer - 1)
            put(sides.at[1], 0, 1)
            half = block // inner // 2
            put(far.at[0], 0, 2)
            put(far.at[1], half, 2)

        @pl.when(place_ref[0] == 0)
        def _():
            place(own_a, sides_a, far_a, wq_ref)
            place(own_b, sides_b, far_b, wo_ref)

        @pl.when(place_ref[0] != 0)
        def _():
            place(own_b, sides_b, far_b, wq_ref)
            place(own_a, sides_a, far_a, wo_ref)

        parts = [front_ref[:, width + p * cands : width + (p + 1) * cands].astype(jnp.float32) for p in range(2)]
        pooled = jnp.concatenate(
            [parts[p][t * group_rows : (t + 1) * group_rows, :] for t in range(sources) for p in range(2)], axis=0
        )
        pooled = jnp.transpose(pooled)
        query_pre = dot_nn(pooled.astype(jnp.bfloat16), wq_ref[:pooled_width, :]) + dot_nn(
            dense_ref[...], wq_ref[pooled_width:, :]
        )
        gate = jax.nn.sigmoid(query_pre)
        query = (query_pre * gate).astype(jnp.bfloat16)
        query_slope = gate * (1.0 + query_pre * (1.0 - gate))

        index = lax.broadcasted_iota(jnp.int32, (cands, row_count), 1)
        within = index % group_rows
        owner = within // own_events
        time = index // group_rows * own_events + within % own_events
        limit = jnp.full((cands, row_count), len_ref[0], jnp.int32)
        for a in range(1, owned):
            limit = jnp.where(owner == a, len_ref[a], limit)
        live = (owner == req_ref[...]) & (time < limit)

        weights, slopes, attended = [], [], []
        for h in range(H):
            cols = slice(h * dim, (h + 1) * dim)
            score = dot_nt(query[:, cols], front_ref[:, cols]) * scale
            sig = jax.nn.sigmoid(score)
            weight = jnp.where(live, score * sig, 0.0)
            weights.append(pltpu.roll(weight, shift, 1).astype(jnp.bfloat16))
            slopes.append(jnp.where(live, sig * (1.0 + score * (1.0 - sig)) * scale, 0.0))
            attended.append(dot_nn(weights[h], front_ref[:, cols]))
        attended = jnp.concatenate(attended, axis=1)
        centered = attended - jnp.mean(attended, axis=1, keepdims=True)
        inverse = lax.rsqrt(jnp.mean(centered * centered, axis=1, keepdims=True) + norm_eps)
        normed = centered * inverse
        mixed = dot_nn(normed.astype(jnp.bfloat16), wo_ref[...])
        out_ref[:, :pooled_width] = (mixed[:, :pooled_width] + pooled).astype(jnp.bfloat16)
        out_ref[:, pooled_width:] = (mixed[:, pooled_width:] + dense_ref[...].astype(jnp.float32)).astype(
            jnp.bfloat16
        )
        cot_copy.wait()
        back_y = dot_nt(cot_ref[...], wo_ref[...])
        back_att = inverse * (
            back_y
            - jnp.mean(back_y, axis=1, keepdims=True)
            - normed * jnp.mean(back_y * normed, axis=1, keepdims=True)
        )
        back_att = back_att.astype(jnp.bfloat16)
        back_query = []
        for h in range(H):
            cols = slice(h * dim, (h + 1) * dim)
            back_w = dot_nt(back_att[:, cols], front_ref[:, cols])
            back_w = pltpu.roll(back_w, row_count - shift, 1)
            back_s = (back_w * slopes[h]).astype(jnp.bfloat16)
            back_query.append(dot_nn(back_s, front_ref[:, cols]))
            back_ref[:, cols] = dot_tn(
                jnp.concatenate([back_s, weights[h]], axis=0),
                jnp.concatenate([query[:, cols], back_att[:, cols]], axis=0),
            ).astype(jnp.bfloat16)
        back_pre = (jnp.concatenate(back_query, axis=1) * query_slope).astype(jnp.bfloat16)
        pool = jnp.transpose(cot_ref[:, :pooled_width].astype(jnp.float32)) + dot_nt(
            wq_ref[:pooled_width, :], back_pre
        )
        for p in range(2):
            part = jnp.concatenate(
                [
                    pool[(2 * t + p) * group_rows : (2 * t + p + 1) * group_rows, :]
                    for t in range(sources)
                ],
                axis=0,
            )
            back_ref[:, width + p * cands : width + (p + 1) * cands] = part.astype(jnp.bfloat16)

    vmem = pl.BlockSpec(memory_space=pltpu.VMEM)
    smem = pl.BlockSpec(memory_space=pltpu.SMEM)
    hbm = pl.BlockSpec(memory_space=pltpu.HBM)
    return pl.pallas_call(
        kernel,
        in_specs=[smem, smem, vmem, vmem, hbm] + [vmem] * 7,
        out_specs=[vmem] * 2,
        out_shape=[
            jax.ShapeDtypeStruct((cands, width), jnp.bfloat16),
            jax.ShapeDtypeStruct(front.shape, jnp.bfloat16),
        ],
        scratch_shapes=[pltpu.VMEM((width, width), jnp.bfloat16)] * 2
        + [pltpu.VMEM((cands, width), jnp.bfloat16), pltpu.SemaphoreType.DMA],
        compiler_params=pltpu.CompilerParams(vmem_limit_bytes=40 << 20),
        cost_estimate=pl.CostEstimate(
            flops=8 * cands * width * width, bytes_accessed=8 * width * width, transcendentals=0
        ),
        name="layer",
    )(place_index, lengths, front, dense, cot, *mine, *other, requests)


def on_device(dense_feat, emb_ids, tables, history_kv, hist_len, cand_request, w_query, w_out, cotangent):
    _, emb_width, _ = tables.shape
    sizes = {a: lax.axis_size(a) for a in ALL}
    cand_devices = sizes["x"] * sizes["yl"] * sizes["core"]
    _, model_width = w_query.shape
    owned, own_events, _ = history_kv.shape
    group = emb_ids.shape[2]
    cands = group // cand_devices
    ring = sizes["x"]
    up = [(i, (i + 1) % ring) for i in range(ring)]
    down = [(i, (i - 1) % ring) for i in range(ring)]
    swap = [(0, 1), (1, 0)]

    first_core = lax.axis_index("core") == 0
    kept = jnp.where(first_core, w_query, w_out)
    got = lax.ppermute(jnp.where(first_core, w_out, w_query), "core", swap)
    own = jnp.concatenate([jnp.where(first_core, kept, got), jnp.where(first_core, got, kept)], axis=0)
    slab = sizes["yh"] * sizes["z"] * sizes["yl"]
    w1 = lax.all_to_all(jnp.broadcast_to(own[None], (slab,) + own.shape), ("yh", "z", "yl"), 0, 0)
    w1 = w1.reshape(-1, model_width)

    history = jnp.transpose(history_kv.reshape(owned, own_events, 2, model_width), (2, 0, 1, 3))
    history = history.reshape(-1, model_width)
    blocks = lookup(emb_ids[0], tables[0], history, cands)

    left = lax.ppermute(w1, "x", up)
    right = lax.ppermute(w1, "x", down)
    other_own = lax.ppermute(w1, "core", swap)

    front = lax.all_to_all(blocks, CAND, 0, 0)
    front = front.reshape(-1, front.shape[2])

    middle = w1.shape[0] // 2
    far_a = lax.ppermute(left[:middle], "x", up)
    far_b = lax.ppermute(right[middle:], "x", down)
    sides = jnp.stack([left, right])
    other_sides = lax.ppermute(sides, "core", swap)
    far = jnp.stack([far_a, far_b])
    other_far = lax.ppermute(far, "core", swap)

    cand_out, back = layer(
        front,
        dense_feat,
        cotangent,
        (w1, sides, far),
        (other_own, other_sides, other_far),
        jnp.stack([lax.axis_index("core"), lax.axis_index("x")]),
        cand_request.reshape(-1, 1),
        hist_len,
        own_events,
    )

    back = lax.all_to_all(back.reshape(cand_devices, -1, back.shape[1]), CAND, 0, 0)
    d_kv = jnp.sum(back[:, :, :model_width].astype(jnp.float32), axis=0)
    d_kv = jnp.transpose(d_kv.reshape(2, owned, own_events, model_width), (1, 2, 0, 3))
    d_kv = d_kv.reshape(owned, own_events, 2 * model_width)
    pool = back[:, :, model_width:].reshape(cand_devices, -1, 2, cands)
    d_pooled = jnp.transpose(pool, (2, 1, 0, 3)).reshape(1, emb_width, group)
    return cand_out, d_kv, d_pooled


def solution(mesh):
    parts = Mesh(mesh.devices.reshape(2, 8, 4, 4, 2), ALL)
    rows = P(ALL, None)
    return jax.shard_map(
        on_device,
        mesh=parts,
        in_specs=(
            rows,
            P(CAND, None, REQ),
            P(CAND, None, None),
            P(REQ, CAND, None),
            P(REQ),
            P(ALL),
            rows,
            rows,
            rows,
        ),
        out_specs=(rows, P(REQ, CAND, None), P(CAND, None, REQ)),
        check_vma=False,
    )
```

time: 128 us -> 134 us (1.047)
  waiting for transfers between devices: 10.3 us -> 28.1 us
  local copies, waits for them, and re-layouts: 13.7 us -> 4.83 us
  starting transfers between devices: 51 us -> 49.1 us
  other arithmetic: 2.74 us -> 1.1 us
    all_to_all x2, waiting for transfers between devices: 1.07 us -> 17.9 us  [the longest x1 17.9 us: on_device(): lax.all_to_all(jnp.broadcast_to(own[None], (slab,) + own.shape), ('yh', '...]
    ppermute x0 -> x1, starting transfers between devices: none -> 7.99 us  [on_device(): got = lax.ppermute(jnp.where(first_core, w_out, w_query), 'core', swap)]
    ppermute x1, starting transfers between devices: 8.41 us -> 2.15 us  [on_device(): other_sides = lax.ppermute(sides, 'core', swap)]
    all_to_all x2, starting transfers between devices: 25.6 us -> 20.9 us  [the longest x1 11.5 us: on_device(): lax.all_to_all(jnp.broadcast_to(own[None], (slab,) + own.shape), ('yh', '...]
    ppermute x1, waiting for transfers between devices: 4.29 us -> 0.01 us  [on_device(): left = lax.ppermute(w1, 'x', up)]
    reshape x10 -> x6, local copies, waits for them, and re-layouts: 5.45 us -> 1.45 us  [the longest x1 0.66 us: on_device(): d_pooled = jnp.transpose(pool, (2, 1, 0, 3)).reshape(1, emb_width, group)]
    ppermute x1, starting transfers between devices: 1.92 us -> 4.67 us  [on_device(): far_b = lax.ppermute(right[middle:], 'x', down)]
    slice x3 -> x0, local copies, waits for them, and re-layouts: 2.74 us -> none  [the longest x1 1.61 us: on_device(): pooled_t = front[:, :, kv_width:].reshape(-1, cands)]
  transfers between devices with their start and end apart: 9 -> 10, of which waited for: 4 -> 5; matrix products, arithmetic and copies ran while one was open for 5% -> 0% of each run, Pallas kernels for 14% -> 14%
where the time goes in v3:
time: 134 us
  starting transfers between devices  49.1 us (37%)
  waiting for transfers between devices  28.1 us (21%)
  Pallas kernels  25.7 us (19%)
  blocking collectives  23.7 us (18%)
  local copies, waits for them, and re-layouts  4.83 us (4%)
    all_to_all x1, blocking collectives, on_device(): lax.all_to_all(back.reshape(cand_devices, -1, back.shape[1]), CAND, 0, 0)  23.7 us
    pallas_call x1, Pallas kernels, lookup(): pl.pallas_call(kernel, grid=(count // step,), in_specs=[pl.BlockSpec((bag...  18.9 us
    all_to_all x1, waiting for transfers between devices, on_device(): lax.all_to_all(jnp.broadcast_to(own[None], (slab,) + own.shape), ('yh', '...  17.9 us
    all_to_all x1, starting transfers between devices, on_device(): lax.all_to_all(jnp.broadcast_to(own[None], (slab,) + own.shape), ('yh', '...  11.5 us
    all_to_all x1, starting transfers between devices, on_device(): front = lax.all_to_all(blocks, CAND, 0, 0)  9.41 us
    ppermute x1, starting transfers between devices, on_device(): got = lax.ppermute(jnp.where(first_core, w_out, w_query), 'core', swap)  7.99 us
    pallas_call x1, Pallas kernels, layer(): pl.pallas_call(kernel, in_specs=[smem, smem, vmem, vmem, hbm] + [vmem] *...  6.76 us
    ppermute x1, starting transfers between devices, on_device(): far_b = lax.ppermute(right[middle:], 'x', down)  4.67 us
  transfers between devices with their start and end apart: 10, of which 5 were waited for; matrix products, arithmetic and copies ran while one was open for 0% of the time, Pallas kernels for 14%

profile of v3, /device:TPU:1, one launch (start us, length us, event | category | flops | bytes accessed | tf_op | source)
XLA Modules:
  0.0 133.5 jit_solution(5006171950978101225)
XLA Ops:
  0.6 0.7 copy-done.6
  1.3 0.8 broadcast_select_fusion.2
  2.1 8.0 %collective-permute-start = (bf16[2,1024]{1,0:T(2,128)(2,1)S(1)}, bf16[2,1024]{1,0:T(2,128)(2,1)S(1)}, u32[]{:S(2)}, u32[]{:S(2)}) collective-permute-start(bf16[2,1024]{1,0:T(2,128)(2,1)S(1)} %broadcast_select_fusion.2), channel_id=1, source_target_pairs={{0,1},{1,0},{2,3},{3,2},{4,5},{5,4},{6,7},{7,6},{8,9},{9,8},{10,11... | collective-permute-start | bytes 12296 | tf_op jit(solution)/shard_map/ppermute | solution.py:249
  10.1 0.8 collective-permute-done
  10.9 0.9 broadcast_in_dim.2
  11.9 11.5 %all-to-all-start.1 = ((bf16[64,4,1024]{2,1,0:T(4,128)(2,1)}), bf16[64,4,1024]{2,1,0:T(4,128)(2,1)S(1)}, u32[]{:S(2)}, u32[]{:S(2)}) async-start(bf16[64,4,1024]{2,1,0:T(4,128)(2,1)} %broadcast_in_dim.2), calls=%async_computation.1 | async-start | bytes 1048576 | tf_op jit(solution)/shard_map/all_to_all | solution.py:252
  23.5 17.9 %all-to-all-done.1 = bf16[64,4,1024]{2,1,0:T(4,128)(2,1)S(1)} async-done(((bf16[64,4,1024]{2,1,0:T(4,128)(2,1)}), bf16[64,4,1024]{2,1,0:T(4,128)(2,1)S(1)}, u32[]{:S(2)}, u32[]{:S(2)}) %all-to-all-start.1) | async-done | bytes 524320 | tf_op jit(solution)/shard_map/all_to_all | solution.py:252
  41.5 4.4 %collective-permute-start.2 = (bf16[256,1024]{1,0:T(8,128)(2,1)S(1)}, bf16[256,1024]{1,0:T(8,128)(2,1)S(1)}, u32[]{:S(2)}, u32[]{:S(2)}) collective-permute-start(bf16[256,1024]{1,0:T(8,128)(2,1)S(1)} %reshape.40.own_a), channel_id=1, source_target_pairs={{0,24},{8,0},{16,8},{24,16},{1,25},{9,1},{17,9},{25,17},{2,26},{10... | collective-permute-start | bytes 1572872 | tf_op jit(solution)/shard_map/ppermute | solution.py:260
  45.9 1.9 %collective-permute-start.1 = (bf16[256,1024]{1,0:T(8,128)(2,1)S(1)}, bf16[256,1024]{1,0:T(8,128)(2,1)S(1)}, u32[]{:S(2)}, u32[]{:S(2)}) collective-permute-start(bf16[256,1024]{1,0:T(8,128)(2,1)S(1)} %reshape.40.own_a), channel_id=1, source_target_pairs={{0,8},{8,16},{16,24},{24,0},{1,9},{9,17},{17,25},{25,1},{2,10},{10... | collective-permute-start | bytes 1572872 | tf_op jit(solution)/shard_map/ppermute | solution.py:259
  47.9 18.9 %lookup.1 = bf16[32,8,1280]{2,1,0:T(8,128)(2,1)} custom-call(s32[4,4096]{1,0:T(4,128)S(1)} %bitcast.31, bf16[16,32768]{1,0:T(8,128)(2,1)S(1)} %bitcast.30, bf16[8,1024]{1,0:T(8,128)(2,1)S(1)} %reshape.38.history_ref), custom_call_target="tpu_custom_call" | custom-call | flops 17179869184 | bytes 1048576 | tf_op jit(solution)/shard_map/lookup/pallas_call | solution.py:62
  66.8 9.4 %all-to-all-start = ((bf16[32,8,1280]{2,1,0:T(8,128)(2,1)}), bf16[32,8,1280]{2,1,0:T(8,128)(2,1)S(1)}, u32[]{:S(2)}, u32[]{:S(2)}) async-start(bf16[32,8,1280]{2,1,0:T(8,128)(2,1)} %lookup.1), calls=%async_computation | async-start | bytes 1310720 | tf_op jit(solution)/shard_map/all_to_all | solution.py:263
  76.4 2.1 %collective-permute-start.6 = (bf16[2,256,1024]{2,1,0:T(8,128)(2,1)S(1)}, bf16[2,256,1024]{2,1,0:T(8,128)(2,1)}, u32[]{:S(2)}, u32[]{:S(2)}) collective-permute-start(bf16[2,256,1024]{2,1,0:T(8,128)(2,1)S(1)} %pad_maximum_fusion.sides_a), channel_id=1, source_target_pairs={{0,1},{1,0},{2,3},{3,2},{4,5},{5,4},{6,7},{7,6},{8,9},{9,8},{10,11... | collective-permute-start | bytes 3145736 | tf_op jit(solution)/shard_map/ppermute | solution.py:270
  78.5 4.7 %collective-permute-start.4 = (bf16[128,1024]{1,0:T(8,128)(2,1)S(1)}, bf16[128,1024]{1,0:T(8,128)(2,1)S(1)}, u32[]{:S(2)}, u32[]{:S(2)}) collective-permute-start(bf16[128,1024]{1,0:T(8,128)(2,1)S(1)} %slice.17), channel_id=1, source_target_pairs={{0,24},{8,0},{16,8},{24,16},{1,25},{9,1},{17,9},{25,17},{2,26},{10... | collective-permute-start | bytes 786440 | tf_op jit(solution)/shard_map/ppermute | solution.py:268
  83.2 1.9 %collective-permute-start.3 = (bf16[128,1024]{1,0:T(8,128)(2,1)S(1)}, bf16[128,1024]{1,0:T(8,128)(2,1)S(1)}, u32[]{:S(2)}, u32[]{:S(2)}) collective-permute-start(bf16[128,1024]{1,0:T(8,128)(2,1)S(1)} %slice.16), channel_id=1, source_target_pairs={{0,8},{8,16},{16,24},{24,0},{1,9},{9,17},{17,25},{25,1},{2,10},{10... | collective-permute-start | bytes 786440 | tf_op jit(solution)/shard_map/ppermute | solution.py:267
  85.2 2.3 %collective-permute-start.5 = (bf16[256,1024]{1,0:T(8,128)(2,1)S(1)}, bf16[256,1024]{1,0:T(8,128)(2,1)S(1)}, u32[]{:S(2)}, u32[]{:S(2)}) collective-permute-start(bf16[256,1024]{1,0:T(8,128)(2,1)S(1)} %reshape.40.own_a), channel_id=1, source_target_pairs={{0,1},{1,0},{2,3},{3,2},{4,5},{5,4},{6,7},{7,6},{8,9},{9,8},{10,11... | collective-permute-start | bytes 1572872 | tf_op jit(solution)/shard_map/ppermute | solution.py:261
  87.5 4.1 %collective-permute-done.4 = bf16[128,1024]{1,0:T(8,128)(2,1)S(1)} collective-permute-done((bf16[128,1024]{1,0:T(8,128)(2,1)S(1)}, bf16[128,1024]{1,0:T(8,128)(2,1)S(1)}, u32[]{:S(2)}, u32[]{:S(2)}) %collective-permute-start.4) | collective-permute-done | bytes 262176 | tf_op jit(solution)/shard_map/ppermute | solution.py:268
  91.6 4.5 %collective-permute-done.3 = bf16[128,1024]{1,0:T(8,128)(2,1)S(1)} collective-permute-done((bf16[128,1024]{1,0:T(8,128)(2,1)S(1)}, bf16[128,1024]{1,0:T(8,128)(2,1)S(1)}, u32[]{:S(2)}, u32[]{:S(2)}) %collective-permute-start.3) | collective-permute-done | bytes 262176 | tf_op jit(solution)/shard_map/ppermute | solution.py:267
  96.1 2.9 %collective-permute-start.7 = (bf16[2,128,1024]{2,1,0:T(8,128)(2,1)S(1)}, bf16[2,128,1024]{2,1,0:T(8,128)(2,1)}, u32[]{:S(2)}, u32[]{:S(2)}) collective-permute-start(bf16[2,128,1024]{2,1,0:T(8,128)(2,1)S(1)} %pad_maximum_fusion.1.far_a), channel_id=1, source_target_pairs={{0,1},{1,0},{2,3},{3,2},{4,5},{5,4},{6,7},{7,6},{8,9},{9,8},{10,11... | collective-permute-start | bytes 1572872 | tf_op jit(solution)/shard_map/ppermute | solution.py:272
  99.0 0.6 copy-done.8
  99.9 0.8 collective-permute-done.7.far_b
  100.7 0.9 copy-done
  101.6 6.8 %layer.1 = (bf16[128,1024]{1,0:T(8,128)(2,1)}, bf16[256,1280]{1,0:T(8,128)(2,1)S(1)}) custom-call(s32[2]{0:T(128)S(1)} %pad_add_fusion.place_ref, s32[2]{0:T(128)S(1)} %copy-done.2, bf16[256,1280]{1,0:T(8,128)(2,1)S(1)} %bitcast.28, bf16[128,512]{1,0:T(8,128)(2,1)S(1)} %copy-done.1, bf16[128,1024]{1,0:T(8,128)(2,1)S(1)} %copy-done, ...), custom_call_target="tpu_custom_call" | custom-call | flops 1073741824 | bytes 8388608 | tf_op jit(solution)/shard_map/layer/pallas_call | solution.py:216
  108.4 23.7 %all_to_all.15 = bf16[32,8,1280]{2,1,0:T(8,128)(2,1)S(1)} all-to-all(bf16[32,8,1280]{2,1,0:T(8,128)(2,1)S(1)} %bitcast.29), channel_id=1, replica_groups=mesh['yh'=2,'z'=8,'x'=4,'yl'=4,'core'=2] {'x','yl','core'}, dimensions={0} | all-to-all | bytes 1310720 | tf_op jit(solution)/shard_map/all_to_all | solution.py:286
  132.9 0.7 copy_bitcast_fusion
  (34 shorter events, 1.3 us)
Async XLA Ops:
  0.6 0.7 copy-start.6
  1.3 9.6 %copy-start.7 = (bf16[2,1024]{1,0:T(2,128)(2,1)S(1)}, bf16[2,1024]{1,0:T(2,128)(2,1)}, u32[]{:S(2)}) copy-start(bf16[2,1024]{1,0:T(2,128)(2,1)} %param.15) | copy-start | bytes 12292
  2.1 8.8 %collective-permute-start = (bf16[2,1024]{1,0:T(2,128)(2,1)S(1)}, bf16[2,1024]{1,0:T(2,128)(2,1)S(1)}, u32[]{:S(2)}, u32[]{:S(2)}) collective-permute-start(bf16[2,1024]{1,0:T(2,128)(2,1)S(1)} %broadcast_select_fusion.2), channel_id=1, source_target_pairs={{0,1},{1,0},{2,3},{3,2},{4,5},{5,4},{6,7},{7,6},{8,9},{9,8},{10,11... | collective-permute-start | bytes 12296 | tf_op jit(solution)/shard_map/ppermute | solution.py:249
  10.9 12.5 %copy-start.5 = (bf16[2,2,2048]{2,1,0:T(2,128)(2,1)S(1)}, bf16[2,2,2048]{2,1,0:T(2,128)(2,1)}, u32[]{:S(2)}) copy-start(bf16[2,2,2048]{2,1,0:T(2,128)(2,1)} %param.12) | copy-start | bytes 49156
  11.9 36.0 %copy-start.3 = (bf16[1,16,32768]{2,1,0:T(8,128)(2,1)S(1)}, bf16[1,16,32768]{2,1,0:T(8,128)(2,1)}, u32[]{:S(2)}) copy-start(bf16[1,16,32768]{2,1,0:T(8,128)(2,1)} %param.11) | copy-start | bytes 3145732
  11.9 29.5 %all-to-all-start.1 = ((bf16[64,4,1024]{2,1,0:T(4,128)(2,1)}), bf16[64,4,1024]{2,1,0:T(4,128)(2,1)S(1)}, u32[]{:S(2)}, u32[]{:S(2)}) async-start(bf16[64,4,1024]{2,1,0:T(4,128)(2,1)} %broadcast_in_dim.2), calls=%async_computation.1 | async-start | bytes 1048576 | tf_op jit(solution)/shard_map/all_to_all | solution.py:252
  23.4 24.4 %copy-start.4 = (s32[1,4,4096]{2,1,0:T(4,128)S(1)}, s32[1,4,4096]{2,1,0:T(4,128)}, u32[]{:S(2)}) copy-start(s32[1,4,4096]{2,1,0:T(4,128)} %param.10) | copy-start | bytes 196612
  41.5 34.7 %collective-permute-start.2 = (bf16[256,1024]{1,0:T(8,128)(2,1)S(1)}, bf16[256,1024]{1,0:T(8,128)(2,1)S(1)}, u32[]{:S(2)}, u32[]{:S(2)}) collective-permute-start(bf16[256,1024]{1,0:T(8,128)(2,1)S(1)} %reshape.40.own_a), channel_id=1, source_target_pairs={{0,24},{8,0},{16,8},{24,16},{1,25},{9,1},{17,9},{25,17},{2,26},{10... | collective-permute-start | bytes 1572872 | tf_op jit(solution)/shard_map/ppermute | solution.py:260
  45.9 30.3 %collective-permute-start.1 = (bf16[256,1024]{1,0:T(8,128)(2,1)S(1)}, bf16[256,1024]{1,0:T(8,128)(2,1)S(1)}, u32[]{:S(2)}, u32[]{:S(2)}) collective-permute-start(bf16[256,1024]{1,0:T(8,128)(2,1)S(1)} %reshape.40.own_a), channel_id=1, source_target_pairs={{0,8},{8,16},{16,24},{24,0},{1,9},{9,17},{17,25},{25,1},{2,10},{10... | collective-permute-start | bytes 1572872 | tf_op jit(solution)/shard_map/ppermute | solution.py:259
  66.8 33.1 %all-to-all-start = ((bf16[32,8,1280]{2,1,0:T(8,128)(2,1)}), bf16[32,8,1280]{2,1,0:T(8,128)(2,1)S(1)}, u32[]{:S(2)}, u32[]{:S(2)}) async-start(bf16[32,8,1280]{2,1,0:T(8,128)(2,1)} %lookup.1), calls=%async_computation | async-start | bytes 1310720 | tf_op jit(solution)/shard_map/all_to_all | solution.py:263
  76.4 24.3 %collective-permute-start.6 = (bf16[2,256,1024]{2,1,0:T(8,128)(2,1)S(1)}, bf16[2,256,1024]{2,1,0:T(8,128)(2,1)}, u32[]{:S(2)}, u32[]{:S(2)}) collective-permute-start(bf16[2,256,1024]{2,1,0:T(8,128)(2,1)S(1)} %pad_maximum_fusion.sides_a), channel_id=1, source_target_pairs={{0,1},{1,0},{2,3},{3,2},{4,5},{5,4},{6,7},{7,6},{8,9},{9,8},{10,11... | collective-permute-start | bytes 3145736 | tf_op jit(solution)/shard_map/ppermute | solution.py:270
  78.5 13.1 %collective-permute-start.4 = (bf16[128,1024]{1,0:T(8,128)(2,1)S(1)}, bf16[128,1024]{1,0:T(8,128)(2,1)S(1)}, u32[]{:S(2)}, u32[]{:S(2)}) collective-permute-start(bf16[128,1024]{1,0:T(8,128)(2,1)S(1)} %slice.17), channel_id=1, source_target_pairs={{0,24},{8,0},{16,8},{24,16},{1,25},{9,1},{17,9},{25,17},{2,26},{10... | collective-permute-start | bytes 786440 | tf_op jit(solution)/shard_map/ppermute | solution.py:268
  83.2 12.8 %collective-permute-start.3 = (bf16[128,1024]{1,0:T(8,128)(2,1)S(1)}, bf16[128,1024]{1,0:T(8,128)(2,1)S(1)}, u32[]{:S(2)}, u32[]{:S(2)}) collective-permute-start(bf16[128,1024]{1,0:T(8,128)(2,1)S(1)} %slice.16), channel_id=1, source_target_pairs={{0,8},{8,16},{16,24},{24,0},{1,9},{9,17},{17,25},{25,1},{2,10},{10... | collective-permute-start | bytes 786440 | tf_op jit(solution)/shard_map/ppermute | solution.py:267
  85.2 14.7 %collective-permute-start.5 = (bf16[256,1024]{1,0:T(8,128)(2,1)S(1)}, bf16[256,1024]{1,0:T(8,128)(2,1)S(1)}, u32[]{:S(2)}, u32[]{:S(2)}) collective-permute-start(bf16[256,1024]{1,0:T(8,128)(2,1)S(1)} %reshape.40.own_a), channel_id=1, source_target_pairs={{0,1},{1,0},{2,3},{3,2},{4,5},{5,4},{6,7},{7,6},{8,9},{9,8},{10,11... | collective-permute-start | bytes 1572872 | tf_op jit(solution)/shard_map/ppermute | solution.py:261
  96.1 4.6 %copy-start.1 = (bf16[128,512]{1,0:T(8,128)(2,1)S(1)}, bf16[128,512]{1,0:T(8,128)(2,1)}, u32[]{:S(2)}) copy-start(bf16[128,512]{1,0:T(8,128)(2,1)} %dense_ref.1) | copy-start | bytes 393220
  96.1 4.5 %collective-permute-start.7 = (bf16[2,128,1024]{2,1,0:T(8,128)(2,1)S(1)}, bf16[2,128,1024]{2,1,0:T(8,128)(2,1)}, u32[]{:S(2)}, u32[]{:S(2)}) collective-permute-start(bf16[2,128,1024]{2,1,0:T(8,128)(2,1)S(1)} %pad_maximum_fusion.1.far_a), channel_id=1, source_target_pairs={{0,1},{1,0},{2,3},{3,2},{4,5},{5,4},{6,7},{7,6},{8,9},{9,8},{10,11... | collective-permute-start | bytes 1572872 | tf_op jit(solution)/shard_map/ppermute | solution.py:272
  99.0 0.7 copy-start.8
  99.9 0.8 copy-start.2
  100.7 1.0 copy-start

commit v4 on v3

--- a/solution.py
+++ b/solution.py
@@ -23,7 +23,8 @@
 def lookup(ids, table, history, cands):
     bag, count = ids.shape
     emb, rows = table.shape
-    hist_rows, hist_width = history.shape
+    hist_rows = history.shape[0]
+    hist_width = history.shape[1] // 2
     highs = rows // LOW
     step = min(count, 4 * TILE)
     half = emb // 2
@@ -36,7 +37,8 @@
 
         low_iota = lax.broadcasted_iota(jnp.int32, (LOW, TILE), 0)
         for run in range(step // cands):
-            out_ref[run, :, :hist_width] = history_ref[...]
+            core = run % 2
+            out_ref[run, :, :hist_width] = history_ref[:, core * hist_width : (core + 1) * hist_width]
         for tile in range(step // TILE):
             span = slice(tile * TILE, (tile + 1) * TILE)
             total = jnp.zeros((emb, TILE), jnp.float32)
@@ -65,7 +67,7 @@
         in_specs=[
             pl.BlockSpec((bag, step), lambda i: (0, i)),
             pl.BlockSpec((emb, rows), lambda i: (0, 0)),
-            pl.BlockSpec((hist_rows, hist_width), lambda i: (0, 0)),
+            pl.BlockSpec(history.shape, lambda i: (0, 0)),
         ],
         out_specs=pl.BlockSpec((step // cands, hist_rows, width), lambda i: (i, 0, 0)),
         out_shape=jax.ShapeDtypeStruct((count // cands, hist_rows, width), jnp.bfloat16),
@@ -90,16 +92,15 @@
     return lax.dot_general(left, right, (((0,), (0,)), ((), ())), preferred_element_type=jnp.float32)
 
 
-def layer(front, dense, cot, mine, other, place_index, requests, lengths, own_events):
+def layer(front, front_other, dense, cot, mine, other, place_index, requests, lengths, own_events):
     cands, dense_width = dense.shape
-    own_shape = mine[0].shape
-    width = own_shape[1]
+    block, width = mine[0].shape
     pooled_width = width - dense_width
-    block = own_shape[0]
     outer = width // block
     inner = 16
     dim = width // H
     row_count = front.shape[0]
+    hist_width = front_other.shape[1]
     owned = lengths.shape[0]
     shift = owned * own_events
     group_rows = 2 * shift
@@ -107,42 +108,45 @@
     scale = 1.0 / math.sqrt(dim)
 
     def kernel(
-        place_ref, len_ref, front_ref, dense_ref, cot_hbm,
-        own_a, sides_a, far_a, own_b, sides_b, far_b, req_ref,
-        out_ref, back_ref, wq_ref, wo_ref, cot_ref, cot_sem,
+        place_ref, len_ref, front_ref, front_other_ref, dense_hbm, cot_hbm, req_ref, *rest
     ):
+        mine_refs, other_refs = rest[:5], rest[5:10]
+        out_ref, back_ref, wq_ref, wo_ref, ev_ref, cot_ref, dense_ref, cot_sem, dense_sem = rest[10:]
         cot_copy = pltpu.make_async_copy(cot_hbm, cot_ref, cot_sem)
+        dense_copy = pltpu.make_async_copy(dense_hbm, dense_ref, dense_sem)
+        dense_copy.start()
         cot_copy.start()
         x = place_ref[1]
 
-        def place(own, sides, far, target):
-            def put(source, first, offset):
-                for i in range(source.shape[0] // inner):
+        def place(pieces, target):
+            half = block // inner // 2
+            for piece, first, offset in zip(pieces, (0, 0, 0, 0, half), (0, outer - 1, 1, 2, 2)):
+                for i in range(piece.shape[0] // inner):
                     start = pl.multiple_of(((first + i) * outer + lax.rem(x + offset, outer)) * inner, inner)
-                    target[pl.ds(start, inner), :] = source[i * inner : (i + 1) * inner, :]
-
-            put(own, 0, 0)
-            put(sides.at[0], 0, outer - 1)
-            put(sides.at[1], 0, 1)
-            half = block // inner // 2
-            put(far.at[0], 0, 2)
-            put(far.at[1], half, 2)
+                    target[pl.ds(start, inner), :] = piece[i * inner : (i + 1) * inner, :]
 
         @pl.when(place_ref[0] == 0)
         def _():
-            place(own_a, sides_a, far_a, wq_ref)
-            place(own_b, sides_b, far_b, wo_ref)
+            place(mine_refs, wq_ref)
+            place(other_refs, wo_ref)
+            ev_ref[:, :hist_width] = front_ref[:, :hist_width]
+            ev_ref[:, hist_width:] = front_other_ref[...]
 
         @pl.when(place_ref[0] != 0)
         def _():
-            place(own_b, sides_b, far_b, wq_ref)
-            place(own_a, sides_a, far_a, wo_ref)
-
-        parts = [front_ref[:, width + p * cands : width + (p + 1) * cands].astype(jnp.float32) for p in range(2)]
+            place(other_refs, wq_ref)
+            place(mine_refs, wo_ref)
+            ev_ref[:, :hist_width] = front_other_ref[...]
+            ev_ref[:, hist_width:] = front_ref[:, :hist_width]
+
+        parts = [
+            front_ref[:, hist_width + p * cands : hist_width + (p + 1) * cands].astype(jnp.float32) for p in range(2)
+        ]
         pooled = jnp.concatenate(
             [parts[p][t * group_rows : (t + 1) * group_rows, :] for t in range(sources) for p in range(2)], axis=0
         )
         pooled = jnp.transpose(pooled)
+        dense_copy.wait()
         query_pre = dot_nn(pooled.astype(jnp.bfloat16), wq_ref[:pooled_width, :]) + dot_nn(
             dense_ref[...], wq_ref[pooled_width:, :]
         )
@@ -157,17 +161,19 @@
         limit = jnp.full((cands, row_count), len_ref[0], jnp.int32)
         for a in range(1, owned):
             limit = jnp.where(owner == a, len_ref[a], limit)
-        live = (owner == req_ref[...]) & (time < limit)
+        request = jnp.transpose(jnp.broadcast_to(req_ref[...].astype(jnp.float32), (cands, cands))).astype(jnp.int32)
+        request = jnp.concatenate([request] * (row_count // cands), axis=1)
+        live = (owner == request) & (time < limit)
 
         weights, slopes, attended = [], [], []
         for h in range(H):
             cols = slice(h * dim, (h + 1) * dim)
-            score = dot_nt(query[:, cols], front_ref[:, cols]) * scale
+            score = dot_nt(query[:, cols], ev_ref[:, cols]) * scale
             sig = jax.nn.sigmoid(score)
             weight = jnp.where(live, score * sig, 0.0)
             weights.append(pltpu.roll(weight, shift, 1).astype(jnp.bfloat16))
             slopes.append(jnp.where(live, sig * (1.0 + score * (1.0 - sig)) * scale, 0.0))
-            attended.append(dot_nn(weights[h], front_ref[:, cols]))
+            attended.append(dot_nn(weights[h], ev_ref[:, cols]))
         attended = jnp.concatenate(attended, axis=1)
         centered = attended - jnp.mean(attended, axis=1, keepdims=True)
         inverse = lax.rsqrt(jnp.mean(centered * centered, axis=1, keepdims=True) + norm_eps)
@@ -188,10 +194,10 @@
         back_query = []
         for h in range(H):
             cols = slice(h * dim, (h + 1) * dim)
-            back_w = dot_nt(back_att[:, cols], front_ref[:, cols])
+            back_w = dot_nt(back_att[:, cols], ev_ref[:, cols])
             back_w = pltpu.roll(back_w, row_count - shift, 1)
             back_s = (back_w * slopes[h]).astype(jnp.bfloat16)
-            back_query.append(dot_nn(back_s, front_ref[:, cols]))
+            back_query.append(dot_nn(back_s, ev_ref[:, cols]))
             back_ref[:, cols] = dot_tn(
                 jnp.concatenate([back_s, weights[h]], axis=0),
                 jnp.concatenate([query[:, cols], back_att[:, cols]], axis=0),
@@ -215,27 +221,43 @@
     hbm = pl.BlockSpec(memory_space=pltpu.HBM)
     return pl.pallas_call(
         kernel,
-        in_specs=[smem, smem, vmem, vmem, hbm] + [vmem] * 7,
+        in_specs=[smem, smem, vmem, vmem, hbm, hbm] + [vmem] * 11,
         out_specs=[vmem] * 2,
         out_shape=[
             jax.ShapeDtypeStruct((cands, width), jnp.bfloat16),
-            jax.ShapeDtypeStruct(front.shape, jnp.bfloat16),
+            jax.ShapeDtypeStruct((row_count, width + 2 * cands), jnp.bfloat16),
         ],
         scratch_shapes=[pltpu.VMEM((width, width), jnp.bfloat16)] * 2
-        + [pltpu.VMEM((cands, width), jnp.bfloat16), pltpu.SemaphoreType.DMA],
+        + [
+            pltpu.VMEM((row_count, width), jnp.bfloat16),
+            pltpu.VMEM((cands, width), jnp.bfloat16),
+            pltpu.VMEM((cands, dense_width), jnp.bfloat16),
+            pltpu.SemaphoreType.DMA,
+            pltpu.SemaphoreType.DMA,
+        ],
         compiler_params=pltpu.CompilerParams(vmem_limit_bytes=40 << 20),
         cost_estimate=pl.CostEstimate(
             flops=8 * cands * width * width, bytes_accessed=8 * width * width, transcendentals=0
         ),
         name="layer",
-    )(place_index, lengths, front, dense, cot, *mine, *other, requests)
+    )(
+        place_index,
+        lengths,
+        front,
+        front_other,
+        pltpu.with_memory_space_constraint(dense, pltpu.HBM),
+        pltpu.with_memory_space_constraint(cot, pltpu.HBM),
+        requests,
+        *mine,
+        *other,
+    )
 
 
 def on_device(dense_feat, emb_ids, tables, history_kv, hist_len, cand_request, w_query, w_out, cotangent):
     _, emb_width, _ = tables.shape
     sizes = {a: lax.axis_size(a) for a in ALL}
     cand_devices = sizes["x"] * sizes["yl"] * sizes["core"]
-    _, model_width = w_query.shape
+    own_rows, model_width = w_query.shape
     owned, own_events, _ = history_kv.shape
     group = emb_ids.shape[2]
     cands = group // cand_devices
@@ -244,12 +266,10 @@
     down = [(i, (i - 1) % ring) for i in range(ring)]
     swap = [(0, 1), (1, 0)]
 
-    first_core = lax.axis_index("core") == 0
-    kept = jnp.where(first_core, w_query, w_out)
-    got = lax.ppermute(jnp.where(first_core, w_out, w_query), "core", swap)
-    own = jnp.concatenate([jnp.where(first_core, kept, got), jnp.where(first_core, got, kept)], axis=0)
+    own = jnp.concatenate([w_query, w_out], axis=0).reshape(1, 2, own_rows, model_width)
     slab = sizes["yh"] * sizes["z"] * sizes["yl"]
-    w1 = lax.all_to_all(jnp.broadcast_to(own[None], (slab,) + own.shape), ("yh", "z", "yl"), 0, 0)
+    own = jnp.broadcast_to(own, (slab, 2, own_rows, model_width)).reshape(2 * slab, own_rows, model_width)
+    w1 = lax.all_to_all(own, ("yh", "z", "yl", "core"), 0, 0)
     w1 = w1.reshape(-1, model_width)
 
     history = jnp.transpose(history_kv.reshape(owned, own_events, 2, model_width), (2, 0, 1, 3))
@@ -258,27 +278,28 @@
 
     left = lax.ppermute(w1, "x", up)
     right = lax.ppermute(w1, "x", down)
-    other_own = lax.ppermute(w1, "core", swap)
-
     front = lax.all_to_all(blocks, CAND, 0, 0)
     front = front.reshape(-1, front.shape[2])
+    hist_width = model_width // 2
+    front_other = lax.ppermute(front[:, :hist_width], "core", swap)
 
     middle = w1.shape[0] // 2
     far_a = lax.ppermute(left[:middle], "x", up)
     far_b = lax.ppermute(right[middle:], "x", down)
-    sides = jnp.stack([left, right])
-    other_sides = lax.ppermute(sides, "core", swap)
-    far = jnp.stack([far_a, far_b])
-    other_far = lax.ppermute(far, "core", swap)
+    mine = (w1, left, right, far_a, far_b)
+    other = []
+    for piece in mine:
+        other.append(lax.ppermute(piece, "core", swap))
 
     cand_out, back = layer(
         front,
+        front_other,
         dense_feat,
         cotangent,
-        (w1, sides, far),
-        (other_own, other_sides, other_far),
+        mine,
+        tuple(other),
         jnp.stack([lax.axis_index("core"), lax.axis_index("x")]),
-        cand_request.reshape(-1, 1),
+        cand_request.reshape(1, -1),
         hist_len,
         own_events,
     )

time: 134 us -> 122 us (0.910)
  waiting for transfers between devices: 28.1 us -> 8.77 us
  starting transfers between devices: 49.1 us -> 54.7 us
    all_to_all x1, waiting for transfers between devices: 17.9 us -> 0.01 us  [on_device(): w1 = lax.all_to_all(own, ('yh', 'z', 'yl', 'core'), 0, 0)]
    all_to_all x1, waiting for transfers between devices: 0.01 us -> 7.35 us  [on_device(): front = lax.all_to_all(blocks, CAND, 0, 0)]
    all_to_all x1, starting transfers between devices: 11.5 us -> 18.5 us  [on_device(): w1 = lax.all_to_all(own, ('yh', 'z', 'yl', 'core'), 0, 0)]
    ppermute x1, waiting for transfers between devices: 4.5 us -> 0.01 us  [on_device(): far_a = lax.ppermute(left[:middle], 'x', up)]
    ppermute x1, waiting for transfers between devices: 4.09 us -> 0.01 us  [on_device(): far_b = lax.ppermute(right[middle:], 'x', down)]
    all_to_all x1, starting transfers between devices: 9.41 us -> 7.72 us  [on_device(): front = lax.all_to_all(blocks, CAND, 0, 0)]
    ppermute x4 -> x6, starting transfers between devices: 15.3 us -> 15.5 us  [the longest x5 13.5 us: on_device(): other.append(lax.ppermute(piece, 'core', swap))]
  transfers between devices with their start and end apart: 10 -> 12, of which waited for: 5 -> 2; matrix products, arithmetic and copies ran while one was open for 0% -> 0% of each run, Pallas kernels for 14% -> 16%
where the time goes in v4:
time: 122 us; the launch traced here: 121 us
  starting transfers between devices  54.7 us (45%)
  Pallas kernels  26.1 us (21%)
  blocking collectives  24.8 us (20%)
  waiting for transfers between devices  8.77 us (7%)
  local copies, waits for them, and re-layouts  5.11 us (4%)
    all_to_all x1, blocking collectives, on_device(): lax.all_to_all(back.reshape(cand_devices, -1, back.shape[1]), CAND, 0, 0)  24.8 us
    pallas_call x1, Pallas kernels, lookup(): pl.pallas_call(kernel, grid=(count // step,), in_specs=[pl.BlockSpec((bag...  18.9 us
    all_to_all x1, starting transfers between devices, on_device(): w1 = lax.all_to_all(own, ('yh', 'z', 'yl', 'core'), 0, 0)  18.5 us
    ppermute x5, starting transfers between devices, on_device(): other.append(lax.ppermute(piece, 'core', swap))  13.5 us
    all_to_all x1, starting transfers between devices, on_device(): front = lax.all_to_all(blocks, CAND, 0, 0)  7.72 us
    all_to_all x1, waiting for transfers between devices, on_device(): front = lax.all_to_all(blocks, CAND, 0, 0)  7.35 us
    pallas_call x1, Pallas kernels, layer(): pl.pallas_call(kernel, in_specs=[smem, smem, vmem, vmem, hbm, hbm] + [vme...  7.2 us
    ppermute x1, starting transfers between devices, on_device(): far_b = lax.ppermute(right[middle:], 'x', down)  4.64 us
  transfers between devices with their start and end apart: 12, of which 2 were waited for; matrix products, arithmetic and copies ran while one was open for 0% of the time, Pallas kernels for 16%

profile of v4, /device:TPU:1, one launch (start us, length us, event | category | flops | bytes accessed | tf_op | source)
XLA Modules:
  0.0 121.3 jit_solution(14208936530787701324)
XLA Ops:
  0.6 0.8 pad_maximum_fusion
  1.5 1.1 broadcast_in_dim.8
  2.5 18.5 %all-to-all-start.1 = ((bf16[128,2,1024]{2,1,0:T(2,128)(2,1)}), bf16[128,2,1024]{2,1,0:T(2,128)(2,1)S(1)}, u32[]{:S(2)}, u32[]{:S(2)}) async-start(bf16[128,2,1024]{2,1,0:T(2,128)(2,1)} %bitcast.7), calls=%async_computation.1 | async-start | bytes 1048576 | tf_op jit(solution)/shard_map/all_to_all | solution.py:272
  21.2 0.8 copy-done.5
  21.9 18.9 %lookup.1 = bf16[32,8,768]{2,1,0:T(8,128)(2,1)} custom-call(s32[4,4096]{1,0:T(4,128)S(1)} %bitcast.30, bf16[16,32768]{1,0:T(8,128)(2,1)S(1)} %bitcast.29, bf16[8,1024]{1,0:T(8,128)(2,1)S(1)} %reshape.42.history_ref), custom_call_target="tpu_custom_call" | custom-call | flops 17179869184 | bytes 1048576 | tf_op jit(solution)/shard_map/lookup/pallas_call | solution.py:64
  40.8 7.7 %all-to-all-start = ((bf16[32,8,768]{2,1,0:T(8,128)(2,1)}), bf16[32,8,768]{2,1,0:T(8,128)(2,1)S(1)}, u32[]{:S(2)}, u32[]{:S(2)}) async-start(bf16[32,8,768]{2,1,0:T(8,128)(2,1)} %lookup.1), calls=%async_computation | async-start | bytes 786432 | tf_op jit(solution)/shard_map/all_to_all | solution.py:281
  48.7 4.5 %collective-permute-start.2 = (bf16[256,1024]{1,0:T(8,128)(2,1)S(1)}, bf16[256,1024]{1,0:T(8,128)(2,1)S(1)}, u32[]{:S(2)}, u32[]{:S(2)}) collective-permute-start(bf16[256,1024]{1,0:T(8,128)(2,1)S(1)} %reshape.46.rest_0_), channel_id=1, source_target_pairs={{0,24},{8,0},{16,8},{24,16},{1,25},{9,1},{17,9},{25,17},{2,26},{10... | collective-permute-start | bytes 1572872 | tf_op jit(solution)/shard_map/ppermute | solution.py:280
  53.3 1.9 %collective-permute-start.1 = (bf16[256,1024]{1,0:T(8,128)(2,1)S(1)}, bf16[256,1024]{1,0:T(8,128)(2,1)S(1)}, u32[]{:S(2)}, u32[]{:S(2)}) collective-permute-start(bf16[256,1024]{1,0:T(8,128)(2,1)S(1)} %reshape.46.rest_0_), channel_id=1, source_target_pairs={{0,8},{8,16},{16,24},{24,0},{1,9},{9,17},{17,25},{25,1},{2,10},{10... | collective-permute-start | bytes 1572872 | tf_op jit(solution)/shard_map/ppermute | solution.py:279
  55.2 7.4 %all-to-all-done = bf16[32,8,768]{2,1,0:T(8,128)(2,1)S(1)} async-done(((bf16[32,8,768]{2,1,0:T(8,128)(2,1)}), bf16[32,8,768]{2,1,0:T(8,128)(2,1)S(1)}, u32[]{:S(2)}, u32[]{:S(2)}) %all-to-all-start) | async-done | bytes 393248 | tf_op jit(solution)/shard_map/all_to_all | solution.py:281
  62.6 1.9 %collective-permute-start = (bf16[256,512]{1,0:T(8,128)(2,1)S(1)}, bf16[256,512]{1,0:T(8,128)(2,1)S(1)}, u32[]{:S(2)}, u32[]{:S(2)}) collective-permute-start(bf16[256,512]{1,0:T(8,128)(2,1)S(1)} %slice.20), channel_id=1, source_target_pairs={{0,1},{1,0},{2,3},{3,2},{4,5},{5,4},{6,7},{7,6},{8,9},{9,8},{10,11... | collective-permute-start | bytes 786440 | tf_op jit(solution)/shard_map/ppermute | solution.py:284
  64.5 2.4 %collective-permute-start.5 = (bf16[256,1024]{1,0:T(8,128)(2,1)S(1)}, bf16[256,1024]{1,0:T(8,128)(2,1)S(1)}, u32[]{:S(2)}, u32[]{:S(2)}) collective-permute-start(bf16[256,1024]{1,0:T(8,128)(2,1)S(1)} %reshape.46.rest_0_), channel_id=1, source_target_pairs={{0,1},{1,0},{2,3},{3,2},{4,5},{5,4},{6,7},{7,6},{8,9},{9,8},{10,11... | collective-permute-start | bytes 1572872 | tf_op jit(solution)/shard_map/ppermute | solution.py:292
  67.0 4.6 %collective-permute-start.4 = (bf16[128,1024]{1,0:T(8,128)(2,1)S(1)}, bf16[128,1024]{1,0:T(8,128)(2,1)}, u32[]{:S(2)}, u32[]{:S(2)}) collective-permute-start(bf16[128,1024]{1,0:T(8,128)(2,1)S(1)} %slice.22), channel_id=1, source_target_pairs={{0,24},{8,0},{16,8},{24,16},{1,25},{9,1},{17,9},{25,17},{2,26},{10... | collective-permute-start | bytes 786440 | tf_op jit(solution)/shard_map/ppermute | solution.py:288
  71.6 1.9 %collective-permute-start.3 = (bf16[128,1024]{1,0:T(8,128)(2,1)S(1)}, bf16[128,1024]{1,0:T(8,128)(2,1)}, u32[]{:S(2)}, u32[]{:S(2)}) collective-permute-start(bf16[128,1024]{1,0:T(8,128)(2,1)S(1)} %slice.21), channel_id=1, source_target_pairs={{0,8},{8,16},{16,24},{24,0},{1,9},{9,17},{17,25},{25,1},{2,10},{10... | collective-permute-start | bytes 786440 | tf_op jit(solution)/shard_map/ppermute | solution.py:287
  73.6 3.0 %collective-permute-start.7 = (bf16[256,1024]{1,0:T(8,128)(2,1)S(1)}, bf16[256,1024]{1,0:T(8,128)(2,1)S(1)}, u32[]{:S(2)}, u32[]{:S(2)}) collective-permute-start(bf16[256,1024]{1,0:T(8,128)(2,1)S(1)} %collective-permute-done.2.rest_2_), channel_id=1, source_target_pairs={{0,1},{1,0},{2,3},{3,2},{4,5},{5,4},{6,7},{7,6},{8,9},{9,8},{10,11... | collective-permute-start | bytes 1572872 | tf_op jit(solution)/shard_map/ppermute | solution.py:292
  76.6 0.7 copy-done
  77.3 1.9 %collective-permute-start.6 = (bf16[256,1024]{1,0:T(8,128)(2,1)S(1)}, bf16[256,1024]{1,0:T(8,128)(2,1)S(1)}, u32[]{:S(2)}, u32[]{:S(2)}) collective-permute-start(bf16[256,1024]{1,0:T(8,128)(2,1)S(1)} %collective-permute-done.1.rest_1_), channel_id=1, source_target_pairs={{0,1},{1,0},{2,3},{3,2},{4,5},{5,4},{6,7},{7,6},{8,9},{9,8},{10,11... | collective-permute-start | bytes 1572872 | tf_op jit(solution)/shard_map/ppermute | solution.py:292
  79.3 2.4 %collective-permute-start.9 = (bf16[128,1024]{1,0:T(8,128)(2,1)}, bf16[128,1024]{1,0:T(8,128)(2,1)}, u32[]{:S(2)}, u32[]{:S(2)}) collective-permute-start(bf16[128,1024]{1,0:T(8,128)(2,1)} %collective-permute-done.4.rest_4_), channel_id=1, source_target_pairs={{0,1},{1,0},{2,3},{3,2},{4,5},{5,4},{6,7},{7,6},{8,9},{9,8},{10,11... | collective-permute-start | bytes 786440 | tf_op jit(solution)/shard_map/ppermute | solution.py:292
  81.7 3.8 %collective-permute-start.8 = (bf16[128,1024]{1,0:T(8,128)(2,1)}, bf16[128,1024]{1,0:T(8,128)(2,1)}, u32[]{:S(2)}, u32[]{:S(2)}) collective-permute-start(bf16[128,1024]{1,0:T(8,128)(2,1)} %collective-permute-done.3.rest_3_), channel_id=1, source_target_pairs={{0,1},{1,0},{2,3},{3,2},{4,5},{5,4},{6,7},{7,6},{8,9},{9,8},{10,11... | collective-permute-start | bytes 786440 | tf_op jit(solution)/shard_map/ppermute | solution.py:292
  85.6 1.4 %collective-permute-done.8.rest_8_ = bf16[128,1024]{1,0:T(8,128)(2,1)} collective-permute-done((bf16[128,1024]{1,0:T(8,128)(2,1)}, bf16[128,1024]{1,0:T(8,128)(2,1)}, u32[]{:S(2)}, u32[]{:S(2)}) %collective-permute-start.8) | collective-permute-done | bytes 262176 | tf_op jit(solution)/shard_map/ppermute | solution.py:292
  87.0 0.9 copy-done.1
  87.9 7.2 %layer.1 = (bf16[128,1024]{1,0:T(8,128)(2,1)}, bf16[256,1280]{1,0:T(8,128)(2,1)S(1)}) custom-call(s32[2]{0:T(128)S(1)} %pad_add_fusion.place_ref, s32[2]{0:T(128)S(1)} %copy-done.2, bf16[256,768]{1,0:T(8,128)(2,1)S(1)} %bitcast.26, bf16[256,512]{1,0:T(8,128)(2,1)S(1)} %copy-done.1, bf16[128,512]{1,0:T(8,128)(2,1)} %dense_hbm.1, bf16[128,1024]{1,0:T(8,128)(2,1)} %cot_hbm.1, ...), custom_call_target="tpu_custom_call" | custom-call | flops 1073741824 | bytes 8388608 | tf_op jit(solution)/shard_map/layer/pallas_call | solution.py:222
  95.1 24.8 %all_to_all.15 = bf16[32,8,1280]{2,1,0:T(8,128)(2,1)S(1)} all-to-all(bf16[32,8,1280]{2,1,0:T(8,128)(2,1)S(1)} %bitcast.27), channel_id=1, replica_groups=mesh['yh'=2,'z'=8,'x'=4,'yl'=4,'core'=2] {'x','yl','core'}, dimensions={0} | all-to-all | bytes 1310720 | tf_op jit(solution)/shard_map/all_to_all | solution.py:307
  120.0 0.6 copy.20
  120.6 0.7 copy_bitcast_fusion
  (31 shorter events, 0.5 us)
Async XLA Ops:
  0.6 20.5 %copy-start.4 = (bf16[1,16,32768]{2,1,0:T(8,128)(2,1)S(1)}, bf16[1,16,32768]{2,1,0:T(8,128)(2,1)}, u32[]{:S(2)}) copy-start(bf16[1,16,32768]{2,1,0:T(8,128)(2,1)} %param.11) | copy-start | bytes 3145732
  2.5 18.6 %copy-start.6 = (bf16[2,2,2048]{2,1,0:T(2,128)(2,1)S(1)}, bf16[2,2,2048]{2,1,0:T(2,128)(2,1)}, u32[]{:S(2)}) copy-start(bf16[2,2,2048]{2,1,0:T(2,128)(2,1)} %param.12) | copy-start | bytes 49156
  2.5 38.3 %all-to-all-start.1 = ((bf16[128,2,1024]{2,1,0:T(2,128)(2,1)}), bf16[128,2,1024]{2,1,0:T(2,128)(2,1)S(1)}, u32[]{:S(2)}, u32[]{:S(2)}) async-start(bf16[128,2,1024]{2,1,0:T(2,128)(2,1)} %bitcast.7), calls=%async_computation.1 | async-start | bytes 1048576 | tf_op jit(solution)/shard_map/all_to_all | solution.py:272
  21.1 0.8 copy-start.5
  40.8 21.7 %all-to-all-start = ((bf16[32,8,768]{2,1,0:T(8,128)(2,1)}), bf16[32,8,768]{2,1,0:T(8,128)(2,1)S(1)}, u32[]{:S(2)}, u32[]{:S(2)}) async-start(bf16[32,8,768]{2,1,0:T(8,128)(2,1)} %lookup.1), calls=%async_computation | async-start | bytes 786432 | tf_op jit(solution)/shard_map/all_to_all | solution.py:281
  48.7 18.2 %collective-permute-start.2 = (bf16[256,1024]{1,0:T(8,128)(2,1)S(1)}, bf16[256,1024]{1,0:T(8,128)(2,1)S(1)}, u32[]{:S(2)}, u32[]{:S(2)}) collective-permute-start(bf16[256,1024]{1,0:T(8,128)(2,1)S(1)} %reshape.46.rest_0_), channel_id=1, source_target_pairs={{0,24},{8,0},{16,8},{24,16},{1,25},{9,1},{17,9},{25,17},{2,26},{10... | collective-permute-start | bytes 1572872 | tf_op jit(solution)/shard_map/ppermute | solution.py:280
  53.3 18.3 %collective-permute-start.1 = (bf16[256,1024]{1,0:T(8,128)(2,1)S(1)}, bf16[256,1024]{1,0:T(8,128)(2,1)S(1)}, u32[]{:S(2)}, u32[]{:S(2)}) collective-permute-start(bf16[256,1024]{1,0:T(8,128)(2,1)S(1)} %reshape.46.rest_0_), channel_id=1, source_target_pairs={{0,8},{8,16},{16,24},{24,0},{1,9},{9,17},{17,25},{25,1},{2,10},{10... | collective-permute-start | bytes 1572872 | tf_op jit(solution)/shard_map/ppermute | solution.py:279
  62.6 14.0 %collective-permute-start = (bf16[256,512]{1,0:T(8,128)(2,1)S(1)}, bf16[256,512]{1,0:T(8,128)(2,1)S(1)}, u32[]{:S(2)}, u32[]{:S(2)}) collective-permute-start(bf16[256,512]{1,0:T(8,128)(2,1)S(1)} %slice.20), channel_id=1, source_target_pairs={{0,1},{1,0},{2,3},{3,2},{4,5},{5,4},{6,7},{7,6},{8,9},{9,8},{10,11... | collective-permute-start | bytes 786440 | tf_op jit(solution)/shard_map/ppermute | solution.py:284
  64.5 21.1 %collective-permute-start.5 = (bf16[256,1024]{1,0:T(8,128)(2,1)S(1)}, bf16[256,1024]{1,0:T(8,128)(2,1)S(1)}, u32[]{:S(2)}, u32[]{:S(2)}) collective-permute-start(bf16[256,1024]{1,0:T(8,128)(2,1)S(1)} %reshape.46.rest_0_), channel_id=1, source_target_pairs={{0,1},{1,0},{2,3},{3,2},{4,5},{5,4},{6,7},{7,6},{8,9},{9,8},{10,11... | collective-permute-start | bytes 1572872 | tf_op jit(solution)/shard_map/ppermute | solution.py:292
  67.0 12.3 %collective-permute-start.4 = (bf16[128,1024]{1,0:T(8,128)(2,1)S(1)}, bf16[128,1024]{1,0:T(8,128)(2,1)}, u32[]{:S(2)}, u32[]{:S(2)}) collective-permute-start(bf16[128,1024]{1,0:T(8,128)(2,1)S(1)} %slice.22), channel_id=1, source_target_pairs={{0,24},{8,0},{16,8},{24,16},{1,25},{9,1},{17,9},{25,17},{2,26},{10... | collective-permute-start | bytes 786440 | tf_op jit(solution)/shard_map/ppermute | solution.py:288
  71.6 10.0 %collective-permute-start.3 = (bf16[128,1024]{1,0:T(8,128)(2,1)S(1)}, bf16[128,1024]{1,0:T(8,128)(2,1)}, u32[]{:S(2)}, u32[]{:S(2)}) collective-permute-start(bf16[128,1024]{1,0:T(8,128)(2,1)S(1)} %slice.21), channel_id=1, source_target_pairs={{0,8},{8,16},{16,24},{24,0},{1,9},{9,17},{17,25},{25,1},{2,10},{10... | collective-permute-start | bytes 786440 | tf_op jit(solution)/shard_map/ppermute | solution.py:287
  73.6 13.4 %collective-permute-start.7 = (bf16[256,1024]{1,0:T(8,128)(2,1)S(1)}, bf16[256,1024]{1,0:T(8,128)(2,1)S(1)}, u32[]{:S(2)}, u32[]{:S(2)}) collective-permute-start(bf16[256,1024]{1,0:T(8,128)(2,1)S(1)} %collective-permute-done.2.rest_2_), channel_id=1, source_target_pairs={{0,1},{1,0},{2,3},{3,2},{4,5},{5,4},{6,7},{7,6},{8,9},{9,8},{10,11... | collective-permute-start | bytes 1572872 | tf_op jit(solution)/shard_map/ppermute | solution.py:292
  76.6 0.7 copy-start
  77.3 9.6 %collective-permute-start.6 = (bf16[256,1024]{1,0:T(8,128)(2,1)S(1)}, bf16[256,1024]{1,0:T(8,128)(2,1)S(1)}, u32[]{:S(2)}, u32[]{:S(2)}) collective-permute-start(bf16[256,1024]{1,0:T(8,128)(2,1)S(1)} %collective-permute-done.1.rest_1_), channel_id=1, source_target_pairs={{0,1},{1,0},{2,3},{3,2},{4,5},{5,4},{6,7},{7,6},{8,9},{9,8},{10,11... | collective-permute-start | bytes 1572872 | tf_op jit(solution)/shard_map/ppermute | solution.py:292
  79.3 6.3 %collective-permute-start.9 = (bf16[128,1024]{1,0:T(8,128)(2,1)}, bf16[128,1024]{1,0:T(8,128)(2,1)}, u32[]{:S(2)}, u32[]{:S(2)}) collective-permute-start(bf16[128,1024]{1,0:T(8,128)(2,1)} %collective-permute-done.4.rest_4_), channel_id=1, source_target_pairs={{0,1},{1,0},{2,3},{3,2},{4,5},{5,4},{6,7},{7,6},{8,9},{9,8},{10,11... | collective-permute-start | bytes 786440 | tf_op jit(solution)/shard_map/ppermute | solution.py:292
  81.7 5.3 %collective-permute-start.8 = (bf16[128,1024]{1,0:T(8,128)(2,1)}, bf16[128,1024]{1,0:T(8,128)(2,1)}, u32[]{:S(2)}, u32[]{:S(2)}) collective-permute-start(bf16[128,1024]{1,0:T(8,128)(2,1)} %collective-permute-done.3.rest_3_), channel_id=1, source_target_pairs={{0,1},{1,0},{2,3},{3,2},{4,5},{5,4},{6,7},{7,6},{8,9},{9,8},{10,11... | collective-permute-start | bytes 786440 | tf_op jit(solution)/shard_map/ppermute | solution.py:292
  85.6 1.4 %copy-start.2 = (s32[2]{0:T(128)S(1)}, s32[2]{0:T(128)}, u32[]{:S(2)}) copy-start(s32[2]{0:T(128)} %len_ref.1) | copy-start | bytes 28
  85.6 1.4 %copy-start.3 = (s32[128]{0:T(128)S(1)}, s32[128]{0:T(128)}, u32[]{:S(2)}) copy-start(s32[128]{0:T(128)} %param.14) | copy-start | bytes 1540
  87.0 1.0 copy-start.1

commit v5 on v4

--- a/solution.py
+++ b/solution.py
@@ -110,8 +110,8 @@
     def kernel(
         place_ref, len_ref, front_ref, front_other_ref, dense_hbm, cot_hbm, req_ref, *rest
     ):
-        mine_refs, other_refs = rest[:5], rest[5:10]
-        out_ref, back_ref, wq_ref, wo_ref, ev_ref, cot_ref, dense_ref, cot_sem, dense_sem = rest[10:]
+        mine_refs, other_refs = rest[:4], rest[4:8]
+        out_ref, back_ref, wq_ref, wo_ref, ev_ref, cot_ref, dense_ref, cot_sem, dense_sem = rest[8:]
         cot_copy = pltpu.make_async_copy(cot_hbm, cot_ref, cot_sem)
         dense_copy = pltpu.make_async_copy(dense_hbm, dense_ref, dense_sem)
         dense_copy.start()
@@ -119,10 +119,9 @@
         x = place_ref[1]
 
         def place(pieces, target):
-            half = block // inner // 2
-            for piece, first, offset in zip(pieces, (0, 0, 0, 0, half), (0, outer - 1, 1, 2, 2)):
-                for i in range(piece.shape[0] // inner):
-                    start = pl.multiple_of(((first + i) * outer + lax.rem(x + offset, outer)) * inner, inner)
+            for piece, offset in zip(pieces, (0, outer - 1, 1, 2)):
+                for i in range(block // inner):
+                    start = pl.multiple_of((i * outer + lax.rem(x + offset, outer)) * inner, inner)
                     target[pl.ds(start, inner), :] = piece[i * inner : (i + 1) * inner, :]
 
         @pl.when(place_ref[0] == 0)
@@ -221,7 +220,7 @@
     hbm = pl.BlockSpec(memory_space=pltpu.HBM)
     return pl.pallas_call(
         kernel,
-        in_specs=[smem, smem, vmem, vmem, hbm, hbm] + [vmem] * 11,
+        in_specs=[smem, smem, vmem, vmem, hbm, hbm] + [vmem] * 9,
         out_specs=[vmem] * 2,
         out_shape=[
             jax.ShapeDtypeStruct((cands, width), jnp.bfloat16),
@@ -283,10 +282,12 @@
     hist_width = model_width // 2
     front_other = lax.ppermute(front[:, :hist_width], "core", swap)
 
-    middle = w1.shape[0] // 2
-    far_a = lax.ppermute(left[:middle], "x", up)
-    far_b = lax.ppermute(right[middle:], "x", down)
-    mine = (w1, left, right, far_a, far_b)
+    both_ways = [(2 * i, 2 * ((i + 1) % ring)) for i in range(ring)] + [
+        (2 * i + 1, 2 * ((i - 1) % ring) + 1) for i in range(ring)
+    ]
+    passed = jnp.where(lax.axis_index("core") == 0, left, right)
+    far = lax.ppermute(passed, ("x", "core"), both_ways)
+    mine = (w1, left, right, far)
     other = []
     for piece in mine:
         other.append(lax.ppermute(piece, "core", swap))

time: 122 us -> 140 us (1.15)
  blocking collectives: 24.8 us -> 60.8 us
  starting transfers between devices: 54.7 us -> 27.7 us
  waiting for transfers between devices: 8.77 us -> 20 us
  local copies, waits for them, and re-layouts: 5.11 us -> 2.56 us
    all_to_all x0 -> x1, blocking collectives: none -> 37.8 us  [on_device(): w1 = lax.all_to_all(own, ('yh', 'z', 'yl', 'core'), 0, 0)]
    all_to_all x1 -> x0, starting transfers between devices: 18.5 us -> none  [on_device(): w1 = lax.all_to_all(own, ('yh', 'z', 'yl', 'core'), 0, 0)]
    ppermute x1, waiting for transfers between devices: 0.01 us -> 7.91 us  [on_device(): right = lax.ppermute(w1, 'x', down)]
    ppermute x1, waiting for transfers between devices: 0.01 us -> 5.05 us  [on_device(): left = lax.ppermute(w1, 'x', up)]
    ppermute x5 -> x4, starting transfers between devices: 13.5 us -> 8.66 us  [on_device(): other.append(lax.ppermute(piece, 'core', swap))]
    ppermute x2 -> x1, starting transfers between devices: 6.56 us -> 1.91 us  [on_device(): far = lax.ppermute(passed, ('x', 'core'), both_ways)]
    unnamed x14 -> x10, local copies, waits for them, and re-layouts: 2.43 us -> 0.02 us
    all_to_all x1, waiting for transfers between devices: 7.35 us -> 5.32 us  [on_device(): front = lax.all_to_all(blocks, CAND, 0, 0)]
  transfers between devices with their start and end apart: 12 -> 9, of which waited for: 2 -> 4; matrix products, arithmetic and copies ran while one was open for 0% -> 1% of each run, Pallas kernels for 16% -> 14%
where the time goes in v5:
time: 140 us
  blocking collectives  60.8 us (43%)
  starting transfers between devices  27.7 us (20%)
  Pallas kernels  26.2 us (19%)
  waiting for transfers between devices  20 us (14%)
  local copies, waits for them, and re-layouts  2.56 us (2%)
  other arithmetic  1.72 us (1%)
    all_to_all x1, blocking collectives, on_device(): w1 = lax.all_to_all(own, ('yh', 'z', 'yl', 'core'), 0, 0)  37.8 us
    all_to_all x1, blocking collectives, on_device(): lax.all_to_all(back.reshape(cand_devices, -1, back.shape[1]), CAND, 0, 0)  23 us
    pallas_call x1, Pallas kernels, lookup(): pl.pallas_call(kernel, grid=(count // step,), in_specs=[pl.BlockSpec((bag...  18.9 us
    all_to_all x1, starting transfers between devices, on_device(): front = lax.all_to_all(blocks, CAND, 0, 0)  8.82 us
    ppermute x4, starting transfers between devices, on_device(): other.append(lax.ppermute(piece, 'core', swap))  8.66 us
    ppermute x1, waiting for transfers between devices, on_device(): right = lax.ppermute(w1, 'x', down)  7.91 us
    pallas_call x1, Pallas kernels, layer(): pl.pallas_call(kernel, in_specs=[smem, smem, vmem, vmem, hbm, hbm] + [vme...  7.3 us
    all_to_all x1, waiting for transfers between devices, on_device(): front = lax.all_to_all(blocks, CAND, 0, 0)  5.32 us
  transfers between devices with their start and end apart: 9, of which 4 were waited for; matrix products, arithmetic and copies ran while one was open for 1% of the time, Pallas kernels for 14%

profile of v5, /device:TPU:1, one launch (start us, length us, event | category | flops | bytes accessed | tf_op | source)
XLA Modules:
  0.0 139.9 jit_solution(12784826594855808067)
XLA Ops:
  0.6 0.7 pad_maximum_fusion
  1.4 0.3 broadcast_in_dim.8
  1.6 37.8 %all_to_all.15 = bf16[128,2,1024]{2,1,0:T(2,128)(2,1)S(1)} all-to-all(bf16[128,2,1024]{2,1,0:T(2,128)(2,1)S(1)} %bitcast.31), channel_id=1, replica_groups=mesh['yh'=2,'z'=8,'x'=4,'yl'=4,'core'=2] {'yh','z','yl','core'}, dimensions={0} | all-to-all | bytes 1048576 | tf_op jit(solution)/shard_map/all_to_all | solution.py:271
  39.4 0.2 reshape.46.rest_0_
  39.6 4.5 %collective-permute-start.2 = (bf16[256,1024]{1,0:T(8,128)(2,1)S(1)}, bf16[256,1024]{1,0:T(8,128)(2,1)S(1)}, u32[]{:S(2)}, u32[]{:S(2)}) collective-permute-start(bf16[256,1024]{1,0:T(8,128)(2,1)S(1)} %reshape.46.rest_0_), channel_id=1, source_target_pairs={{0,24},{8,0},{16,8},{24,16},{1,25},{9,1},{17,9},{25,17},{2,26},{10... | collective-permute-start | bytes 1572872 | tf_op jit(solution)/shard_map/ppermute | solution.py:279
  44.2 1.9 %collective-permute-start.1 = (bf16[256,1024]{1,0:T(8,128)(2,1)S(1)}, bf16[256,1024]{1,0:T(8,128)(2,1)S(1)}, u32[]{:S(2)}, u32[]{:S(2)}) collective-permute-start(bf16[256,1024]{1,0:T(8,128)(2,1)S(1)} %reshape.46.rest_0_), channel_id=1, source_target_pairs={{0,8},{8,16},{16,24},{24,0},{1,9},{9,17},{17,25},{25,1},{2,10},{10... | collective-permute-start | bytes 1572872 | tf_op jit(solution)/shard_map/ppermute | solution.py:278
  46.2 7.9 %collective-permute-done.2.rest_2_ = bf16[256,1024]{1,0:T(8,128)(2,1)S(1)} collective-permute-done((bf16[256,1024]{1,0:T(8,128)(2,1)S(1)}, bf16[256,1024]{1,0:T(8,128)(2,1)S(1)}, u32[]{:S(2)}, u32[]{:S(2)}) %collective-permute-start.2) | collective-permute-done | bytes 524320 | tf_op jit(solution)/shard_map/ppermute | solution.py:279
  54.1 5.0 %collective-permute-done.1.rest_1_ = bf16[256,1024]{1,0:T(8,128)(2,1)S(1)} collective-permute-done((bf16[256,1024]{1,0:T(8,128)(2,1)S(1)}, bf16[256,1024]{1,0:T(8,128)(2,1)S(1)}, u32[]{:S(2)}, u32[]{:S(2)}) %collective-permute-start.1) | collective-permute-done | bytes 524320 | tf_op jit(solution)/shard_map/ppermute | solution.py:278
  59.1 0.8 broadcast_select_fusion
  60.0 1.9 %collective-permute-start.3 = (bf16[256,1024]{1,0:T(8,128)(2,1)}, bf16[256,1024]{1,0:T(8,128)(2,1)S(1)}, u32[]{:S(2)}, u32[]{:S(2)}) collective-permute-start(bf16[256,1024]{1,0:T(8,128)(2,1)} %broadcast_select_fusion), channel_id=1, source_target_pairs={{0,8},{8,16},{16,24},{24,0},{1,25},{9,1},{17,9},{25,17},{2,10},{10... | collective-permute-start | bytes 1572872 | tf_op jit(solution)/shard_map/ppermute | solution.py:289
  61.9 18.9 %lookup.1 = bf16[32,8,768]{2,1,0:T(8,128)(2,1)} custom-call(s32[4,4096]{1,0:T(4,128)S(1)} %bitcast.30, bf16[16,32768]{1,0:T(8,128)(2,1)S(1)} %bitcast.29, bf16[8,1024]{1,0:T(8,128)(2,1)S(1)} %reshape.42.history_ref), custom_call_target="tpu_custom_call" | custom-call | flops 17179869184 | bytes 1048576 | tf_op jit(solution)/shard_map/lookup/pallas_call | solution.py:64
  80.8 8.8 %all-to-all-start = ((bf16[32,8,768]{2,1,0:T(8,128)(2,1)}), bf16[32,8,768]{2,1,0:T(8,128)(2,1)S(1)}, u32[]{:S(2)}, u32[]{:S(2)}) async-start(bf16[32,8,768]{2,1,0:T(8,128)(2,1)} %lookup.1), calls=%async_computation | async-start | bytes 786432 | tf_op jit(solution)/shard_map/all_to_all | solution.py:280
  89.6 2.1 %collective-permute-start.4 = (bf16[256,1024]{1,0:T(8,128)(2,1)S(1)}, bf16[256,1024]{1,0:T(8,128)(2,1)S(1)}, u32[]{:S(2)}, u32[]{:S(2)}) collective-permute-start(bf16[256,1024]{1,0:T(8,128)(2,1)S(1)} %reshape.46.rest_0_), channel_id=1, source_target_pairs={{0,1},{1,0},{2,3},{3,2},{4,5},{5,4},{6,7},{7,6},{8,9},{9,8},{10,11... | collective-permute-start | bytes 1572872 | tf_op jit(solution)/shard_map/ppermute | solution.py:293
  91.8 2.2 %collective-permute-start.6 = (bf16[256,1024]{1,0:T(8,128)(2,1)S(1)}, bf16[256,1024]{1,0:T(8,128)(2,1)S(1)}, u32[]{:S(2)}, u32[]{:S(2)}) collective-permute-start(bf16[256,1024]{1,0:T(8,128)(2,1)S(1)} %collective-permute-done.2.rest_2_), channel_id=1, source_target_pairs={{0,1},{1,0},{2,3},{3,2},{4,5},{5,4},{6,7},{7,6},{8,9},{9,8},{10,11... | collective-permute-start | bytes 1572872 | tf_op jit(solution)/shard_map/ppermute | solution.py:293
  94.0 2.1 %collective-permute-start.5 = (bf16[256,1024]{1,0:T(8,128)(2,1)S(1)}, bf16[256,1024]{1,0:T(8,128)(2,1)}, u32[]{:S(2)}, u32[]{:S(2)}) collective-permute-start(bf16[256,1024]{1,0:T(8,128)(2,1)S(1)} %collective-permute-done.1.rest_1_), channel_id=1, source_target_pairs={{0,1},{1,0},{2,3},{3,2},{4,5},{5,4},{6,7},{7,6},{8,9},{9,8},{10,11... | collective-permute-start | bytes 1572872 | tf_op jit(solution)/shard_map/ppermute | solution.py:293
  96.1 2.2 %collective-permute-start.7 = (bf16[256,1024]{1,0:T(8,128)(2,1)S(1)}, bf16[256,1024]{1,0:T(8,128)(2,1)}, u32[]{:S(2)}, u32[]{:S(2)}) collective-permute-start(bf16[256,1024]{1,0:T(8,128)(2,1)S(1)} %collective-permute-done.3.rest_3_), channel_id=1, source_target_pairs={{0,1},{1,0},{2,3},{3,2},{4,5},{5,4},{6,7},{7,6},{8,9},{9,8},{10,11... | collective-permute-start | bytes 1572872 | tf_op jit(solution)/shard_map/ppermute | solution.py:293
  98.3 5.3 %all-to-all-done = bf16[32,8,768]{2,1,0:T(8,128)(2,1)S(1)} async-done(((bf16[32,8,768]{2,1,0:T(8,128)(2,1)}), bf16[32,8,768]{2,1,0:T(8,128)(2,1)S(1)}, u32[]{:S(2)}, u32[]{:S(2)}) %all-to-all-start) | async-done | bytes 393248 | tf_op jit(solution)/shard_map/all_to_all | solution.py:280
  103.6 0.7 slice.12
  104.4 1.9 %collective-permute-start = (bf16[256,512]{1,0:T(8,128)(2,1)}, bf16[256,512]{1,0:T(8,128)(2,1)}, u32[]{:S(2)}, u32[]{:S(2)}) collective-permute-start(bf16[256,512]{1,0:T(8,128)(2,1)} %slice.12), channel_id=1, source_target_pairs={{0,1},{1,0},{2,3},{3,2},{4,5},{5,4},{6,7},{7,6},{8,9},{9,8},{10,11... | collective-permute-start | bytes 786440 | tf_op jit(solution)/shard_map/ppermute | solution.py:283
  106.4 1.8 %collective-permute-done.front_other_ref = bf16[256,512]{1,0:T(8,128)(2,1)} collective-permute-done((bf16[256,512]{1,0:T(8,128)(2,1)}, bf16[256,512]{1,0:T(8,128)(2,1)}, u32[]{:S(2)}, u32[]{:S(2)}) %collective-permute-start) | collective-permute-done | bytes 262176 | tf_op jit(solution)/shard_map/ppermute | solution.py:283
  108.2 7.3 %layer.1 = (bf16[128,1024]{1,0:T(8,128)(2,1)}, bf16[256,1280]{1,0:T(8,128)(2,1)S(1)}) custom-call(s32[2]{0:T(128)S(1)} %pad_add_fusion.place_ref, s32[2]{0:T(128)S(1)} %copy-done, bf16[256,768]{1,0:T(8,128)(2,1)S(1)} %bitcast.26, bf16[256,512]{1,0:T(8,128)(2,1)} %collective-permute-done.front_other_ref, bf16[128,512]{1,0:T(8,128)(2,1)} %dense_hbm.1, ...), custom_call_target="tpu_custom_call" | custom-call | flops 1073741824 | bytes 8388608 | tf_op jit(solution)/shard_map/layer/pallas_call | solution.py:221
  115.5 23.0 %all_to_all.16 = bf16[32,8,1280]{2,1,0:T(8,128)(2,1)S(1)} all-to-all(bf16[32,8,1280]{2,1,0:T(8,128)(2,1)S(1)} %bitcast.27), channel_id=1, replica_groups=mesh['yh'=2,'z'=8,'x'=4,'yl'=4,'core'=2] {'x','yl','core'}, dimensions={0} | all-to-all | bytes 1310720 | tf_op jit(solution)/shard_map/all_to_all | solution.py:308
  138.6 0.6 copy.20
  139.2 0.7 copy_bitcast_fusion
  (21 shorter events, 0.3 us)
Async XLA Ops:
  39.4 6.7 %copy-start.4 = (bf16[2,2,2048]{2,1,0:T(2,128)(2,1)S(1)}, bf16[2,2,2048]{2,1,0:T(2,128)(2,1)}, u32[]{:S(2)}) copy-start(bf16[2,2,2048]{2,1,0:T(2,128)(2,1)} %param.12) | copy-start | bytes 49156
  39.6 22.3 %copy-start.2 = (bf16[1,16,32768]{2,1,0:T(8,128)(2,1)S(1)}, bf16[1,16,32768]{2,1,0:T(8,128)(2,1)}, u32[]{:S(2)}) copy-start(bf16[1,16,32768]{2,1,0:T(8,128)(2,1)} %param.11) | copy-start | bytes 3145732
  39.6 14.4 %collective-permute-start.2 = (bf16[256,1024]{1,0:T(8,128)(2,1)S(1)}, bf16[256,1024]{1,0:T(8,128)(2,1)S(1)}, u32[]{:S(2)}, u32[]{:S(2)}) collective-permute-start(bf16[256,1024]{1,0:T(8,128)(2,1)S(1)} %reshape.46.rest_0_), channel_id=1, source_target_pairs={{0,24},{8,0},{16,8},{24,16},{1,25},{9,1},{17,9},{25,17},{2,26},{10... | collective-permute-start | bytes 1572872 | tf_op jit(solution)/shard_map/ppermute | solution.py:279
  44.2 15.0 %collective-permute-start.1 = (bf16[256,1024]{1,0:T(8,128)(2,1)S(1)}, bf16[256,1024]{1,0:T(8,128)(2,1)S(1)}, u32[]{:S(2)}, u32[]{:S(2)}) collective-permute-start(bf16[256,1024]{1,0:T(8,128)(2,1)S(1)} %reshape.46.rest_0_), channel_id=1, source_target_pairs={{0,8},{8,16},{16,24},{24,0},{1,9},{9,17},{17,25},{25,1},{2,10},{10... | collective-permute-start | bytes 1572872 | tf_op jit(solution)/shard_map/ppermute | solution.py:278
  46.1 15.7 %copy-start.3 = (s32[1,4,4096]{2,1,0:T(4,128)S(1)}, s32[1,4,4096]{2,1,0:T(4,128)}, u32[]{:S(2)}) copy-start(s32[1,4,4096]{2,1,0:T(4,128)} %param.10) | copy-start | bytes 196612
  60.0 36.2 %collective-permute-start.3 = (bf16[256,1024]{1,0:T(8,128)(2,1)}, bf16[256,1024]{1,0:T(8,128)(2,1)S(1)}, u32[]{:S(2)}, u32[]{:S(2)}) collective-permute-start(bf16[256,1024]{1,0:T(8,128)(2,1)} %broadcast_select_fusion), channel_id=1, source_target_pairs={{0,8},{8,16},{16,24},{24,0},{1,25},{9,1},{17,9},{25,17},{2,10},{10... | collective-permute-start | bytes 1572872 | tf_op jit(solution)/shard_map/ppermute | solution.py:289
  80.8 22.8 %all-to-all-start = ((bf16[32,8,768]{2,1,0:T(8,128)(2,1)}), bf16[32,8,768]{2,1,0:T(8,128)(2,1)S(1)}, u32[]{:S(2)}, u32[]{:S(2)}) async-start(bf16[32,8,768]{2,1,0:T(8,128)(2,1)} %lookup.1), calls=%async_computation | async-start | bytes 786432 | tf_op jit(solution)/shard_map/all_to_all | solution.py:280
  89.6 18.5 %collective-permute-start.4 = (bf16[256,1024]{1,0:T(8,128)(2,1)S(1)}, bf16[256,1024]{1,0:T(8,128)(2,1)S(1)}, u32[]{:S(2)}, u32[]{:S(2)}) collective-permute-start(bf16[256,1024]{1,0:T(8,128)(2,1)S(1)} %reshape.46.rest_0_), channel_id=1, source_target_pairs={{0,1},{1,0},{2,3},{3,2},{4,5},{5,4},{6,7},{7,6},{8,9},{9,8},{10,11... | collective-permute-start | bytes 1572872 | tf_op jit(solution)/shard_map/ppermute | solution.py:293
  91.8 16.4 %collective-permute-start.6 = (bf16[256,1024]{1,0:T(8,128)(2,1)S(1)}, bf16[256,1024]{1,0:T(8,128)(2,1)S(1)}, u32[]{:S(2)}, u32[]{:S(2)}) collective-permute-start(bf16[256,1024]{1,0:T(8,128)(2,1)S(1)} %collective-permute-done.2.rest_2_), channel_id=1, source_target_pairs={{0,1},{1,0},{2,3},{3,2},{4,5},{5,4},{6,7},{7,6},{8,9},{9,8},{10,11... | collective-permute-start | bytes 1572872 | tf_op jit(solution)/shard_map/ppermute | solution.py:293
  94.0 14.2 %collective-permute-start.5 = (bf16[256,1024]{1,0:T(8,128)(2,1)S(1)}, bf16[256,1024]{1,0:T(8,128)(2,1)}, u32[]{:S(2)}, u32[]{:S(2)}) collective-permute-start(bf16[256,1024]{1,0:T(8,128)(2,1)S(1)} %collective-permute-done.1.rest_1_), channel_id=1, source_target_pairs={{0,1},{1,0},{2,3},{3,2},{4,5},{5,4},{6,7},{7,6},{8,9},{9,8},{10,11... | collective-permute-start | bytes 1572872 | tf_op jit(solution)/shard_map/ppermute | solution.py:293
  96.1 12.0 %collective-permute-start.7 = (bf16[256,1024]{1,0:T(8,128)(2,1)S(1)}, bf16[256,1024]{1,0:T(8,128)(2,1)}, u32[]{:S(2)}, u32[]{:S(2)}) collective-permute-start(bf16[256,1024]{1,0:T(8,128)(2,1)S(1)} %collective-permute-done.3.rest_3_), channel_id=1, source_target_pairs={{0,1},{1,0},{2,3},{3,2},{4,5},{5,4},{6,7},{7,6},{8,9},{9,8},{10,11... | collective-permute-start | bytes 1572872 | tf_op jit(solution)/shard_map/ppermute | solution.py:293
  104.4 3.8 %collective-permute-start = (bf16[256,512]{1,0:T(8,128)(2,1)}, bf16[256,512]{1,0:T(8,128)(2,1)}, u32[]{:S(2)}, u32[]{:S(2)}) collective-permute-start(bf16[256,512]{1,0:T(8,128)(2,1)} %slice.12), channel_id=1, source_target_pairs={{0,1},{1,0},{2,3},{3,2},{4,5},{5,4},{6,7},{7,6},{8,9},{9,8},{10,11... | collective-permute-start | bytes 786440 | tf_op jit(solution)/shard_map/ppermute | solution.py:283
  106.4 1.8 %copy-start = (s32[2]{0:T(128)S(1)}, s32[2]{0:T(128)}, u32[]{:S(2)}) copy-start(s32[2]{0:T(128)} %len_ref.1) | copy-start | bytes 28
  106.4 1.8 %copy-start.1 = (s32[128]{0:T(128)S(1)}, s32[128]{0:T(128)}, u32[]{:S(2)}) copy-start(s32[128]{0:T(128)} %param.14) | copy-start | bytes 1540

commit v6 on v5

--- a/solution.py
+++ b/solution.py
@@ -20,8 +20,8 @@
 TILE = 256
 
 
-def lookup(ids, table, history, cands):
-    bag, count = ids.shape
+def lookup(ids, table, history, cands, first, count, into=None):
+    bag, total_count = ids.shape
     emb, rows = table.shape
     hist_rows = history.shape[0]
     hist_width = history.shape[1] // 2
@@ -29,18 +29,24 @@
     step = min(count, 4 * TILE)
     half = emb // 2
 
-    def kernel(ids_ref, table_ref, history_ref, out_ref, stacked_ref):
+    def kernel(ids_hbm, table_ref, history_ref, *rest):
+        out_ref, stacked_ref, ids_ref, ids_sem = rest[-4:]
+
         @pl.when(pl.program_id(0) == 0)
         def _():
+            ids_copy = pltpu.make_async_copy(ids_hbm.at[:, pl.ds(first, count)], ids_ref, ids_sem)
+            ids_copy.start()
             for high in range(highs):
                 stacked_ref[high * emb : (high + 1) * emb, :] = table_ref[:, high * LOW : (high + 1) * LOW]
-
+            ids_copy.wait()
+
+        offset = pl.program_id(0) * step
         low_iota = lax.broadcasted_iota(jnp.int32, (LOW, TILE), 0)
         for run in range(step // cands):
             core = run % 2
             out_ref[run, :, :hist_width] = history_ref[:, core * hist_width : (core + 1) * hist_width]
         for tile in range(step // TILE):
-            span = slice(tile * TILE, (tile + 1) * TILE)
+            span = pl.ds(pl.multiple_of(offset + tile * TILE, TILE), TILE)
             total = jnp.zeros((emb, TILE), jnp.float32)
             for slot in range(bag):
                 row = ids_ref[slot : slot + 1, span]
@@ -55,29 +61,37 @@
             for run in range(TILE // cands):
                 cols = slice(run * cands, (run + 1) * cands)
                 for part in range(2):
-                    first = hist_width + part * cands
-                    out_ref[tile * (TILE // cands) + run, :, first : first + cands] = total[
+                    column = hist_width + part * cands
+                    out_ref[tile * (TILE // cands) + run, :, column : column + cands] = total[
                         part * half : (part + 1) * half, cols
                     ].astype(jnp.bfloat16)
 
     width = hist_width + 2 * cands
+    hbm = pl.BlockSpec(memory_space=pltpu.HBM)
+    arguments = (pltpu.with_memory_space_constraint(ids, pltpu.HBM), table, history)
     return pl.pallas_call(
         kernel,
         grid=(count // step,),
         in_specs=[
-            pl.BlockSpec((bag, step), lambda i: (0, i)),
+            hbm,
             pl.BlockSpec((emb, rows), lambda i: (0, 0)),
             pl.BlockSpec(history.shape, lambda i: (0, 0)),
+        ]
+        + ([] if into is None else [hbm]),
+        out_specs=pl.BlockSpec((step // cands, hist_rows, width), lambda i: (first // step + i, 0, 0)),
+        out_shape=jax.ShapeDtypeStruct((total_count // cands, hist_rows, width), jnp.bfloat16),
+        input_output_aliases={} if into is None else {3: 0},
+        scratch_shapes=[
+            pltpu.VMEM((highs * emb, LOW), jnp.bfloat16),
+            pltpu.VMEM((bag, count), jnp.int32),
+            pltpu.SemaphoreType.DMA,
         ],
-        out_specs=pl.BlockSpec((step // cands, hist_rows, width), lambda i: (i, 0, 0)),
-        out_shape=jax.ShapeDtypeStruct((count // cands, hist_rows, width), jnp.bfloat16),
-        scratch_shapes=[pltpu.VMEM((highs * emb, LOW), jnp.bfloat16)],
         compiler_params=pltpu.CompilerParams(vmem_limit_bytes=32 << 20),
         cost_estimate=pl.CostEstimate(
             flops=2 * emb * rows * bag * count, bytes_accessed=2 * emb * rows, transcendentals=0
         ),
         name="lookup",
-    )(ids, table, history)
+    )(*arguments, *(() if into is None else (into,)))
 
 
 def dot_nn(left, right):
@@ -265,18 +279,21 @@
     down = [(i, (i - 1) % ring) for i in range(ring)]
     swap = [(0, 1), (1, 0)]
 
-    own = jnp.concatenate([w_query, w_out], axis=0).reshape(1, 2, own_rows, model_width)
     slab = sizes["yh"] * sizes["z"] * sizes["yl"]
-    own = jnp.broadcast_to(own, (slab, 2, own_rows, model_width)).reshape(2 * slab, own_rows, model_width)
+    to_core = lax.broadcasted_iota(jnp.int32, (2 * slab, own_rows, model_width), 0) % 2
+    own = jnp.where(to_core == 0, w_query[None], w_out[None])
     w1 = lax.all_to_all(own, ("yh", "z", "yl", "core"), 0, 0)
     w1 = w1.reshape(-1, model_width)
 
     history = jnp.transpose(history_kv.reshape(owned, own_events, 2, model_width), (2, 0, 1, 3))
     history = history.reshape(-1, model_width)
-    blocks = lookup(emb_ids[0], tables[0], history, cands)
+    early = group // 4 * 3
+    blocks = lookup(emb_ids[0], tables[0], history, cands, 0, early)
 
     left = lax.ppermute(w1, "x", up)
     right = lax.ppermute(w1, "x", down)
+    blocks = lookup(emb_ids[0], tables[0], history, cands, early, group - early, blocks)
+
     front = lax.all_to_all(blocks, CAND, 0, 0)
     front = front.reshape(-1, front.shape[2])
     hist_width = model_width // 2

time: 140 us -> 132 us (0.943)
  blocking collectives: 60.8 us -> 23 us
  starting transfers between devices: 27.7 us -> 45.8 us
  waiting for transfers between devices: 20 us -> 26.6 us
  Pallas kernels: 26.2 us -> 28.3 us
  other arithmetic: 1.72 us -> 3.38 us
    all_to_all x1 -> x0, blocking collectives: 37.8 us -> none  [on_device(): w1 = lax.all_to_all(own, ('yh', 'z', 'yl', 'core'), 0, 0)]
    all_to_all x0 -> x1, waiting for transfers between devices: none -> 19.5 us  [on_device(): w1 = lax.all_to_all(own, ('yh', 'z', 'yl', 'core'), 0, 0)]
    all_to_all x0 -> x1, starting transfers between devices: none -> 18.5 us  [on_device(): w1 = lax.all_to_all(own, ('yh', 'z', 'yl', 'core'), 0, 0)]
    ppermute x1, waiting for transfers between devices: 7.91 us -> 0.01 us  [on_device(): right = lax.ppermute(w1, 'x', down)]
    ppermute x1, waiting for transfers between devices: 5.05 us -> 0.01 us  [on_device(): left = lax.ppermute(w1, 'x', up)]
    all_to_all x1, starting transfers between devices: 8.82 us -> 5.83 us  [on_device(): front = lax.all_to_all(blocks, CAND, 0, 0)]
    ppermute x1, starting transfers between devices: 1.91 us -> 4.56 us  [on_device(): far = lax.ppermute(passed, ('x', 'core'), both_ways)]
    select_n x0 -> x1, other arithmetic: none -> 2.36 us  [on_device(): own = jnp.where(to_core == 0, w_query[None], w_out[None])]
  transfers between devices with their start and end apart: 9 -> 10, of which waited for: 4 -> 3; matrix products, arithmetic and copies ran while one was open for 1% -> 1% of each run, Pallas kernels for 14% -> 16%
where the time goes in v6:
time: 132 us; the launch traced here: 131 us
  starting transfers between devices  45.8 us (35%)
  Pallas kernels  28.3 us (21%)
  waiting for transfers between devices  26.6 us (20%)
  blocking collectives  23 us (17%)
  other arithmetic  3.38 us (3%)
  local copies, waits for them, and re-layouts  2.93 us (2%)
    all_to_all x1, blocking collectives, on_device(): lax.all_to_all(back.reshape(cand_devices, -1, back.shape[1]), CAND, 0, 0)  23 us
    pallas_call x2, Pallas kernels, lookup(): pl.pallas_call(kernel, grid=(count // step,), in_specs=[hbm, pl.BlockSpec...  21 us
    all_to_all x1, waiting for transfers between devices, on_device(): w1 = lax.all_to_all(own, ('yh', 'z', 'yl', 'core'), 0, 0)  19.5 us
    all_to_all x1, starting transfers between devices, on_device(): w1 = lax.all_to_all(own, ('yh', 'z', 'yl', 'core'), 0, 0)  18.5 us
    ppermute x4, starting transfers between devices, on_device(): other.append(lax.ppermute(piece, 'core', swap))  8.66 us
    pallas_call x1, Pallas kernels, layer(): pl.pallas_call(kernel, in_specs=[smem, smem, vmem, vmem, hbm, hbm] + [vme...  7.3 us
    all_to_all x1, starting transfers between devices, on_device(): front = lax.all_to_all(blocks, CAND, 0, 0)  5.83 us
    all_to_all x1, waiting for transfers between devices, on_device(): front = lax.all_to_all(blocks, CAND, 0, 0)  5.32 us
  transfers between devices with their start and end apart: 10, of which 3 were waited for; matrix products, arithmetic and copies ran while one was open for 1% of the time, Pallas kernels for 16%

profile of v6, /device:TPU:1, one launch (start us, length us, event | category | flops | bytes accessed | tf_op | source)
XLA Modules:
  0.0 130.9 jit_solution(5894761446142470710)
XLA Ops:
  0.7 0.7 copy-done.4
  1.3 2.4 %compare_select_fusion = bf16[128,2,1024]{2,1,0:T(2,128)(2,1)} fusion(pred[128]{0:T(512)(128)(4,1)S(1)} %compare_and_fusion, s32[128]{0:T(128)S(1)} %get-tuple-element.7, s32[128]{0:T(128)S(1)} %get-tuple-element.8, bf16[2,1024]{1,0:T(2,128)(2,1)S(1)} %copy-done.4, bf16[2,1024]{1,0:T(2,128)(2,1)} %param.15), kind=kLoop, calls=%fused_computation | loop fusion | flops 786432 | bytes 533632 | tf_op jit(solution)/shard_map/jit(_where)/select_n | solution.py:284
  3.7 18.5 %all-to-all-start.1 = ((bf16[128,2,1024]{2,1,0:T(2,128)(2,1)}), bf16[128,2,1024]{2,1,0:T(2,128)(2,1)S(1)}, u32[]{:S(2)}, u32[]{:S(2)}) async-start(bf16[128,2,1024]{2,1,0:T(2,128)(2,1)} %compare_select_fusion), calls=%async_computation.1 | async-start | bytes 1048576 | tf_op jit(solution)/shard_map/all_to_all | solution.py:285
  22.3 19.5 %all-to-all-done.1 = bf16[128,2,1024]{2,1,0:T(2,128)(2,1)S(1)} async-done(((bf16[128,2,1024]{2,1,0:T(2,128)(2,1)}), bf16[128,2,1024]{2,1,0:T(2,128)(2,1)S(1)}, u32[]{:S(2)}, u32[]{:S(2)}) %all-to-all-start.1) | async-done | bytes 524320 | tf_op jit(solution)/shard_map/all_to_all | solution.py:285
  41.8 0.2 reshape.42.rest_0_
  42.0 4.4 %collective-permute-start.2 = (bf16[256,1024]{1,0:T(8,128)(2,1)S(1)}, bf16[256,1024]{1,0:T(8,128)(2,1)S(1)}, u32[]{:S(2)}, u32[]{:S(2)}) collective-permute-start(bf16[256,1024]{1,0:T(8,128)(2,1)S(1)} %reshape.42.rest_0_), channel_id=1, source_target_pairs={{0,24},{8,0},{16,8},{24,16},{1,25},{9,1},{17,9},{25,17},{2,26},{10... | collective-permute-start | bytes 1572872 | tf_op jit(solution)/shard_map/ppermute | solution.py:294
  46.4 1.9 %collective-permute-start.1 = (bf16[256,1024]{1,0:T(8,128)(2,1)S(1)}, bf16[256,1024]{1,0:T(8,128)(2,1)S(1)}, u32[]{:S(2)}, u32[]{:S(2)}) collective-permute-start(bf16[256,1024]{1,0:T(8,128)(2,1)S(1)} %reshape.42.rest_0_), channel_id=1, source_target_pairs={{0,8},{8,16},{16,24},{24,0},{1,9},{9,17},{17,25},{25,1},{2,10},{10... | collective-permute-start | bytes 1572872 | tf_op jit(solution)/shard_map/ppermute | solution.py:293
  48.3 15.1 %lookup.2.rest_0_ = bf16[32,8,768]{2,1,0:T(8,128)(2,1)} custom-call(s32[4,4096]{1,0:T(4,128)} %bitcast.34, bf16[16,32768]{1,0:T(8,128)(2,1)S(1)} %bitcast.28, bf16[8,1024]{1,0:T(8,128)(2,1)S(1)} %reshape.39.history_ref), custom_call_target="tpu_custom_call" | custom-call | flops 12884901888 | bytes 1048576 | tf_op jit(solution)/shard_map/lookup/pallas_call | solution.py:72
  63.5 0.9 broadcast_select_fusion
  64.3 4.6 %collective-permute-start.3 = (bf16[256,1024]{1,0:T(8,128)(2,1)}, bf16[256,1024]{1,0:T(8,128)(2,1)S(1)}, u32[]{:S(2)}, u32[]{:S(2)}) collective-permute-start(bf16[256,1024]{1,0:T(8,128)(2,1)} %broadcast_select_fusion), channel_id=1, source_target_pairs={{0,8},{8,16},{16,24},{24,0},{1,25},{9,1},{17,9},{25,17},{2,10},{10... | collective-permute-start | bytes 1572872 | tf_op jit(solution)/shard_map/ppermute | solution.py:306
  68.9 5.9 %lookup.3 = bf16[32,8,768]{2,1,0:T(8,128)(2,1)} custom-call(s32[4,4096]{1,0:T(4,128)} %bitcast.35, bf16[16,32768]{1,0:T(8,128)(2,1)S(1)} %bitcast.29, bf16[8,1024]{1,0:T(8,128)(2,1)S(1)} %reshape.39.history_ref, bf16[32,8,768]{2,1,0:T(8,128)(2,1)} %lookup.2.rest_0_), custom_call_target="tpu_custom_call", output_to_operand_aliasing={{}: (3, {})} | custom-call | flops 4294967296 | bytes 1048576 | tf_op jit(solution)/shard_map/lookup/pallas_call | solution.py:72
  74.8 5.8 %all-to-all-start = ((bf16[32,8,768]{2,1,0:T(8,128)(2,1)}), bf16[32,8,768]{2,1,0:T(8,128)(2,1)S(1)}, u32[]{:S(2)}, u32[]{:S(2)}) async-start(bf16[32,8,768]{2,1,0:T(8,128)(2,1)} %lookup.3), calls=%async_computation | async-start | bytes 786432 | tf_op jit(solution)/shard_map/all_to_all | solution.py:297
  80.6 2.1 %collective-permute-start.4 = (bf16[256,1024]{1,0:T(8,128)(2,1)S(1)}, bf16[256,1024]{1,0:T(8,128)(2,1)S(1)}, u32[]{:S(2)}, u32[]{:S(2)}) collective-permute-start(bf16[256,1024]{1,0:T(8,128)(2,1)S(1)} %reshape.42.rest_0_), channel_id=1, source_target_pairs={{0,1},{1,0},{2,3},{3,2},{4,5},{5,4},{6,7},{7,6},{8,9},{9,8},{10,11... | collective-permute-start | bytes 1572872 | tf_op jit(solution)/shard_map/ppermute | solution.py:310
  82.8 2.2 %collective-permute-start.6 = (bf16[256,1024]{1,0:T(8,128)(2,1)S(1)}, bf16[256,1024]{1,0:T(8,128)(2,1)S(1)}, u32[]{:S(2)}, u32[]{:S(2)}) collective-permute-start(bf16[256,1024]{1,0:T(8,128)(2,1)S(1)} %collective-permute-done.2.rest_2_), channel_id=1, source_target_pairs={{0,1},{1,0},{2,3},{3,2},{4,5},{5,4},{6,7},{7,6},{8,9},{9,8},{10,11... | collective-permute-start | bytes 1572872 | tf_op jit(solution)/shard_map/ppermute | solution.py:310
  85.0 2.1 %collective-permute-start.5 = (bf16[256,1024]{1,0:T(8,128)(2,1)S(1)}, bf16[256,1024]{1,0:T(8,128)(2,1)}, u32[]{:S(2)}, u32[]{:S(2)}) collective-permute-start(bf16[256,1024]{1,0:T(8,128)(2,1)S(1)} %collective-permute-done.1.rest_1_), channel_id=1, source_target_pairs={{0,1},{1,0},{2,3},{3,2},{4,5},{5,4},{6,7},{7,6},{8,9},{9,8},{10,11... | collective-permute-start | bytes 1572872 | tf_op jit(solution)/shard_map/ppermute | solution.py:310
  87.1 2.2 %collective-permute-start.7 = (bf16[256,1024]{1,0:T(8,128)(2,1)S(1)}, bf16[256,1024]{1,0:T(8,128)(2,1)}, u32[]{:S(2)}, u32[]{:S(2)}) collective-permute-start(bf16[256,1024]{1,0:T(8,128)(2,1)S(1)} %collective-permute-done.3.rest_3_), channel_id=1, source_target_pairs={{0,1},{1,0},{2,3},{3,2},{4,5},{5,4},{6,7},{7,6},{8,9},{9,8},{10,11... | collective-permute-start | bytes 1572872 | tf_op jit(solution)/shard_map/ppermute | solution.py:310
  89.3 5.3 %all-to-all-done = bf16[32,8,768]{2,1,0:T(8,128)(2,1)S(1)} async-done(((bf16[32,8,768]{2,1,0:T(8,128)(2,1)}), bf16[32,8,768]{2,1,0:T(8,128)(2,1)S(1)}, u32[]{:S(2)}, u32[]{:S(2)}) %all-to-all-start) | async-done | bytes 393248 | tf_op jit(solution)/shard_map/all_to_all | solution.py:297
  94.6 0.7 slice.12
  95.4 1.9 %collective-permute-start = (bf16[256,512]{1,0:T(8,128)(2,1)}, bf16[256,512]{1,0:T(8,128)(2,1)}, u32[]{:S(2)}, u32[]{:S(2)}) collective-permute-start(bf16[256,512]{1,0:T(8,128)(2,1)} %slice.12), channel_id=1, source_target_pairs={{0,1},{1,0},{2,3},{3,2},{4,5},{5,4},{6,7},{7,6},{8,9},{9,8},{10,11... | collective-permute-start | bytes 786440 | tf_op jit(solution)/shard_map/ppermute | solution.py:300
  97.4 1.8 %collective-permute-done.front_other_ref = bf16[256,512]{1,0:T(8,128)(2,1)} collective-permute-done((bf16[256,512]{1,0:T(8,128)(2,1)}, bf16[256,512]{1,0:T(8,128)(2,1)}, u32[]{:S(2)}, u32[]{:S(2)}) %collective-permute-start) | collective-permute-done | bytes 262176 | tf_op jit(solution)/shard_map/ppermute | solution.py:300
  99.2 7.3 %layer.1 = (bf16[128,1024]{1,0:T(8,128)(2,1)}, bf16[256,1280]{1,0:T(8,128)(2,1)S(1)}) custom-call(s32[2]{0:T(128)S(1)} %pad_add_fusion.place_ref, s32[2]{0:T(128)S(1)} %copy-done, bf16[256,768]{1,0:T(8,128)(2,1)S(1)} %bitcast.25, bf16[256,512]{1,0:T(8,128)(2,1)} %collective-permute-done.front_other_ref, bf16[128,512]{1,0:T(8,128)(2,1)} %dense_hbm.1, ...), custom_call_target="tpu_custom_call" | custom-call | flops 1073741824 | bytes 8388608 | tf_op jit(solution)/shard_map/layer/pallas_call | solution.py:235
  106.5 23.0 %all_to_all.15 = bf16[32,8,1280]{2,1,0:T(8,128)(2,1)S(1)} all-to-all(bf16[32,8,1280]{2,1,0:T(8,128)(2,1)S(1)} %bitcast.26), channel_id=1, replica_groups=mesh['yh'=2,'z'=8,'x'=4,'yl'=4,'core'=2] {'x','yl','core'}, dimensions={0} | all-to-all | bytes 1310720 | tf_op jit(solution)/shard_map/all_to_all | solution.py:325
  129.6 0.6 copy.21
  130.2 0.7 copy_bitcast_fusion
  (23 shorter events, 0.3 us)
Async XLA Ops:
  0.6 0.7 copy-start.4
  1.3 20.9 %copy-start.3 = (bf16[2,2,2048]{2,1,0:T(2,128)(2,1)S(1)}, bf16[2,2,2048]{2,1,0:T(2,128)(2,1)}, u32[]{:S(2)}) copy-start(bf16[2,2,2048]{2,1,0:T(2,128)(2,1)} %param.12) | copy-start | bytes 49156
  3.7 44.6 %copy-start.2 = (bf16[1,16,32768]{2,1,0:T(8,128)(2,1)S(1)}, bf16[1,16,32768]{2,1,0:T(8,128)(2,1)}, u32[]{:S(2)}) copy-start(bf16[1,16,32768]{2,1,0:T(8,128)(2,1)} %param.11) | copy-start | bytes 3145732
  3.7 38.1 %all-to-all-start.1 = ((bf16[128,2,1024]{2,1,0:T(2,128)(2,1)}), bf16[128,2,1024]{2,1,0:T(2,128)(2,1)S(1)}, u32[]{:S(2)}, u32[]{:S(2)}) async-start(bf16[128,2,1024]{2,1,0:T(2,128)(2,1)} %compare_select_fusion), calls=%async_computation.1 | async-start | bytes 1048576 | tf_op jit(solution)/shard_map/all_to_all | solution.py:285
  42.0 21.5 %collective-permute-start.2 = (bf16[256,1024]{1,0:T(8,128)(2,1)S(1)}, bf16[256,1024]{1,0:T(8,128)(2,1)S(1)}, u32[]{:S(2)}, u32[]{:S(2)}) collective-permute-start(bf16[256,1024]{1,0:T(8,128)(2,1)S(1)} %reshape.42.rest_0_), channel_id=1, source_target_pairs={{0,24},{8,0},{16,8},{24,16},{1,25},{9,1},{17,9},{25,17},{2,26},{10... | collective-permute-start | bytes 1572872 | tf_op jit(solution)/shard_map/ppermute | solution.py:294
  46.4 17.1 %collective-permute-start.1 = (bf16[256,1024]{1,0:T(8,128)(2,1)S(1)}, bf16[256,1024]{1,0:T(8,128)(2,1)S(1)}, u32[]{:S(2)}, u32[]{:S(2)}) collective-permute-start(bf16[256,1024]{1,0:T(8,128)(2,1)S(1)} %reshape.42.rest_0_), channel_id=1, source_target_pairs={{0,8},{8,16},{16,24},{24,0},{1,9},{9,17},{17,25},{25,1},{2,10},{10... | collective-permute-start | bytes 1572872 | tf_op jit(solution)/shard_map/ppermute | solution.py:293
  64.3 22.8 %collective-permute-start.3 = (bf16[256,1024]{1,0:T(8,128)(2,1)}, bf16[256,1024]{1,0:T(8,128)(2,1)S(1)}, u32[]{:S(2)}, u32[]{:S(2)}) collective-permute-start(bf16[256,1024]{1,0:T(8,128)(2,1)} %broadcast_select_fusion), channel_id=1, source_target_pairs={{0,8},{8,16},{16,24},{24,0},{1,25},{9,1},{17,9},{25,17},{2,10},{10... | collective-permute-start | bytes 1572872 | tf_op jit(solution)/shard_map/ppermute | solution.py:306
  74.8 19.9 %all-to-all-start = ((bf16[32,8,768]{2,1,0:T(8,128)(2,1)}), bf16[32,8,768]{2,1,0:T(8,128)(2,1)S(1)}, u32[]{:S(2)}, u32[]{:S(2)}) async-start(bf16[32,8,768]{2,1,0:T(8,128)(2,1)} %lookup.3), calls=%async_computation | async-start | bytes 786432 | tf_op jit(solution)/shard_map/all_to_all | solution.py:297
  80.6 18.5 %collective-permute-start.4 = (bf16[256,1024]{1,0:T(8,128)(2,1)S(1)}, bf16[256,1024]{1,0:T(8,128)(2,1)S(1)}, u32[]{:S(2)}, u32[]{:S(2)}) collective-permute-start(bf16[256,1024]{1,0:T(8,128)(2,1)S(1)} %reshape.42.rest_0_), channel_id=1, source_target_pairs={{0,1},{1,0},{2,3},{3,2},{4,5},{5,4},{6,7},{7,6},{8,9},{9,8},{10,11... | collective-permute-start | bytes 1572872 | tf_op jit(solution)/shard_map/ppermute | solution.py:310
  82.8 16.4 %collective-permute-start.6 = (bf16[256,1024]{1,0:T(8,128)(2,1)S(1)}, bf16[256,1024]{1,0:T(8,128)(2,1)S(1)}, u32[]{:S(2)}, u32[]{:S(2)}) collective-permute-start(bf16[256,1024]{1,0:T(8,128)(2,1)S(1)} %collective-permute-done.2.rest_2_), channel_id=1, source_target_pairs={{0,1},{1,0},{2,3},{3,2},{4,5},{5,4},{6,7},{7,6},{8,9},{9,8},{10,11... | collective-permute-start | bytes 1572872 | tf_op jit(solution)/shard_map/ppermute | solution.py:310
  85.0 14.2 %collective-permute-start.5 = (bf16[256,1024]{1,0:T(8,128)(2,1)S(1)}, bf16[256,1024]{1,0:T(8,128)(2,1)}, u32[]{:S(2)}, u32[]{:S(2)}) collective-permute-start(bf16[256,1024]{1,0:T(8,128)(2,1)S(1)} %collective-permute-done.1.rest_1_), channel_id=1, source_target_pairs={{0,1},{1,0},{2,3},{3,2},{4,5},{5,4},{6,7},{7,6},{8,9},{9,8},{10,11... | collective-permute-start | bytes 1572872 | tf_op jit(solution)/shard_map/ppermute | solution.py:310
  87.1 12.0 %collective-permute-start.7 = (bf16[256,1024]{1,0:T(8,128)(2,1)S(1)}, bf16[256,1024]{1,0:T(8,128)(2,1)}, u32[]{:S(2)}, u32[]{:S(2)}) collective-permute-start(bf16[256,1024]{1,0:T(8,128)(2,1)S(1)} %collective-permute-done.3.rest_3_), channel_id=1, source_target_pairs={{0,1},{1,0},{2,3},{3,2},{4,5},{5,4},{6,7},{7,6},{8,9},{9,8},{10,11... | collective-permute-start | bytes 1572872 | tf_op jit(solution)/shard_map/ppermute | solution.py:310
  95.4 3.8 %collective-permute-start = (bf16[256,512]{1,0:T(8,128)(2,1)}, bf16[256,512]{1,0:T(8,128)(2,1)}, u32[]{:S(2)}, u32[]{:S(2)}) collective-permute-start(bf16[256,512]{1,0:T(8,128)(2,1)} %slice.12), channel_id=1, source_target_pairs={{0,1},{1,0},{2,3},{3,2},{4,5},{5,4},{6,7},{7,6},{8,9},{9,8},{10,11... | collective-permute-start | bytes 786440 | tf_op jit(solution)/shard_map/ppermute | solution.py:300
  97.4 1.8 %copy-start = (s32[2]{0:T(128)S(1)}, s32[2]{0:T(128)}, u32[]{:S(2)}) copy-start(s32[2]{0:T(128)} %len_ref.1) | copy-start | bytes 28
  97.4 1.8 %copy-start.1 = (s32[128]{0:T(128)S(1)}, s32[128]{0:T(128)}, u32[]{:S(2)}) copy-start(s32[128]{0:T(128)} %param.14) | copy-start | bytes 1540

commit v7 on v6

--- a/solution.py
+++ b/solution.py
@@ -26,7 +26,7 @@
     hist_rows = history.shape[0]
     hist_width = history.shape[1] // 2
     highs = rows // LOW
-    step = min(count, 4 * TILE)
+    step = min(count, 2 * TILE)
     half = emb // 2
 
     def kernel(ids_hbm, table_ref, history_ref, *rest):
@@ -108,13 +108,13 @@
 
 def layer(front, front_other, dense, cot, mine, other, place_index, requests, lengths, own_events):
     cands, dense_width = dense.shape
-    block, width = mine[0].shape
+    block, width = mine[1].shape
     pooled_width = width - dense_width
     outer = width // block
     inner = 16
     dim = width // H
     row_count = front.shape[0]
-    hist_width = front_other.shape[1]
+    hist_width = width // 2
     owned = lengths.shape[0]
     shift = owned * own_events
     group_rows = 2 * shift
@@ -124,8 +124,8 @@
     def kernel(
         place_ref, len_ref, front_ref, front_other_ref, dense_hbm, cot_hbm, req_ref, *rest
     ):
-        mine_refs, other_refs = rest[:4], rest[4:8]
-        out_ref, back_ref, wq_ref, wo_ref, ev_ref, cot_ref, dense_ref, cot_sem, dense_sem = rest[8:]
+        mine_refs, other_refs = rest[:2], rest[2:4]
+        out_ref, back_ref, wq_ref, wo_ref, ev_ref, cot_ref, dense_ref, cot_sem, dense_sem = rest[4:]
         cot_copy = pltpu.make_async_copy(cot_hbm, cot_ref, cot_sem)
         dense_copy = pltpu.make_async_copy(dense_hbm, dense_ref, dense_sem)
         dense_copy.start()
@@ -133,7 +133,8 @@
         x = place_ref[1]
 
         def place(pieces, target):
-            for piece, offset in zip(pieces, (0, outer - 1, 1, 2)):
+            near, far = pieces
+            for piece, offset in ((near.at[0], 0), (near.at[1], outer - 1), (near.at[2], 1), (far, 2)):
                 for i in range(block // inner):
                     start = pl.multiple_of((i * outer + lax.rem(x + offset, outer)) * inner, inner)
                     target[pl.ds(start, inner), :] = piece[i * inner : (i + 1) * inner, :]
@@ -143,13 +144,13 @@
             place(mine_refs, wq_ref)
             place(other_refs, wo_ref)
             ev_ref[:, :hist_width] = front_ref[:, :hist_width]
-            ev_ref[:, hist_width:] = front_other_ref[...]
+            ev_ref[:, hist_width:] = front_other_ref[:, :hist_width]
 
         @pl.when(place_ref[0] != 0)
         def _():
             place(other_refs, wq_ref)
             place(mine_refs, wo_ref)
-            ev_ref[:, :hist_width] = front_other_ref[...]
+            ev_ref[:, :hist_width] = front_other_ref[:, :hist_width]
             ev_ref[:, hist_width:] = front_ref[:, :hist_width]
 
         parts = [
@@ -234,7 +235,7 @@
     hbm = pl.BlockSpec(memory_space=pltpu.HBM)
     return pl.pallas_call(
         kernel,
-        in_specs=[smem, smem, vmem, vmem, hbm, hbm] + [vmem] * 9,
+        in_specs=[smem, smem, vmem, vmem, hbm, hbm] + [vmem] * 5,
         out_specs=[vmem] * 2,
         out_shape=[
             jax.ShapeDtypeStruct((cands, width), jnp.bfloat16),
@@ -280,14 +281,14 @@
     swap = [(0, 1), (1, 0)]
 
     slab = sizes["yh"] * sizes["z"] * sizes["yl"]
-    to_core = lax.broadcasted_iota(jnp.int32, (2 * slab, own_rows, model_width), 0) % 2
-    own = jnp.where(to_core == 0, w_query[None], w_out[None])
+    own = jnp.concatenate([w_query, w_out], axis=0).reshape(1, 2, own_rows, model_width)
+    own = jnp.broadcast_to(own, (slab, 2, own_rows, model_width)).reshape(2 * slab, own_rows, model_width)
     w1 = lax.all_to_all(own, ("yh", "z", "yl", "core"), 0, 0)
-    w1 = w1.reshape(-1, model_width)
+    w1 = lax.optimization_barrier(w1.reshape(-1, model_width))
 
     history = jnp.transpose(history_kv.reshape(owned, own_events, 2, model_width), (2, 0, 1, 3))
     history = history.reshape(-1, model_width)
-    early = group // 4 * 3
+    early = group // 8 * 7
     blocks = lookup(emb_ids[0], tables[0], history, cands, 0, early)
 
     left = lax.ppermute(w1, "x", up)
@@ -296,26 +297,24 @@
 
     front = lax.all_to_all(blocks, CAND, 0, 0)
     front = front.reshape(-1, front.shape[2])
-    hist_width = model_width // 2
-    front_other = lax.ppermute(front[:, :hist_width], "core", swap)
+    front_other = lax.ppermute(front, "core", swap)
 
     both_ways = [(2 * i, 2 * ((i + 1) % ring)) for i in range(ring)] + [
         (2 * i + 1, 2 * ((i - 1) % ring) + 1) for i in range(ring)
     ]
     passed = jnp.where(lax.axis_index("core") == 0, left, right)
     far = lax.ppermute(passed, ("x", "core"), both_ways)
-    mine = (w1, left, right, far)
-    other = []
-    for piece in mine:
-        other.append(lax.ppermute(piece, "core", swap))
+    near = jnp.stack([w1, left, right])
+    near_other = lax.ppermute(near, "core", swap)
+    far_other = lax.ppermute(far, "core", swap)
 
     cand_out, back = layer(
         front,
         front_other,
         dense_feat,
         cotangent,
-        mine,
-        tuple(other),
+        (near, far),
+        (near_other, far_other),
         jnp.stack([lax.axis_index("core"), lax.axis_index("x")]),
         cand_request.reshape(1, -1),
         hist_len,

time: 132 us -> 145 us (1.098)
  blocking collectives: 23 us -> 62.5 us
  starting transfers between devices: 45.8 us -> 25.1 us
  waiting for transfers between devices: 26.6 us -> 22.6 us
    all_to_all x0 -> x1, blocking collectives: none -> 37.8 us  [on_device(): w1 = lax.all_to_all(own, ('yh', 'z', 'yl', 'core'), 0, 0)]
    all_to_all x1 -> x0, waiting for transfers between devices: 19.5 us -> none  [on_device(): w1 = lax.all_to_all(own, ('yh', 'z', 'yl', 'core'), 0, 0)]
    all_to_all x1 -> x0, starting transfers between devices: 18.5 us -> none  [on_device(): w1 = lax.all_to_all(own, ('yh', 'z', 'yl', 'core'), 0, 0)]
    ppermute x1, waiting for transfers between devices: 0.01 us -> 7.93 us  [on_device(): right = lax.ppermute(w1, 'x', down)]
    ppermute x1, waiting for transfers between devices: 0.01 us -> 7.9 us  [on_device(): far = lax.ppermute(passed, ('x', 'core'), both_ways)]
    all_to_all x1, waiting for transfers between devices: 5.32 us -> 0.01 us  [on_device(): front = lax.all_to_all(blocks, CAND, 0, 0)]
    ppermute x1, waiting for transfers between devices: 0.01 us -> 5.04 us  [on_device(): left = lax.ppermute(w1, 'x', up)]
    select_n x1 -> x0, other arithmetic: 2.36 us -> none  [on_device(): own = jnp.where(to_core == 0, w_query[None], w_out[None])]
  transfers between devices with their start and end apart: 10 -> 7, of which waited for: 3 -> 4; matrix products, arithmetic and copies ran while one was open for 1% -> 1% of each run, Pallas kernels for 16% -> 14%
where the time goes in v7:
time: 145 us; the launch traced here: 144 us
  blocking collectives  62.5 us (43%)
  Pallas kernels  27.8 us (19%)
  starting transfers between devices  25.1 us (17%)
  waiting for transfers between devices  22.6 us (16%)
  local copies, waits for them, and re-layouts  3.38 us (2%)
  other arithmetic  2.16 us (1%)
    all_to_all x1, blocking collectives, on_device(): w1 = lax.all_to_all(own, ('yh', 'z', 'yl', 'core'), 0, 0)  37.8 us
    all_to_all x1, blocking collectives, on_device(): lax.all_to_all(back.reshape(cand_devices, -1, back.shape[1]), CAND, 0, 0)  24.7 us
    pallas_call x2, Pallas kernels, lookup(): pl.pallas_call(kernel, grid=(count // step,), in_specs=[hbm, pl.BlockSpec...  20.4 us
    ppermute x1, waiting for transfers between devices, on_device(): right = lax.ppermute(w1, 'x', down)  7.93 us
    ppermute x1, waiting for transfers between devices, on_device(): far = lax.ppermute(passed, ('x', 'core'), both_ways)  7.9 us
    pallas_call x1, Pallas kernels, layer(): pl.pallas_call(kernel, in_specs=[smem, smem, vmem, vmem, hbm, hbm] + [vme...  7.33 us
    ppermute x1, waiting for transfers between devices, on_device(): left = lax.ppermute(w1, 'x', up)  5.04 us
    ppermute x1, starting transfers between devices, on_device(): near_other = lax.ppermute(near, 'core', swap)  4.53 us
  transfers between devices with their start and end apart: 7, of which 4 were waited for; matrix products, arithmetic and copies ran while one was open for 1% of the time, Pallas kernels for 14%

profile of v7, /device:TPU:1, one launch (start us, length us, event | category | flops | bytes accessed | tf_op | source)
XLA Modules:
  0.0 144.4 jit_solution(1386687404020229659)
XLA Ops:
  0.6 0.7 pad_maximum_fusion.1
  1.4 0.3 broadcast_in_dim.8
  1.7 37.8 %all_to_all.15 = bf16[128,2,1024]{2,1,0:T(2,128)(2,1)S(1)} all-to-all(bf16[128,2,1024]{2,1,0:T(2,128)(2,1)S(1)} %bitcast.34), channel_id=1, replica_groups=mesh['yh'=2,'z'=8,'x'=4,'yl'=4,'core'=2] {'yh','z','yl','core'}, dimensions={0} | all-to-all | bytes 1048576 | tf_op jit(solution)/shard_map/all_to_all | solution.py:286
  39.4 0.2 reshape.46
  39.6 4.4 %collective-permute-start.2 = (bf16[256,1024]{1,0:T(8,128)(2,1)S(1)}, bf16[256,1024]{1,0:T(8,128)(2,1)S(1)}, u32[]{:S(2)}, u32[]{:S(2)}) collective-permute-start(bf16[256,1024]{1,0:T(8,128)(2,1)S(1)} %reshape.46), channel_id=1, source_target_pairs={{0,24},{8,0},{16,8},{24,16},{1,25},{9,1},{17,9},{25,17},{2,26},{10... | collective-permute-start | bytes 1572872 | tf_op jit(solution)/shard_map/ppermute | solution.py:295
  44.0 1.9 %collective-permute-start.1 = (bf16[256,1024]{1,0:T(8,128)(2,1)S(1)}, bf16[256,1024]{1,0:T(8,128)(2,1)S(1)}, u32[]{:S(2)}, u32[]{:S(2)}) collective-permute-start(bf16[256,1024]{1,0:T(8,128)(2,1)S(1)} %reshape.46), channel_id=1, source_target_pairs={{0,8},{8,16},{16,24},{24,0},{1,9},{9,17},{17,25},{25,1},{2,10},{10... | collective-permute-start | bytes 1572872 | tf_op jit(solution)/shard_map/ppermute | solution.py:294
  46.0 7.9 %collective-permute-done.2 = bf16[256,1024]{1,0:T(8,128)(2,1)S(1)} collective-permute-done((bf16[256,1024]{1,0:T(8,128)(2,1)S(1)}, bf16[256,1024]{1,0:T(8,128)(2,1)S(1)}, u32[]{:S(2)}, u32[]{:S(2)}) %collective-permute-start.2) | collective-permute-done | bytes 524320 | tf_op jit(solution)/shard_map/ppermute | solution.py:295
  53.9 5.0 %collective-permute-done.1 = bf16[256,1024]{1,0:T(8,128)(2,1)S(1)} collective-permute-done((bf16[256,1024]{1,0:T(8,128)(2,1)S(1)}, bf16[256,1024]{1,0:T(8,128)(2,1)S(1)}, u32[]{:S(2)}, u32[]{:S(2)}) %collective-permute-start.1) | collective-permute-done | bytes 524320 | tf_op jit(solution)/shard_map/ppermute | solution.py:294
  59.0 0.8 copy-done.5
  60.0 4.5 %collective-permute-start.4 = (bf16[3,256,1024]{2,1,0:T(8,128)(2,1)S(1)}, bf16[3,256,1024]{2,1,0:T(8,128)(2,1)S(1)}, u32[]{:S(2)}, u32[]{:S(2)}) collective-permute-start(bf16[3,256,1024]{2,1,0:T(8,128)(2,1)S(1)} %pad_maximum_fusion.rest_0_), channel_id=1, source_target_pairs={{0,1},{1,0},{2,3},{3,2},{4,5},{5,4},{6,7},{7,6},{8,9},{9,8},{10,11... | collective-permute-start | bytes 4718600 | tf_op jit(solution)/shard_map/ppermute | solution.py:308
  64.5 17.4 %lookup.2.rest_0_ = bf16[32,8,768]{2,1,0:T(8,128)(2,1)S(1)} custom-call(s32[4,4096]{1,0:T(4,128)} %bitcast.42, bf16[16,32768]{1,0:T(8,128)(2,1)S(1)} %bitcast.32, bf16[8,1024]{1,0:T(8,128)(2,1)S(1)} %reshape.42.history_ref), custom_call_target="tpu_custom_call" | custom-call | flops 15032385536 | bytes 1048576 | tf_op jit(solution)/shard_map/lookup/pallas_call | solution.py:72
  81.9 3.1 %lookup.3 = bf16[32,8,768]{2,1,0:T(8,128)(2,1)S(1)} custom-call(s32[4,4096]{1,0:T(4,128)} %bitcast.43, bf16[16,32768]{1,0:T(8,128)(2,1)S(1)} %bitcast.33, bf16[8,1024]{1,0:T(8,128)(2,1)S(1)} %reshape.42.history_ref, bf16[32,8,768]{2,1,0:T(8,128)(2,1)S(1)} %lookup.2.rest_0_), custom_call_target="tpu_custom_call", output_to_operand_aliasing={{}: (3, {})} | custom-call | flops 2147483648 | bytes 1048576 | tf_op jit(solution)/shard_map/lookup/pallas_call | solution.py:72
  85.0 0.8 copy-done
  85.7 3.9 %all-to-all-start = ((bf16[32,8,768]{2,1,0:T(8,128)(2,1)}), bf16[32,8,768]{2,1,0:T(8,128)(2,1)S(1)}, u32[]{:S(2)}, u32[]{:S(2)}) async-start(bf16[32,8,768]{2,1,0:T(8,128)(2,1)} %copy-done), calls=%async_computation | async-start | bytes 786432 | tf_op jit(solution)/shard_map/all_to_all | solution.py:298
  89.7 1.1 broadcast_select_fusion
  90.8 4.5 %collective-permute-start.3 = (bf16[256,1024]{1,0:T(8,128)(2,1)S(1)}, bf16[256,1024]{1,0:T(8,128)(2,1)}, u32[]{:S(2)}, u32[]{:S(2)}) collective-permute-start(bf16[256,1024]{1,0:T(8,128)(2,1)S(1)} %broadcast_select_fusion), channel_id=1, source_target_pairs={{0,8},{8,16},{16,24},{24,0},{1,25},{9,1},{17,9},{25,17},{2,10},{10... | collective-permute-start | bytes 1572872 | tf_op jit(solution)/shard_map/ppermute | solution.py:306
  95.3 7.9 %collective-permute-done.3.rest_1_ = bf16[256,1024]{1,0:T(8,128)(2,1)} collective-permute-done((bf16[256,1024]{1,0:T(8,128)(2,1)S(1)}, bf16[256,1024]{1,0:T(8,128)(2,1)}, u32[]{:S(2)}, u32[]{:S(2)}) %collective-permute-start.3) | collective-permute-done | bytes 524320 | tf_op jit(solution)/shard_map/ppermute | solution.py:306
  103.2 3.9 %collective-permute-start.5 = (bf16[256,1024]{1,0:T(8,128)(2,1)}, bf16[256,1024]{1,0:T(8,128)(2,1)}, u32[]{:S(2)}, u32[]{:S(2)}) collective-permute-start(bf16[256,1024]{1,0:T(8,128)(2,1)} %collective-permute-done.3.rest_1_), channel_id=1, source_target_pairs={{0,1},{1,0},{2,3},{3,2},{4,5},{5,4},{6,7},{7,6},{8,9},{9,8},{10,11... | collective-permute-start | bytes 1572872 | tf_op jit(solution)/shard_map/ppermute | solution.py:309
  107.2 1.9 %collective-permute-start = (bf16[256,768]{1,0:T(8,128)(2,1)S(1)}, bf16[256,768]{1,0:T(8,128)(2,1)}, u32[]{:S(2)}, u32[]{:S(2)}) collective-permute-start(bf16[256,768]{1,0:T(8,128)(2,1)S(1)} %bitcast.28), channel_id=1, source_target_pairs={{0,1},{1,0},{2,3},{3,2},{4,5},{5,4},{6,7},{7,6},{8,9},{9,8},{10,11... | collective-permute-start | bytes 1179656 | tf_op jit(solution)/shard_map/ppermute | solution.py:300
  109.2 1.7 %collective-permute-done.front_other_ref = bf16[256,768]{1,0:T(8,128)(2,1)} collective-permute-done((bf16[256,768]{1,0:T(8,128)(2,1)S(1)}, bf16[256,768]{1,0:T(8,128)(2,1)}, u32[]{:S(2)}, u32[]{:S(2)}) %collective-permute-start) | collective-permute-done | bytes 393248 | tf_op jit(solution)/shard_map/ppermute | solution.py:300
  110.9 7.3 %layer.1 = (bf16[128,1024]{1,0:T(8,128)(2,1)}, bf16[256,1280]{1,0:T(8,128)(2,1)S(1)}) custom-call(s32[2]{0:T(128)S(1)} %pad_add_fusion.place_ref, s32[2]{0:T(128)S(1)} %copy-done.1, bf16[256,768]{1,0:T(8,128)(2,1)S(1)} %bitcast.29, bf16[256,768]{1,0:T(8,128)(2,1)} %collective-permute-done.front_other_ref, bf16[128,512]{1,0:T(8,128)(2,1)} %dense_hbm.1, ...), custom_call_target="tpu_custom_call" | custom-call | flops 1073741824 | bytes 8388608 | tf_op jit(solution)/shard_map/layer/pallas_call | solution.py:236
  118.3 24.7 %all_to_all.16 = bf16[32,8,1280]{2,1,0:T(8,128)(2,1)S(1)} all-to-all(bf16[32,8,1280]{2,1,0:T(8,128)(2,1)S(1)} %bitcast.30), channel_id=1, replica_groups=mesh['yh'=2,'z'=8,'x'=4,'yl'=4,'core'=2] {'x','yl','core'}, dimensions={0} | all-to-all | bytes 1310720 | tf_op jit(solution)/shard_map/all_to_all | solution.py:324
  143.1 0.6 copy.21
  143.7 0.7 copy_bitcast_fusion
  (22 shorter events, 0.4 us)
Async XLA Ops:
  0.6 45.3 %copy-start.6 = (bf16[2,2,2048]{2,1,0:T(2,128)(2,1)S(1)}, bf16[2,2,2048]{2,1,0:T(2,128)(2,1)}, u32[]{:S(2)}) copy-start(bf16[2,2,2048]{2,1,0:T(2,128)(2,1)} %param.12) | copy-start | bytes 49156
  39.6 14.3 %collective-permute-start.2 = (bf16[256,1024]{1,0:T(8,128)(2,1)S(1)}, bf16[256,1024]{1,0:T(8,128)(2,1)S(1)}, u32[]{:S(2)}, u32[]{:S(2)}) collective-permute-start(bf16[256,1024]{1,0:T(8,128)(2,1)S(1)} %reshape.46), channel_id=1, source_target_pairs={{0,24},{8,0},{16,8},{24,16},{1,25},{9,1},{17,9},{25,17},{2,26},{10... | collective-permute-start | bytes 1572872 | tf_op jit(solution)/shard_map/ppermute | solution.py:295
  44.0 15.0 %collective-permute-start.1 = (bf16[256,1024]{1,0:T(8,128)(2,1)S(1)}, bf16[256,1024]{1,0:T(8,128)(2,1)S(1)}, u32[]{:S(2)}, u32[]{:S(2)}) collective-permute-start(bf16[256,1024]{1,0:T(8,128)(2,1)S(1)} %reshape.46), channel_id=1, source_target_pairs={{0,8},{8,16},{16,24},{24,0},{1,9},{9,17},{17,25},{25,1},{2,10},{10... | collective-permute-start | bytes 1572872 | tf_op jit(solution)/shard_map/ppermute | solution.py:294
  53.9 5.1 %copy-start.4 = (bf16[256,1024]{1,0:T(8,128)(2,1)}, bf16[256,1024]{1,0:T(8,128)(2,1)S(1)}, u32[]{:S(2)}) copy-start(bf16[256,1024]{1,0:T(8,128)(2,1)S(1)} %collective-permute-done.2) | copy-start | bytes 1572868
  59.0 0.8 copy-start.5
  59.8 4.7 %copy-start.3 = (bf16[1,16,32768]{2,1,0:T(8,128)(2,1)S(1)}, bf16[1,16,32768]{2,1,0:T(8,128)(2,1)}, u32[]{:S(2)}) copy-start(bf16[1,16,32768]{2,1,0:T(8,128)(2,1)} %param.11) | copy-start | bytes 3145732
  60.0 51.0 %collective-permute-start.4 = (bf16[3,256,1024]{2,1,0:T(8,128)(2,1)S(1)}, bf16[3,256,1024]{2,1,0:T(8,128)(2,1)S(1)}, u32[]{:S(2)}, u32[]{:S(2)}) collective-permute-start(bf16[3,256,1024]{2,1,0:T(8,128)(2,1)S(1)} %pad_maximum_fusion.rest_0_), channel_id=1, source_target_pairs={{0,1},{1,0},{2,3},{3,2},{4,5},{5,4},{6,7},{7,6},{8,9},{9,8},{10,11... | collective-permute-start | bytes 4718600 | tf_op jit(solution)/shard_map/ppermute | solution.py:308
  85.0 0.8 copy-start
  85.7 25.2 %copy-start.1 = (s32[2]{0:T(128)S(1)}, s32[2]{0:T(128)}, u32[]{:S(2)}) copy-start(s32[2]{0:T(128)} %len_ref.1) | copy-start | bytes 28
  85.7 25.2 %copy-start.2 = (s32[128]{0:T(128)S(1)}, s32[128]{0:T(128)}, u32[]{:S(2)}) copy-start(s32[128]{0:T(128)} %param.14) | copy-start | bytes 1540
  85.7 21.4 %all-to-all-start = ((bf16[32,8,768]{2,1,0:T(8,128)(2,1)}), bf16[32,8,768]{2,1,0:T(8,128)(2,1)S(1)}, u32[]{:S(2)}, u32[]{:S(2)}) async-start(bf16[32,8,768]{2,1,0:T(8,128)(2,1)} %copy-done), calls=%async_computation | async-start | bytes 786432 | tf_op jit(solution)/shard_map/all_to_all | solution.py:298
  90.8 12.4 %collective-permute-start.3 = (bf16[256,1024]{1,0:T(8,128)(2,1)S(1)}, bf16[256,1024]{1,0:T(8,128)(2,1)}, u32[]{:S(2)}, u32[]{:S(2)}) collective-permute-start(bf16[256,1024]{1,0:T(8,128)(2,1)S(1)} %broadcast_select_fusion), channel_id=1, source_target_pairs={{0,8},{8,16},{16,24},{24,0},{1,25},{9,1},{17,9},{25,17},{2,10},{10... | collective-permute-start | bytes 1572872 | tf_op jit(solution)/shard_map/ppermute | solution.py:306
  103.2 7.7 %collective-permute-start.5 = (bf16[256,1024]{1,0:T(8,128)(2,1)}, bf16[256,1024]{1,0:T(8,128)(2,1)}, u32[]{:S(2)}, u32[]{:S(2)}) collective-permute-start(bf16[256,1024]{1,0:T(8,128)(2,1)} %collective-permute-done.3.rest_1_), channel_id=1, source_target_pairs={{0,1},{1,0},{2,3},{3,2},{4,5},{5,4},{6,7},{7,6},{8,9},{9,8},{10,11... | collective-permute-start | bytes 1572872 | tf_op jit(solution)/shard_map/ppermute | solution.py:309
  107.2 3.7 %collective-permute-start = (bf16[256,768]{1,0:T(8,128)(2,1)S(1)}, bf16[256,768]{1,0:T(8,128)(2,1)}, u32[]{:S(2)}, u32[]{:S(2)}) collective-permute-start(bf16[256,768]{1,0:T(8,128)(2,1)S(1)} %bitcast.28), channel_id=1, source_target_pairs={{0,1},{1,0},{2,3},{3,2},{4,5},{5,4},{6,7},{7,6},{8,9},{9,8},{10,11... | collective-permute-start | bytes 1179656 | tf_op jit(solution)/shard_map/ppermute | solution.py:300

commit v8 on v7

--- a/solution.py
+++ b/solution.py
@@ -132,24 +132,24 @@
         cot_copy.start()
         x = place_ref[1]
 
-        def place(pieces, target):
+        def place(pieces, target, first, second):
             near, far = pieces
-            for piece, offset in ((near.at[0], 0), (near.at[1], outer - 1), (near.at[2], 1), (far, 2)):
+            for piece, offset in ((near.at[0], 0), (near.at[1], first), (near.at[2], second), (far, 2)):
                 for i in range(block // inner):
                     start = pl.multiple_of((i * outer + lax.rem(x + offset, outer)) * inner, inner)
                     target[pl.ds(start, inner), :] = piece[i * inner : (i + 1) * inner, :]
 
         @pl.when(place_ref[0] == 0)
         def _():
-            place(mine_refs, wq_ref)
-            place(other_refs, wo_ref)
+            place(mine_refs, wq_ref, outer - 1, 1)
+            place(other_refs, wo_ref, 1, outer - 1)
             ev_ref[:, :hist_width] = front_ref[:, :hist_width]
             ev_ref[:, hist_width:] = front_other_ref[:, :hist_width]
 
         @pl.when(place_ref[0] != 0)
         def _():
-            place(other_refs, wq_ref)
-            place(mine_refs, wo_ref)
+            place(other_refs, wq_ref, outer - 1, 1)
+            place(mine_refs, wo_ref, 1, outer - 1)
             ev_ref[:, :hist_width] = front_other_ref[:, :hist_width]
             ev_ref[:, hist_width:] = front_ref[:, :hist_width]
 
@@ -276,8 +276,6 @@
     group = emb_ids.shape[2]
     cands = group // cand_devices
     ring = sizes["x"]
-    up = [(i, (i + 1) % ring) for i in range(ring)]
-    down = [(i, (i - 1) % ring) for i in range(ring)]
     swap = [(0, 1), (1, 0)]
 
     slab = sizes["yh"] * sizes["z"] * sizes["yl"]
@@ -291,20 +289,21 @@
     early = group // 8 * 7
     blocks = lookup(emb_ids[0], tables[0], history, cands, 0, early)
 
-    left = lax.ppermute(w1, "x", up)
-    right = lax.ppermute(w1, "x", down)
+    outward = [(2 * i, 2 * ((i + 1) % ring)) for i in range(ring)] + [
+        (2 * i + 1, 2 * ((i - 1) % ring) + 1) for i in range(ring)
+    ]
+    inward = [(target, source) for source, target in outward]
+    side_a = lax.ppermute(w1, ("x", "core"), outward)
+    side_b = lax.ppermute(w1, ("x", "core"), inward)
+
     blocks = lookup(emb_ids[0], tables[0], history, cands, early, group - early, blocks)
 
     front = lax.all_to_all(blocks, CAND, 0, 0)
     front = front.reshape(-1, front.shape[2])
     front_other = lax.ppermute(front, "core", swap)
 
-    both_ways = [(2 * i, 2 * ((i + 1) % ring)) for i in range(ring)] + [
-        (2 * i + 1, 2 * ((i - 1) % ring) + 1) for i in range(ring)
-    ]
-    passed = jnp.where(lax.axis_index("core") == 0, left, right)
-    far = lax.ppermute(passed, ("x", "core"), both_ways)
-    near = jnp.stack([w1, left, right])
+    far = lax.ppermute(side_a, ("x", "core"), outward)
+    near = jnp.stack([w1, side_a, side_b])
     near_other = lax.ppermute(near, "core", swap)
     far_other = lax.ppermute(far, "core", swap)
 

time: 145 us -> 144 us (level)
    ppermute x1, starting transfers between devices: 4.53 us -> 2.42 us  [on_device(): near_other = lax.ppermute(near, 'core', swap)]
    all_to_all x1, starting transfers between devices: 3.93 us -> 5.69 us  [on_device(): front = lax.all_to_all(blocks, CAND, 0, 0)]
  transfers between devices with their start and end apart: 7 -> 7, of which waited for: 4 -> 4; matrix products, arithmetic and copies ran while one was open for 1% -> 0% of each run, Pallas kernels for 14% -> 14%
where the time goes in v8:
time: 144 us; the launch traced here: 143 us
  blocking collectives  62.5 us (43%)
  Pallas kernels  27.8 us (19%)
  starting transfers between devices  24.9 us (17%)
  waiting for transfers between devices  21.7 us (15%)
  local copies, waits for them, and re-layouts  4.69 us (3%)
    all_to_all x1, blocking collectives, on_device(): w1 = lax.all_to_all(own, ('yh', 'z', 'yl', 'core'), 0, 0)  37.8 us
    all_to_all x1, blocking collectives, on_device(): lax.all_to_all(back.reshape(cand_devices, -1, back.shape[1]), CAND, 0, 0)  24.8 us
    pallas_call x2, Pallas kernels, lookup(): pl.pallas_call(kernel, grid=(count // step,), in_specs=[hbm, pl.BlockSpec...  20.4 us
    ppermute x1, waiting for transfers between devices, on_device(): far = lax.ppermute(side_a, ('x', 'core'), outward)  8.6 us
    pallas_call x1, Pallas kernels, layer(): pl.pallas_call(kernel, in_specs=[smem, smem, vmem, vmem, hbm, hbm] + [vme...  7.32 us
    ppermute x1, waiting for transfers between devices, on_device(): side_a = lax.ppermute(w1, ('x', 'core'), outward)  6.79 us
    all_to_all x1, starting transfers between devices, on_device(): front = lax.all_to_all(blocks, CAND, 0, 0)  5.69 us
    ppermute x1, waiting for transfers between devices, on_device(): side_b = lax.ppermute(w1, ('x', 'core'), inward)  4.58 us
  transfers between devices with their start and end apart: 7, of which 4 were waited for; matrix products, arithmetic and copies ran while one was open for 0% of the time, Pallas kernels for 14%

profile of v8, /device:TPU:1, one launch (start us, length us, event | category | flops | bytes accessed | tf_op | source)
XLA Modules:
  0.0 143.5 jit_solution(12962719696905319980)
XLA Ops:
  0.6 0.7 pad_maximum_fusion.1
  1.4 0.3 broadcast_in_dim.8
  1.7 37.8 %all_to_all.15 = bf16[128,2,1024]{2,1,0:T(2,128)(2,1)S(1)} all-to-all(bf16[128,2,1024]{2,1,0:T(2,128)(2,1)S(1)} %bitcast.34), channel_id=1, replica_groups=mesh['yh'=2,'z'=8,'x'=4,'yl'=4,'core'=2] {'yh','z','yl','core'}, dimensions={0} | all-to-all | bytes 1048576 | tf_op jit(solution)/shard_map/all_to_all | solution.py:284
  39.6 3.1 %collective-permute-start.2 = (bf16[256,1024]{1,0:T(8,128)(2,1)S(1)}, bf16[256,1024]{1,0:T(8,128)(2,1)S(1)}, u32[]{:S(2)}, u32[]{:S(2)}) collective-permute-start(bf16[256,1024]{1,0:T(8,128)(2,1)S(1)} %reshape.46), channel_id=1, source_target_pairs={{8,0},{16,8},{24,16},{0,24},{25,1},{1,9},{9,17},{17,25},{10,2},{18... | collective-permute-start | bytes 1572872 | tf_op jit(solution)/shard_map/ppermute | solution.py:297
  42.8 3.4 %collective-permute-start.1 = (bf16[256,1024]{1,0:T(8,128)(2,1)S(1)}, bf16[256,1024]{1,0:T(8,128)(2,1)S(1)}, u32[]{:S(2)}, u32[]{:S(2)}) collective-permute-start(bf16[256,1024]{1,0:T(8,128)(2,1)S(1)} %reshape.46), channel_id=1, source_target_pairs={{0,8},{8,16},{16,24},{24,0},{1,25},{9,1},{17,9},{25,17},{2,10},{10... | collective-permute-start | bytes 1572872 | tf_op jit(solution)/shard_map/ppermute | solution.py:296
  46.2 4.6 %collective-permute-done.2 = bf16[256,1024]{1,0:T(8,128)(2,1)S(1)} collective-permute-done((bf16[256,1024]{1,0:T(8,128)(2,1)S(1)}, bf16[256,1024]{1,0:T(8,128)(2,1)S(1)}, u32[]{:S(2)}, u32[]{:S(2)}) %collective-permute-start.2) | collective-permute-done | bytes 524320 | tf_op jit(solution)/shard_map/ppermute | solution.py:297
  50.8 6.8 %collective-permute-done.1 = bf16[256,1024]{1,0:T(8,128)(2,1)S(1)} collective-permute-done((bf16[256,1024]{1,0:T(8,128)(2,1)S(1)}, bf16[256,1024]{1,0:T(8,128)(2,1)S(1)}, u32[]{:S(2)}, u32[]{:S(2)}) %collective-permute-start.1) | collective-permute-done | bytes 524320 | tf_op jit(solution)/shard_map/ppermute | solution.py:296
  57.6 0.8 copy-done.4
  58.5 2.4 %collective-permute-start.4 = (bf16[3,256,1024]{2,1,0:T(8,128)(2,1)S(1)}, bf16[3,256,1024]{2,1,0:T(8,128)(2,1)S(1)}, u32[]{:S(2)}, u32[]{:S(2)}) collective-permute-start(bf16[3,256,1024]{2,1,0:T(8,128)(2,1)S(1)} %pad_maximum_fusion.rest_0_), channel_id=1, source_target_pairs={{0,1},{1,0},{2,3},{3,2},{4,5},{5,4},{6,7},{7,6},{8,9},{9,8},{10,11... | collective-permute-start | bytes 4718600 | tf_op jit(solution)/shard_map/ppermute | solution.py:307
  61.0 17.4 %lookup.2.rest_0_ = bf16[32,8,768]{2,1,0:T(8,128)(2,1)S(1)} custom-call(s32[4,4096]{1,0:T(4,128)} %bitcast.42, bf16[16,32768]{1,0:T(8,128)(2,1)S(1)} %bitcast.32, bf16[8,1024]{1,0:T(8,128)(2,1)S(1)} %reshape.42.history_ref), custom_call_target="tpu_custom_call" | custom-call | flops 15032385536 | bytes 1048576 | tf_op jit(solution)/shard_map/lookup/pallas_call | solution.py:72
  78.4 3.1 %lookup.3 = bf16[32,8,768]{2,1,0:T(8,128)(2,1)S(1)} custom-call(s32[4,4096]{1,0:T(4,128)} %bitcast.43, bf16[16,32768]{1,0:T(8,128)(2,1)S(1)} %bitcast.33, bf16[8,1024]{1,0:T(8,128)(2,1)S(1)} %reshape.42.history_ref, bf16[32,8,768]{2,1,0:T(8,128)(2,1)S(1)} %lookup.2.rest_0_), custom_call_target="tpu_custom_call", output_to_operand_aliasing={{}: (3, {})} | custom-call | flops 2147483648 | bytes 1048576 | tf_op jit(solution)/shard_map/lookup/pallas_call | solution.py:72
  81.4 0.8 copy-done
  82.2 5.7 %all-to-all-start = ((bf16[32,8,768]{2,1,0:T(8,128)(2,1)}), bf16[32,8,768]{2,1,0:T(8,128)(2,1)S(1)}, u32[]{:S(2)}, u32[]{:S(2)}) async-start(bf16[32,8,768]{2,1,0:T(8,128)(2,1)} %copy-done), calls=%async_computation | async-start | bytes 786432 | tf_op jit(solution)/shard_map/all_to_all | solution.py:301
  87.9 4.5 %collective-permute-start.3 = (bf16[256,1024]{1,0:T(8,128)(2,1)}, bf16[256,1024]{1,0:T(8,128)(2,1)}, u32[]{:S(2)}, u32[]{:S(2)}) collective-permute-start(bf16[256,1024]{1,0:T(8,128)(2,1)} %copy-done.4), channel_id=1, source_target_pairs={{0,8},{8,16},{16,24},{24,0},{1,25},{9,1},{17,9},{25,17},{2,10},{10... | collective-permute-start | bytes 1572872 | tf_op jit(solution)/shard_map/ppermute | solution.py:305
  92.4 8.6 %collective-permute-done.3.rest_1_ = bf16[256,1024]{1,0:T(8,128)(2,1)} collective-permute-done((bf16[256,1024]{1,0:T(8,128)(2,1)}, bf16[256,1024]{1,0:T(8,128)(2,1)}, u32[]{:S(2)}, u32[]{:S(2)}) %collective-permute-start.3) | collective-permute-done | bytes 524320 | tf_op jit(solution)/shard_map/ppermute | solution.py:305
  101.0 3.8 %collective-permute-start.5 = (bf16[256,1024]{1,0:T(8,128)(2,1)}, bf16[256,1024]{1,0:T(8,128)(2,1)}, u32[]{:S(2)}, u32[]{:S(2)}) collective-permute-start(bf16[256,1024]{1,0:T(8,128)(2,1)} %collective-permute-done.3.rest_1_), channel_id=1, source_target_pairs={{0,1},{1,0},{2,3},{3,2},{4,5},{5,4},{6,7},{7,6},{8,9},{9,8},{10,11... | collective-permute-start | bytes 1572872 | tf_op jit(solution)/shard_map/ppermute | solution.py:308
  104.9 1.9 %collective-permute-start = (bf16[256,768]{1,0:T(8,128)(2,1)S(1)}, bf16[256,768]{1,0:T(8,128)(2,1)}, u32[]{:S(2)}, u32[]{:S(2)}) collective-permute-start(bf16[256,768]{1,0:T(8,128)(2,1)S(1)} %bitcast.28), channel_id=1, source_target_pairs={{0,1},{1,0},{2,3},{3,2},{4,5},{5,4},{6,7},{7,6},{8,9},{9,8},{10,11... | collective-permute-start | bytes 1179656 | tf_op jit(solution)/shard_map/ppermute | solution.py:303
  106.9 1.7 %collective-permute-done.front_other_ref = bf16[256,768]{1,0:T(8,128)(2,1)} collective-permute-done((bf16[256,768]{1,0:T(8,128)(2,1)S(1)}, bf16[256,768]{1,0:T(8,128)(2,1)}, u32[]{:S(2)}, u32[]{:S(2)}) %collective-permute-start) | collective-permute-done | bytes 393248 | tf_op jit(solution)/shard_map/ppermute | solution.py:303
  108.7 0.7 copy-done.1
  109.3 0.7 copy-done.2
  110.0 7.3 %layer.1 = (bf16[128,1024]{1,0:T(8,128)(2,1)}, bf16[256,1280]{1,0:T(8,128)(2,1)S(1)}) custom-call(s32[2]{0:T(128)S(1)} %pad_add_fusion.place_ref, s32[2]{0:T(128)S(1)} %copy-done.1, bf16[256,768]{1,0:T(8,128)(2,1)S(1)} %bitcast.29, bf16[256,768]{1,0:T(8,128)(2,1)} %collective-permute-done.front_other_ref, bf16[128,512]{1,0:T(8,128)(2,1)} %dense_hbm.1, ...), custom_call_target="tpu_custom_call" | custom-call | flops 1073741824 | bytes 8388608 | tf_op jit(solution)/shard_map/layer/pallas_call | solution.py:236
  117.3 24.8 %all_to_all.16 = bf16[32,8,1280]{2,1,0:T(8,128)(2,1)S(1)} all-to-all(bf16[32,8,1280]{2,1,0:T(8,128)(2,1)S(1)} %bitcast.30), channel_id=1, replica_groups=mesh['yh'=2,'z'=8,'x'=4,'yl'=4,'core'=2] {'x','yl','core'}, dimensions={0} | all-to-all | bytes 1310720 | tf_op jit(solution)/shard_map/all_to_all | solution.py:323
  142.2 0.6 copy.21
  142.8 0.7 copy_bitcast_fusion
  (19 shorter events, 0.6 us)
Async XLA Ops:
  0.6 45.5 %copy-start.5 = (bf16[2,2,2048]{2,1,0:T(2,128)(2,1)S(1)}, bf16[2,2,2048]{2,1,0:T(2,128)(2,1)}, u32[]{:S(2)}) copy-start(bf16[2,2,2048]{2,1,0:T(2,128)(2,1)} %param.12) | copy-start | bytes 49156
  39.6 11.1 %collective-permute-start.2 = (bf16[256,1024]{1,0:T(8,128)(2,1)S(1)}, bf16[256,1024]{1,0:T(8,128)(2,1)S(1)}, u32[]{:S(2)}, u32[]{:S(2)}) collective-permute-start(bf16[256,1024]{1,0:T(8,128)(2,1)S(1)} %reshape.46), channel_id=1, source_target_pairs={{8,0},{16,8},{24,16},{0,24},{25,1},{1,9},{9,17},{17,25},{10,2},{18... | collective-permute-start | bytes 1572872 | tf_op jit(solution)/shard_map/ppermute | solution.py:297
  42.8 14.8 %collective-permute-start.1 = (bf16[256,1024]{1,0:T(8,128)(2,1)S(1)}, bf16[256,1024]{1,0:T(8,128)(2,1)S(1)}, u32[]{:S(2)}, u32[]{:S(2)}) collective-permute-start(bf16[256,1024]{1,0:T(8,128)(2,1)S(1)} %reshape.46), channel_id=1, source_target_pairs={{0,8},{8,16},{16,24},{24,0},{1,25},{9,1},{17,9},{25,17},{2,10},{10... | collective-permute-start | bytes 1572872 | tf_op jit(solution)/shard_map/ppermute | solution.py:296
  57.6 0.8 copy-start.4
  58.4 2.6 %copy-start.3 = (bf16[1,16,32768]{2,1,0:T(8,128)(2,1)S(1)}, bf16[1,16,32768]{2,1,0:T(8,128)(2,1)}, u32[]{:S(2)}) copy-start(bf16[1,16,32768]{2,1,0:T(8,128)(2,1)} %param.11) | copy-start | bytes 3145732
  58.5 50.1 %collective-permute-start.4 = (bf16[3,256,1024]{2,1,0:T(8,128)(2,1)S(1)}, bf16[3,256,1024]{2,1,0:T(8,128)(2,1)S(1)}, u32[]{:S(2)}, u32[]{:S(2)}) collective-permute-start(bf16[3,256,1024]{2,1,0:T(8,128)(2,1)S(1)} %pad_maximum_fusion.rest_0_), channel_id=1, source_target_pairs={{0,1},{1,0},{2,3},{3,2},{4,5},{5,4},{6,7},{7,6},{8,9},{9,8},{10,11... | collective-permute-start | bytes 4718600 | tf_op jit(solution)/shard_map/ppermute | solution.py:307
  81.4 0.8 copy-start
  82.2 22.7 %all-to-all-start = ((bf16[32,8,768]{2,1,0:T(8,128)(2,1)}), bf16[32,8,768]{2,1,0:T(8,128)(2,1)S(1)}, u32[]{:S(2)}, u32[]{:S(2)}) async-start(bf16[32,8,768]{2,1,0:T(8,128)(2,1)} %copy-done), calls=%async_computation | async-start | bytes 786432 | tf_op jit(solution)/shard_map/all_to_all | solution.py:301
  87.9 13.1 %collective-permute-start.3 = (bf16[256,1024]{1,0:T(8,128)(2,1)}, bf16[256,1024]{1,0:T(8,128)(2,1)}, u32[]{:S(2)}, u32[]{:S(2)}) collective-permute-start(bf16[256,1024]{1,0:T(8,128)(2,1)} %copy-done.4), channel_id=1, source_target_pairs={{0,8},{8,16},{16,24},{24,0},{1,25},{9,1},{17,9},{25,17},{2,10},{10... | collective-permute-start | bytes 1572872 | tf_op jit(solution)/shard_map/ppermute | solution.py:305
  101.0 7.6 %collective-permute-start.5 = (bf16[256,1024]{1,0:T(8,128)(2,1)}, bf16[256,1024]{1,0:T(8,128)(2,1)}, u32[]{:S(2)}, u32[]{:S(2)}) collective-permute-start(bf16[256,1024]{1,0:T(8,128)(2,1)} %collective-permute-done.3.rest_1_), channel_id=1, source_target_pairs={{0,1},{1,0},{2,3},{3,2},{4,5},{5,4},{6,7},{7,6},{8,9},{9,8},{10,11... | collective-permute-start | bytes 1572872 | tf_op jit(solution)/shard_map/ppermute | solution.py:308
  104.9 3.7 %collective-permute-start = (bf16[256,768]{1,0:T(8,128)(2,1)S(1)}, bf16[256,768]{1,0:T(8,128)(2,1)}, u32[]{:S(2)}, u32[]{:S(2)}) collective-permute-start(bf16[256,768]{1,0:T(8,128)(2,1)S(1)} %bitcast.28), channel_id=1, source_target_pairs={{0,1},{1,0},{2,3},{3,2},{4,5},{5,4},{6,7},{7,6},{8,9},{9,8},{10,11... | collective-permute-start | bytes 1179656 | tf_op jit(solution)/shard_map/ppermute | solution.py:303
  108.6 0.7 copy-start.1
  109.3 0.7 copy-start.2
